TPU v7x, 32 devices: a whole 2x2x4 slice. The times are simulated.
32 devices in a mesh: vol: 8 (over z, x), slab: 4 (over y, core).
Axes of the slice: x: 2, y: 2, z: 4, core: 2. Of those that a mesh axis runs over, the one named last changes fastest.
Arguments:
- face_disp: bfloat16 [64, 65536], P(None, ('vol', 'slab')), may hold values from -6 to 6
- contact_owner: int32 [65536, 1], P(('vol', 'slab')), may hold values from 0 to 7; in each aligned block of 2048 rows (0 to 2047, 2048 to 4095, ...) at most 1024 rows name the same one
- segment: int32 [65536], P(('vol', 'slab')), may hold values from 0 to 7
- face_area: float32 [65536], P(('vol', 'slab')), may hold values from 0.5 to 5
- face_nodes: int32 [4, 65536], P(None, ('vol', 'slab')), may hold values from 0 to 1023
- mortar_blocks: bfloat16 [256, 64, 64], P(('vol', 'slab')), may hold values from -0.75 to 0.75
- gap_offset: bfloat16 [256, 64], P(('vol', 'slab')), may hold values from -6 to 6
- shape_table: float32 [12, 64], replicated, may hold values from -0.75 to 0.75
- node_disp: float32 [3, 32768], P(None, ('vol', 'slab')), may hold values from -6 to 6
- stiffness: float32 [32768], P(('vol', 'slab')), may hold values from 0.2 to 2
- connect: int32 [8, 32768], P(None, ('vol', 'slab')), may hold values from 0 to 1023
- elem_matrix: float32 [24, 24], replicated, may hold values from -1.25 to 1.25
Outputs:
- residual: float32 [3, 32768], P(None, ('vol', 'slab'))
Inputs may be any that keep to these rules, and one draw needn't show every extreme that they name: `contact_owner`: in each block of 2048 faces no owner index is named by more than 1024 faces, and some owner index is named by exactly 1024.
All inputs are finite; a program needn't handle non-finite values.
Results may differ from a plain program's by a relative error of at most 0.0028.
Values may be sent and summed in bfloat16 or wider, within the bound.
No kernel may reach another device: no remote copies, remote signals or barrier semaphores. Data moves between devices by JAX's collectives and lax.ppermute only.
A program may use at most 64 MiB of HBM per device.

v0:
```python
import jax
import jax.numpy as jnp
from jax import lax
from jax.experimental import pallas as pl
from jax.experimental.pallas import tpu as pltpu
from jax.sharding import PartitionSpec as P

SH = 256
LANES = 128
PACK_ROWS = 16
CHUNK = 16

f32, bf16, i32 = jnp.float32, jnp.bfloat16, jnp.int32


def split(values):
    high = values.astype(bf16)
    return high, (values - high.astype(f32)).astype(bf16)


def nt_dot(left, right):
    return lax.dot_general(left, right, (((1,), (1,)), ((), ())), preferred_element_type=f32)


def pack_kernel(mortar_ref, offset_ref, out_ref):
    segments, order, _ = mortar_ref.shape
    per_row = out_ref.shape[1] // order
    for first in range(0, segments, per_row):
        row = first // per_row * order
        blocks = [mortar_ref[first + place] for place in range(per_row)]
        out_ref[row : row + order, :] = jnp.concatenate(blocks, axis=1)
    rows = segments // per_row * order
    out_ref[rows:, :] = jnp.zeros((PACK_ROWS, out_ref.shape[1]), bf16)
    out_ref[rows : rows + segments, :order] = offset_ref[...]


def scatter_terms(value_rows, node_row, high_count):
    width = node_row.shape[1]
    high = jnp.broadcast_to(node_row // LANES, (high_count, width))
    mask = high == lax.broadcasted_iota(i32, (high_count, width), 0)
    rows = [jnp.where(mask, jnp.broadcast_to(v, (high_count, width)), 0.0) for v in value_rows]
    rows = jnp.concatenate(rows, axis=0)
    low = jnp.broadcast_to(node_row % LANES, (LANES, width))
    table = (low == lax.broadcasted_iota(i32, (LANES, width), 0)).astype(f32).astype(bf16)
    rows_high, rows_low = split(rows)
    return jnp.concatenate([rows_high, rows_low], axis=0), table


def element_kernel(disp_ref, connect_ref, stiffness_ref, matrix_ref, out_ref, elem_ref, force_ref):
    node_count = disp_ref.shape[1]
    elem_count = connect_ref.shape[1]
    corners = connect_ref.shape[0]
    high_count = node_count // LANES
    for start in range(0, elem_count, LANES):
        index = connect_ref[:, start : start + LANES]
        high, low = index // LANES, index % LANES
        for comp in range(3):
            picked = jnp.zeros(index.shape, f32)
            for part in range(high_count):
                line = disp_ref[comp : comp + 1, part * LANES : (part + 1) * LANES]
                table = jnp.broadcast_to(line, (corners, LANES))
                found = jnp.take_along_axis(table, low, axis=1, mode="promise_in_bounds")
                picked = jnp.where(high == part, found, picked)
            elem_ref[start // LANES, pl.ds(comp, corners, stride=3), :] = picked
    m_high, m_low = split(matrix_ref[...])
    d_high, d_low = split(jnp.concatenate([elem_ref[k] for k in range(elem_count // LANES)], axis=1))
    force = (
        jnp.dot(m_high, d_high, preferred_element_type=f32)
        + jnp.dot(m_high, d_low, preferred_element_type=f32)
        + jnp.dot(m_low, d_high, preferred_element_type=f32)
    )
    force_ref[...] = force * stiffness_ref[...]
    total = jnp.zeros((6 * high_count, LANES), f32)
    for corner in range(corners):
        values = [force_ref[3 * corner + c : 3 * corner + c + 1, :] for c in range(3)]
        rows, table = scatter_terms(values, connect_ref[corner : corner + 1, :], high_count)
        total = total + nt_dot(rows, table)
    out_ref[...] = total[: 3 * high_count] + total[3 * high_count :]


def contact_kernel(
    vol_ref, disp_ref, owner_ref, segment_ref, area_ref, nodes_ref, shape_ref, inner_ref, *rest, relative, tile
):
    payload_refs = rest[:-7]
    out_ref, edge_ref, far_ref, blocks_ref, offsets_ref, table_ref, nodal_ref = rest[-7:]
    order, faces = disp_ref.shape
    width = payload_refs[0].shape[1]
    per_row = width // order
    chunks = table_ref.shape[0]
    high_count = inner_ref.shape[0] // 3
    vol_count = offsets_ref.shape[1] // PACK_ROWS
    seg_rows = blocks_ref.shape[0] // vol_count
    groups = seg_rows // order
    piece = seg_rows + PACK_ROWS

    place = 0
    for ref in payload_refs:
        for start in range(0, ref.shape[0], piece):
            blocks_ref[place * seg_rows : (place + 1) * seg_rows, :] = ref[start : start + seg_rows, :]
            offsets_ref[:, place * PACK_ROWS : (place + 1) * PACK_ROWS] = jnp.transpose(
                ref[start + seg_rows : start + piece, :order].astype(f32)
            ).astype(bf16)
            place += 1

    sixteen = jnp.concatenate([shape_ref[...], jnp.zeros((16 - shape_ref.shape[0], order), f32)], axis=0)
    zero = jnp.zeros_like(sixteen)
    diagonal = jnp.concatenate(
        [jnp.concatenate([sixteen if r == c else zero for c in range(per_row)], axis=1) for r in range(per_row)],
        axis=0,
    )
    shape_high, shape_low = split(diagonal)
    shape_both = jnp.concatenate([shape_high, shape_low], axis=0)
    half = 16 * per_row
    quads = CHUNK // per_row

    def build(chunk, _):
        start = pl.multiple_of(chunk * (CHUNK * order), CHUNK * order)
        product = nt_dot(shape_both, blocks_ref[pl.ds(start, CHUNK * order), :])
        product = product[:half] + product[half:]
        for quad in range(quads):
            cut = product[:, quad * width : (quad + 1) * width]
            high, low = split(cut)
            both = jnp.concatenate([high, low], axis=0)
            table_ref[chunk, quad * 2 * half : (quad + 1) * 2 * half, :width] = both
            table_ref[chunk, quad * 2 * half : (quad + 1) * 2 * half, width:] = both
        return 0

    if chunks == 1:
        build(0, 0)
    else:
        lax.fori_loop(0, chunks, build, 0)

    def step(index, total):
        cols = pl.ds(pl.multiple_of(index * tile, tile), tile)
        owner = owner_ref[:, cols]
        segment = segment_ref[:, cols]
        if relative:
            owner = vol_ref[0] - owner
            owner = jnp.where(owner < 0, owner + vol_count, owner)
        slot = segment % per_row
        group = owner * groups + segment // per_row
        disp = disp_ref[:, cols]

        def masked(values, row, number):
            return values * (row == number).astype(f32).astype(bf16)

        spread = jnp.concatenate([masked(disp, slot, place) for place in range(per_row)], axis=0)
        target = owner * PACK_ROWS + segment
        picks = jnp.broadcast_to(target, (vol_count * PACK_ROWS, tile)) == lax.broadcasted_iota(
            i32, (vol_count * PACK_ROWS, tile), 0
        )
        gap = -jnp.dot(offsets_ref[...], picks.astype(f32).astype(bf16), preferred_element_type=f32)
        group_wide = jnp.broadcast_to(group, (order, tile))

        def add_gap(chunk, found):
            start = pl.multiple_of(chunk * (CHUNK * order), CHUNK * order)
            product = jnp.dot(blocks_ref[pl.ds(start, CHUNK * order), :], spread, preferred_element_type=f32)
            for place in range(CHUNK):
                found = jnp.where(
                    group_wide == chunk * CHUNK + place, product[place * order : (place + 1) * order], found
                )
            return found

        zero_gap = jnp.zeros((order, tile), f32)
        gap = gap + (add_gap(0, zero_gap) if chunks == 1 else lax.fori_loop(0, chunks, add_gap, zero_gap))
        pressure = -gap
        traction = jnp.maximum(pressure, 0.0) + jnp.log1p(jnp.exp(-jnp.abs(pressure)))
        t_high, t_low = split(traction)
        inner = group % per_row
        outer = (group // per_row) * per_row + slot
        pieces = [masked(t, inner, place) for t in (t_high, t_low) for place in range(per_row)]
        pressed = jnp.concatenate(pieces, axis=0)
        outer_wide = jnp.broadcast_to(outer, (16, tile))

        def add_nodal(chunk, found):
            product = jnp.dot(table_ref[chunk], pressed, preferred_element_type=f32)
            for quad in range(quads):
                for place in range(per_row):
                    row = quad * 2 * half + place * 16
                    value = product[row : row + 16] + product[row + half : row + half + 16]
                    number = (chunk * quads + quad) * per_row + place
                    found = jnp.where(outer_wide == number, value, found)
            return found

        zero_nodal = jnp.zeros((16, tile), f32)
        nodal = add_nodal(0, zero_nodal) if chunks == 1 else lax.fori_loop(0, chunks, add_nodal, zero_nodal)
        nodal_ref[...] = nodal * (-area_ref[:, cols])
        for corner in range(nodes_ref.shape[0]):
            values = [nodal_ref[3 * corner + c : 3 * corner + c + 1, :] for c in range(3)]
            rows, table = scatter_terms(values, nodes_ref[corner : corner + 1, cols], high_count)
            total = total + nt_dot(rows, table)
        return total

    total = lax.fori_loop(0, faces // tile, step, jnp.zeros((6 * high_count, LANES), f32))
    unsummed = total[: 3 * high_count] + total[3 * high_count :] + inner_ref[...]
    out_ref[...] = unsummed
    edge = edge_ref.shape[0] // 3
    lower = [unsummed[c * high_count : c * high_count + edge] for c in range(3)]
    upper = [unsummed[(c + 1) * high_count - edge : (c + 1) * high_count] for c in range(3)]
    lower, upper = jnp.concatenate(lower, axis=0), jnp.concatenate(upper, axis=0)
    odd = vol_ref[1] == 1
    edge_ref[...] = jnp.where(odd, lower, upper)
    far_ref[...] = jnp.where(odd, upper, lower)


def close_kernel(slab_ref, whole_ref, edge_ref, far_ref, out_ref):
    high_count = whole_ref.shape[0] // 3
    edge = edge_ref.shape[0] // 3
    odd = slab_ref[1] == 1
    lower = jnp.where(odd, edge_ref[...], far_ref[...])
    upper = jnp.where(odd, far_ref[...], edge_ref[...])
    whole = whole_ref[...]
    for c in range(3):
        for part in range(high_count):
            line = whole[c * high_count + part : c * high_count + part + 1]
            if part < edge:
                line = line + lower[c * edge + part : c * edge + part + 1]
            if part >= high_count - edge:
                near = c * edge + part - (high_count - edge)
                line = line + upper[near : near + 1]
            out_ref[c : c + 1, part * LANES : (part + 1) * LANES] = line


def vmem():
    return pl.BlockSpec(memory_space=pltpu.VMEM)


def smem():
    return pl.BlockSpec(memory_space=pltpu.SMEM)


def shards(
    face_disp,
    contact_owner,
    segment,
    face_area,
    face_nodes,
    mortar_blocks,
    gap_offset,
    shape_table,
    node_disp,
    stiffness,
    connect,
    elem_matrix,
):
    vol_count, slab_count = lax.axis_size("vol"), lax.axis_size("slab")
    segments, order, _ = mortar_blocks.shape
    faces = face_disp.shape[1]
    node_count = node_disp.shape[1]
    elem_count = connect.shape[1]
    high_count = node_count // LANES
    per_row = 256 // order
    seg_rows = segments // per_row * order
    width = per_row * order
    vol = lax.axis_index("vol")
    slab = lax.axis_index("slab")
    scalars = jnp.stack([vol, slab % 2]).astype(i32)

    payload = pl.pallas_call(
        pack_kernel,
        out_shape=jax.ShapeDtypeStruct((seg_rows + PACK_ROWS, width), bf16),
        in_specs=[vmem(), vmem()],
        out_specs=vmem(),
        name="pack",
    )(mortar_blocks, gap_offset)
    relative = vol_count <= 8
    if relative:
        payloads = [payload] + [
            lax.ppermute(payload, "vol", [(i, (i + k) % vol_count) for i in range(vol_count)])
            for k in range(1, vol_count)
        ]
    else:
        payloads = [lax.all_gather(payload, "vol", tiled=True)]

    internal = pl.pallas_call(
        element_kernel,
        out_shape=jax.ShapeDtypeStruct((3 * high_count, LANES), f32),
        in_specs=[vmem()] * 4,
        out_specs=vmem(),
        scratch_shapes=[pltpu.VMEM((elem_count // LANES, 24, LANES), f32), pltpu.VMEM((24, elem_count), f32)],
        cost_estimate=pl.CostEstimate(flops=2_000_000_000, bytes_accessed=100_000, transcendentals=0),
        name="element",
    )(node_disp, connect, stiffness[None, :], elem_matrix)

    chunks = vol_count * (segments // per_row) // CHUNK
    tile = min(512, faces)
    edge_rows = 3 * (SH // LANES)
    unsummed, edge, far = pl.pallas_call(
        lambda *refs: contact_kernel(*refs, relative=relative, tile=tile),
        out_shape=[
            jax.ShapeDtypeStruct((3 * high_count, LANES), f32),
            jax.ShapeDtypeStruct((edge_rows, LANES), f32),
            jax.ShapeDtypeStruct((edge_rows, LANES), f32),
        ],
        in_specs=[smem()] + [vmem()] * (7 + len(payloads)),
        out_specs=[vmem()] * 3,
        scratch_shapes=[
            pltpu.VMEM((vol_count * seg_rows, width), bf16),
            pltpu.VMEM((order, vol_count * PACK_ROWS), bf16),
            pltpu.VMEM((chunks, 2 * 16 * CHUNK, 2 * width), bf16),
            pltpu.VMEM((16, tile), f32),
        ],
        name="contact",
    )(
        scalars,
        face_disp,
        contact_owner.reshape(1, faces),
        segment[None, :],
        face_area[None, :],
        face_nodes,
        shape_table,
        internal,
        *payloads,
    )
    near_pairs = [(i, i + 1) for i in range(0, slab_count - 1, 2)]
    far_pairs = [(i, i + 1) for i in range(1, slab_count - 1, 2)]
    far_in = lax.ppermute(far, "slab", far_pairs + [(b, a) for a, b in far_pairs])
    edge_in = lax.ppermute(edge, "slab", near_pairs + [(b, a) for a, b in near_pairs])
    return pl.pallas_call(
        close_kernel,
        out_shape=jax.ShapeDtypeStruct((3, node_count), f32),
        in_specs=[smem()] + [vmem()] * 3,
        out_specs=vmem(),
        name="close",
    )(scalars, unsummed, edge_in, far_in)


def solution(mesh):
    in_specs = (
        P(None, ("vol", "slab")),
        P(("vol", "slab"), None),
        P(("vol", "slab")),
        P(("vol", "slab")),
        P(None, ("vol", "slab")),
        P(("vol", "slab"), None, None),
        P(("vol", "slab"), None),
        P(),
        P(None, ("vol", "slab")),
        P(("vol", "slab")),
        P(None, ("vol", "slab")),
        P(),
    )
    out_specs = P(None, ("vol", "slab"))
    return jax.shard_map(shards, mesh=mesh, in_specs=in_specs, out_specs=out_specs, check_vma=False)
```

profile of v0, /device:TPU:1, one launch (start us, length us, event | category | flops | bytes accessed | tf_op | source)
XLA Modules:
  0.0 38.9 jit_solution(13100784252701406252)
XLA Ops:
  0.0 1.6 %pack.1.refs_8_ = bf16[144,256]{1,0:T(8,128)(2,1)} custom-call(bf16[8,64,64]{2,1,0:T(8,128)(2,1)} %mortar_ref.1, bf16[8,64]{1,0:T(8,128)(2,1)} %offset_ref.1), custom_call_target="tpu_custom_call" | custom-call | tf_op jit(solution)/shard_map/pack/pallas_call | solution.py:259
  1.6 5.1 %collective-permute-start.6 = (bf16[144,256]{1,0:T(8,128)(2,1)}, bf16[144,256]{1,0:T(8,128)(2,1)S(1)}, u32[]{:S(2)}, u32[]{:S(2)}) collective-permute-start(bf16[144,256]{1,0:T(8,128)(2,1)} %pack.1.refs_8_), channel_id=1, source_target_pairs={{0,28},{4,0},{8,4},{12,8},{16,12},{20,16},{24,20},{28,24},{1,29},{... | collective-permute-start | bytes 221192 | tf_op jit(solution)/shard_map/ppermute | solution.py:269
  6.7 0.2 collective-permute-start.5
  6.9 0.0 collective-permute-start.4
  6.9 2.4 %collective-permute-start.3 = (bf16[144,256]{1,0:T(8,128)(2,1)}, bf16[144,256]{1,0:T(8,128)(2,1)S(1)}, u32[]{:S(2)}, u32[]{:S(2)}) collective-permute-start(bf16[144,256]{1,0:T(8,128)(2,1)} %pack.1.refs_8_), channel_id=1, source_target_pairs={{0,16},{4,20},{8,24},{12,28},{16,0},{20,4},{24,8},{28,12},{1,17},{... | collective-permute-start | bytes 221192 | tf_op jit(solution)/shard_map/ppermute | solution.py:269
  9.3 0.0 collective-permute-start.2
  9.3 0.0 copy-start
  9.3 2.9 %element.1.refs_7_ = f32[24,128]{1,0:T(8,128)} custom-call(f32[3,1024]{1,0:T(4,128)} %disp_ref.1, s32[8,1024]{1,0:T(8,128)} %connect_ref.1, f32[1,1024]{1,0:T(1,128)} %bitcast.9, f32[24,24]{1,0:T(8,128)} %matrix_ref.1), custom_call_target="tpu_custom_call" | custom-call | flops 2000000000 | bytes 100000 | tf_op jit(solution)/shard_map/element/pallas_call | solution.py:275
  12.2 0.0 collective-permute-done.6.refs_15_
  12.2 0.0 copy-done
  12.2 0.0 copy-start.1
  12.2 1.3 %collective-permute-start.1 = (bf16[144,256]{1,0:T(8,128)(2,1)S(1)}, bf16[144,256]{1,0:T(8,128)(2,1)S(1)}, u32[]{:S(2)}, u32[]{:S(2)}) collective-permute-start(bf16[144,256]{1,0:T(8,128)(2,1)S(1)} %copy-done), channel_id=1, source_target_pairs={{0,8},{4,12},{8,16},{12,20},{16,24},{20,28},{24,0},{28,4},{1,9},{5... | collective-permute-start | bytes 221192 | tf_op jit(solution)/shard_map/ppermute | solution.py:269
  13.5 0.0 collective-permute-done.5.refs_14_
  13.5 0.0 copy-start.2
  13.5 1.1 %collective-permute-start = (bf16[144,256]{1,0:T(8,128)(2,1)S(1)}, bf16[144,256]{1,0:T(8,128)(2,1)S(1)}, u32[]{:S(2)}, u32[]{:S(2)}) collective-permute-start(bf16[144,256]{1,0:T(8,128)(2,1)S(1)} %copy-done), channel_id=1, source_target_pairs={{0,4},{4,8},{8,12},{12,16},{16,20},{20,24},{24,28},{28,0},{1,5},{5... | collective-permute-start | bytes 221192 | tf_op jit(solution)/shard_map/ppermute | solution.py:269
  14.7 0.7 %pad_add_fusion.refs_0_.slab_ref = s32[2]{0:T(128)} fusion(s32[1]{0:T(128)} %bitcast.1, s32[1]{0:T(128)} %bitcast), kind=kLoop, calls=%fused_computation | loop fusion | flops 2 | bytes 16 | tf_op jit(solution)/shard_map/stack | solution.py:257
  15.3 0.0 collective-permute-done.4.refs_13_
  15.3 0.0 copy-start.3
  15.3 1.2 %collective-permute-done.3.refs_12_ = bf16[144,256]{1,0:T(8,128)(2,1)S(1)} collective-permute-done((bf16[144,256]{1,0:T(8,128)(2,1)}, bf16[144,256]{1,0:T(8,128)(2,1)S(1)}, u32[]{:S(2)}, u32[]{:S(2)}) %collective-permute-start.3) | collective-permute-done | bytes 73760 | tf_op jit(solution)/shard_map/ppermute | solution.py:269
  16.5 0.0 copy-start.4
  16.5 4.2 %collective-permute-done.2.refs_11_ = bf16[144,256]{1,0:T(8,128)(2,1)S(1)} collective-permute-done((bf16[144,256]{1,0:T(8,128)(2,1)}, bf16[144,256]{1,0:T(8,128)(2,1)S(1)}, u32[]{:S(2)}, u32[]{:S(2)}) %collective-permute-start.2) | collective-permute-done | bytes 73760 | tf_op jit(solution)/shard_map/ppermute | solution.py:269
  20.7 0.0 copy-start.5
  20.7 0.0 collective-permute-done.1.refs_10_
  20.7 0.0 copy-start.6
  20.7 0.0 collective-permute-done.refs_9_
  20.7 0.0 copy-start.7
  20.8 0.0 copy-done.1
  20.8 0.0 copy-done.2
  20.8 0.0 copy-done.3
  20.8 0.0 copy-done.4
  20.8 0.6 %copy-done.5 = bf16[144,256]{1,0:T(8,128)(2,1)} copy-done((bf16[144,256]{1,0:T(8,128)(2,1)}, bf16[144,256]{1,0:T(8,128)(2,1)S(1)}, u32[]{:S(2)}) %copy-start.5) | copy-done | bytes 73752
  21.4 0.0 copy-done.6
  21.4 0.0 copy-done.7
  21.4 7.9 %contact.1 = (f32[24,128]{1,0:T(8,128)}, f32[6,128]{1,0:T(8,128)}, f32[6,128]{1,0:T(8,128)}) custom-call(s32[2]{0:T(128)} %pad_add_fusion.refs_0_.slab_ref, bf16[64,2048]{1,0:T(8,128)(2,1)} %refs_1_.1, s32[1,2048]{1,0:T(1,128)} %bitcast.6, s32[1,2048]{1,0:T(1,128)} %bitcast.7, f32[1,2048]{1,0:T(1,128)} %bitcast.8, s32[4,2048]{1,0:T(4,128)} %refs_5_.1, ...), custom_call_target="tpu_custom_call" | custom-call | tf_op jit(solution)/shard_map/contact/pallas_call | solution.py:288
  29.3 2.4 %collective-permute-start.7 = (f32[6,128]{1,0:T(8,128)}, f32[6,128]{1,0:T(8,128)S(1)}, u32[]{:S(2)}, u32[]{:S(2)}) collective-permute-start(f32[6,128]{1,0:T(8,128)} %get-tuple-element.9), channel_id=1, source_target_pairs={{0,1},{2,3},{1,0},{3,2},{4,5},{6,7},{5,4},{7,6},{8,9},{10,11},{9,8... | collective-permute-start | bytes 9224 | tf_op jit(solution)/shard_map/ppermute | solution.py:318
  31.8 3.0 %collective-permute-start.8 = (f32[6,128]{1,0:T(8,128)}, f32[6,128]{1,0:T(8,128)S(1)}, u32[]{:S(2)}, u32[]{:S(2)}) collective-permute-start(f32[6,128]{1,0:T(8,128)} %get-tuple-element.10), channel_id=1, source_target_pairs={{1,2},{2,1},{5,6},{6,5},{9,10},{10,9},{13,14},{14,13},{17,18},{18,... | collective-permute-start | bytes 9224 | tf_op jit(solution)/shard_map/ppermute | solution.py:317
  34.8 0.0 collective-permute-done.7.edge_ref
  34.8 0.0 copy-start.8
  34.8 2.1 %collective-permute-done.8.far_ref = f32[6,128]{1,0:T(8,128)S(1)} collective-permute-done((f32[6,128]{1,0:T(8,128)}, f32[6,128]{1,0:T(8,128)S(1)}, u32[]{:S(2)}, u32[]{:S(2)}) %collective-permute-start.8) | collective-permute-done | bytes 3104 | tf_op jit(solution)/shard_map/ppermute | solution.py:317
  36.9 0.0 copy-start.9
  36.9 0.0 copy-done.8
  36.9 0.6 %copy-done.9 = f32[6,128]{1,0:T(8,128)} copy-done((f32[6,128]{1,0:T(8,128)}, f32[6,128]{1,0:T(8,128)S(1)}, u32[]{:S(2)}) %copy-start.9) | copy-done | bytes 3096
  37.5 1.4 %close.1 = f32[3,1024]{1,0:T(4,128)} custom-call(s32[2]{0:T(128)} %pad_add_fusion.refs_0_.slab_ref, f32[24,128]{1,0:T(8,128)} %get-tuple-element.8.whole_ref, f32[6,128]{1,0:T(8,128)} %copy-done.8, f32[6,128]{1,0:T(8,128)} %copy-done.9), custom_call_target="tpu_custom_call" | custom-call | tf_op jit(solution)/shard_map/close/pallas_call | solution.py:319
Async XLA Ops:
  1.6 10.6 %collective-permute-start.6 = (bf16[144,256]{1,0:T(8,128)(2,1)}, bf16[144,256]{1,0:T(8,128)(2,1)S(1)}, u32[]{:S(2)}, u32[]{:S(2)}) collective-permute-start(bf16[144,256]{1,0:T(8,128)(2,1)} %pack.1.refs_8_), channel_id=1, source_target_pairs={{0,28},{4,0},{8,4},{12,8},{16,12},{20,16},{24,20},{28,24},{1,29},{... | collective-permute-start | bytes 221192 | tf_op jit(solution)/shard_map/ppermute | solution.py:269
  6.7 6.8 %collective-permute-start.5 = (bf16[144,256]{1,0:T(8,128)(2,1)}, bf16[144,256]{1,0:T(8,128)(2,1)S(1)}, u32[]{:S(2)}, u32[]{:S(2)}) collective-permute-start(bf16[144,256]{1,0:T(8,128)(2,1)} %pack.1.refs_8_), channel_id=1, source_target_pairs={{0,24},{4,28},{8,0},{12,4},{16,8},{20,12},{24,16},{28,20},{1,25},{... | collective-permute-start | bytes 221192 | tf_op jit(solution)/shard_map/ppermute | solution.py:269
  6.9 8.5 %collective-permute-start.4 = (bf16[144,256]{1,0:T(8,128)(2,1)}, bf16[144,256]{1,0:T(8,128)(2,1)S(1)}, u32[]{:S(2)}, u32[]{:S(2)}) collective-permute-start(bf16[144,256]{1,0:T(8,128)(2,1)} %pack.1.refs_8_), channel_id=1, source_target_pairs={{0,20},{4,24},{8,28},{12,0},{16,4},{20,8},{24,12},{28,16},{1,21},{... | collective-permute-start | bytes 221192 | tf_op jit(solution)/shard_map/ppermute | solution.py:269
  6.9 9.7 %collective-permute-start.3 = (bf16[144,256]{1,0:T(8,128)(2,1)}, bf16[144,256]{1,0:T(8,128)(2,1)S(1)}, u32[]{:S(2)}, u32[]{:S(2)}) collective-permute-start(bf16[144,256]{1,0:T(8,128)(2,1)} %pack.1.refs_8_), channel_id=1, source_target_pairs={{0,16},{4,20},{8,24},{12,28},{16,0},{20,4},{24,8},{28,12},{1,17},{... | collective-permute-start | bytes 221192 | tf_op jit(solution)/shard_map/ppermute | solution.py:269
  9.3 11.4 %collective-permute-start.2 = (bf16[144,256]{1,0:T(8,128)(2,1)}, bf16[144,256]{1,0:T(8,128)(2,1)S(1)}, u32[]{:S(2)}, u32[]{:S(2)}) collective-permute-start(bf16[144,256]{1,0:T(8,128)(2,1)} %pack.1.refs_8_), channel_id=1, source_target_pairs={{0,12},{4,16},{8,20},{12,24},{16,28},{20,0},{24,4},{28,8},{1,13},{... | collective-permute-start | bytes 221192 | tf_op jit(solution)/shard_map/ppermute | solution.py:269
  9.3 2.9 %copy-start = (bf16[144,256]{1,0:T(8,128)(2,1)S(1)}, bf16[144,256]{1,0:T(8,128)(2,1)}, u32[]{:S(2)}) copy-start(bf16[144,256]{1,0:T(8,128)(2,1)} %pack.1.refs_8_) | copy-start | bytes 221188
  12.2 8.6 %copy-start.1 = (bf16[144,256]{1,0:T(8,128)(2,1)}, bf16[144,256]{1,0:T(8,128)(2,1)S(1)}, u32[]{:S(2)}) copy-start(bf16[144,256]{1,0:T(8,128)(2,1)S(1)} %collective-permute-done.6.refs_15_) | copy-start | bytes 221188
  12.2 8.5 %collective-permute-start.1 = (bf16[144,256]{1,0:T(8,128)(2,1)S(1)}, bf16[144,256]{1,0:T(8,128)(2,1)S(1)}, u32[]{:S(2)}, u32[]{:S(2)}) collective-permute-start(bf16[144,256]{1,0:T(8,128)(2,1)S(1)} %copy-done), channel_id=1, source_target_pairs={{0,8},{4,12},{8,16},{12,20},{16,24},{20,28},{24,0},{28,4},{1,9},{5... | collective-permute-start | bytes 221192 | tf_op jit(solution)/shard_map/ppermute | solution.py:269
  13.5 7.3 %copy-start.2 = (bf16[144,256]{1,0:T(8,128)(2,1)}, bf16[144,256]{1,0:T(8,128)(2,1)S(1)}, u32[]{:S(2)}) copy-start(bf16[144,256]{1,0:T(8,128)(2,1)S(1)} %collective-permute-done.5.refs_14_) | copy-start | bytes 221188
  13.5 7.2 %collective-permute-start = (bf16[144,256]{1,0:T(8,128)(2,1)S(1)}, bf16[144,256]{1,0:T(8,128)(2,1)S(1)}, u32[]{:S(2)}, u32[]{:S(2)}) collective-permute-start(bf16[144,256]{1,0:T(8,128)(2,1)S(1)} %copy-done), channel_id=1, source_target_pairs={{0,4},{4,8},{8,12},{12,16},{16,20},{20,24},{24,28},{28,0},{1,5},{5... | collective-permute-start | bytes 221192 | tf_op jit(solution)/shard_map/ppermute | solution.py:269
  15.3 5.5 %copy-start.3 = (bf16[144,256]{1,0:T(8,128)(2,1)}, bf16[144,256]{1,0:T(8,128)(2,1)S(1)}, u32[]{:S(2)}) copy-start(bf16[144,256]{1,0:T(8,128)(2,1)S(1)} %collective-permute-done.4.refs_13_) | copy-start | bytes 221188
  16.5 4.3 %copy-start.4 = (bf16[144,256]{1,0:T(8,128)(2,1)}, bf16[144,256]{1,0:T(8,128)(2,1)S(1)}, u32[]{:S(2)}) copy-start(bf16[144,256]{1,0:T(8,128)(2,1)S(1)} %collective-permute-done.3.refs_12_) | copy-start | bytes 221188
  20.7 0.6 %copy-start.5 = (bf16[144,256]{1,0:T(8,128)(2,1)}, bf16[144,256]{1,0:T(8,128)(2,1)S(1)}, u32[]{:S(2)}) copy-start(bf16[144,256]{1,0:T(8,128)(2,1)S(1)} %collective-permute-done.2.refs_11_) | copy-start | bytes 221188
  20.7 0.6 %copy-start.6 = (bf16[144,256]{1,0:T(8,128)(2,1)}, bf16[144,256]{1,0:T(8,128)(2,1)S(1)}, u32[]{:S(2)}) copy-start(bf16[144,256]{1,0:T(8,128)(2,1)S(1)} %collective-permute-done.1.refs_10_) | copy-start | bytes 221188
  20.7 0.7 %copy-start.7 = (bf16[144,256]{1,0:T(8,128)(2,1)}, bf16[144,256]{1,0:T(8,128)(2,1)S(1)}, u32[]{:S(2)}) copy-start(bf16[144,256]{1,0:T(8,128)(2,1)S(1)} %collective-permute-done.refs_9_) | copy-start | bytes 221188
  29.3 5.5 %collective-permute-start.7 = (f32[6,128]{1,0:T(8,128)}, f32[6,128]{1,0:T(8,128)S(1)}, u32[]{:S(2)}, u32[]{:S(2)}) collective-permute-start(f32[6,128]{1,0:T(8,128)} %get-tuple-element.9), channel_id=1, source_target_pairs={{0,1},{2,3},{1,0},{3,2},{4,5},{6,7},{5,4},{7,6},{8,9},{10,11},{9,8... | collective-permute-start | bytes 9224 | tf_op jit(solution)/shard_map/ppermute | solution.py:318
  31.8 5.1 %collective-permute-start.8 = (f32[6,128]{1,0:T(8,128)}, f32[6,128]{1,0:T(8,128)S(1)}, u32[]{:S(2)}, u32[]{:S(2)}) collective-permute-start(f32[6,128]{1,0:T(8,128)} %get-tuple-element.10), channel_id=1, source_target_pairs={{1,2},{2,1},{5,6},{6,5},{9,10},{10,9},{13,14},{14,13},{17,18},{18,... | collective-permute-start | bytes 9224 | tf_op jit(solution)/shard_map/ppermute | solution.py:317
  34.8 2.1 %copy-start.8 = (f32[6,128]{1,0:T(8,128)}, f32[6,128]{1,0:T(8,128)S(1)}, u32[]{:S(2)}) copy-start(f32[6,128]{1,0:T(8,128)S(1)} %collective-permute-done.7.edge_ref) | copy-start | bytes 9220
  36.9 0.6 %copy-start.9 = (f32[6,128]{1,0:T(8,128)}, f32[6,128]{1,0:T(8,128)S(1)}, u32[]{:S(2)}) copy-start(f32[6,128]{1,0:T(8,128)S(1)} %collective-permute-done.8.far_ref) | copy-start | bytes 9220
where the time goes:
time: 39.1 us; the launch traced here: 38.9 us
  starting transfers between devices  15.6 us (40%)
  Pallas kernels  13.8 us (35%)
  waiting for transfers between devices  7.48 us (19%)
  local copies, waits for them, and re-layouts  1.23 us (3%)
  other arithmetic  0.66 us (2%)
    ppermute x7, starting transfers between devices, shards(): lax.ppermute(payload, 'vol', [(i, (i + k) % vol_count) for i in range(vol...  10.1 us
    pallas_call x1, Pallas kernels, shards(): pl.pallas_call(lambda *refs: contact_kernel(*refs, relative=relative, til...  7.93 us
    ppermute x7, waiting for transfers between devices, shards(): lax.ppermute(payload, 'vol', [(i, (i + k) % vol_count) for i in range(vol...  5.43 us
    ppermute x1, starting transfers between devices, shards(): lax.ppermute(far, 'slab', far_pairs + [(b, a) for a, b in far_pairs])  3.04 us
    pallas_call x1, Pallas kernels, shards(): pl.pallas_call(element_kernel, out_shape=jax.ShapeDtypeStruct((3 * high_c...  2.87 us
    ppermute x1, starting transfers between devices, shards(): lax.ppermute(edge, 'slab', near_pairs + [(b, a) for a, b in near_pairs])  2.41 us
    ppermute x1, waiting for transfers between devices, shards(): lax.ppermute(far, 'slab', far_pairs + [(b, a) for a, b in far_pairs])  2.05 us
    pallas_call x1, Pallas kernels, shards(): pl.pallas_call(pack_kernel, out_shape=jax.ShapeDtypeStruct((seg_rows + PA...  1.62 us
  transfers between devices with their start and end apart: 9, of which 3 were waited for; matrix products, arithmetic and copies ran while one was open for 2% of the time, Pallas kernels for 7%

commit v1 on v0

v1 whole, which is shorter than its diff:
```python
import functools

import jax
import jax.numpy as jnp
from jax import lax
from jax.experimental import pallas as pl
from jax.experimental.pallas import tpu as pltpu
from jax.sharding import PartitionSpec as P

SH = 256
LANES = 128
PACK_ROWS = 16
CHUNK = 16
LIMIT = 16 * 1024 * 1024

f32, bf16, i32 = jnp.float32, jnp.bfloat16, jnp.int32


def split(values):
    high = values.astype(bf16)
    return high, (values - high.astype(f32)).astype(bf16)


def nt_dot(left, right):
    return lax.dot_general(left, right, (((1,), (1,)), ((), ())), preferred_element_type=f32)


def low_table(node_row):
    shape = (LANES, node_row.shape[1])
    low = jnp.broadcast_to(node_row % LANES, shape)
    return (low == lax.broadcasted_iota(i32, shape, 0)).astype(f32).astype(bf16)


def scatter_rows(value_rows, high_row, high_count):
    shape = (high_count, high_row.shape[1])
    mask = jnp.broadcast_to(high_row, shape) == lax.broadcasted_iota(i32, shape, 0)
    rows = [jnp.where(mask, jnp.broadcast_to(v, shape), 0.0) for v in value_rows]
    return jnp.concatenate(split(jnp.concatenate(rows, axis=0)), axis=0)


def masked(values, row, number):
    return values * (row == number).astype(f32).astype(bf16)


def pack_kernel(mortar_ref, offset_ref, out_ref):
    segments, order, _ = mortar_ref.shape
    per_row = out_ref.shape[1] // order
    for first in range(0, segments, per_row):
        row = first // per_row * order
        blocks = [mortar_ref[first + place] for place in range(per_row)]
        out_ref[row : row + order, :] = jnp.concatenate(blocks, axis=1)
    rows = segments // per_row * order
    out_ref[rows:, :] = jnp.zeros((PACK_ROWS, out_ref.shape[1]), bf16)
    out_ref[rows : rows + segments, :order] = offset_ref[...]


def join_kernel(*refs):
    out_ref = refs[-1]
    place = 0
    for ref in refs[:-1]:
        if len(ref.shape) == 2 and ref.shape[1] == out_ref.shape[1]:
            out_ref[place : place + ref.shape[0], :] = ref[...]
            place += ref.shape[0]


def element_part(disp_ref, connect_ref, stiffness_ref, matrix_ref, out_ref, elem_ref, force_ref):
    node_count = disp_ref.shape[1]
    corners, elem_count = connect_ref.shape
    high_count = node_count // LANES
    for start in range(0, elem_count, LANES):
        index = connect_ref[:, start : start + LANES]
        high, low = index // LANES, index % LANES
        for comp in range(3):
            picked = jnp.zeros(index.shape, f32)
            for part in range(high_count):
                line = disp_ref[comp : comp + 1, part * LANES : (part + 1) * LANES]
                table = jnp.broadcast_to(line, (corners, LANES))
                found = jnp.take_along_axis(table, low, axis=1, mode="promise_in_bounds")
                picked = jnp.where(high == part, found, picked)
            elem_ref[start // LANES, pl.ds(comp, corners, stride=3), :] = picked
    m_high, m_low = split(matrix_ref[...])
    d_high, d_low = split(jnp.concatenate([elem_ref[k] for k in range(elem_count // LANES)], axis=1))
    force = (
        jnp.dot(m_high, d_high, preferred_element_type=f32)
        + jnp.dot(m_high, d_low, preferred_element_type=f32)
        + jnp.dot(m_low, d_high, preferred_element_type=f32)
    )
    force_ref[...] = force * stiffness_ref[...]
    total = jnp.zeros((6 * high_count, LANES), f32)
    for corner in range(corners):
        values = [force_ref[3 * corner + c : 3 * corner + c + 1, :] for c in range(3)]
        row = connect_ref[corner : corner + 1, :]
        total = total + nt_dot(scatter_rows(values, row // LANES, high_count), low_table(row))
    out_ref[...] = total[: 3 * high_count] + total[3 * high_count :]


def local_kernel(*refs, place_owner, groups):
    vol_ref, node_ref, connect_ref, stiff_ref, matrix_ref, shape_ref, owner_ref, segment_ref, face_area_ref, face_ref = refs[:10]
    table_ref, rows_ref, area_ref, nodes_ref, both_ref, inner_ref, elem_ref, force_ref = refs[10:]
    element_part(node_ref, connect_ref, stiff_ref, matrix_ref, inner_ref, elem_ref, force_ref)
    order = shape_ref.shape[1]
    per_row = both_ref.shape[1] // order
    segment = segment_ref[...]
    slot = segment % per_row
    rows_ref[0:1, :] = slot
    rows_ref[1:2, :] = segment
    for corner in range(face_ref.shape[0]):
        table_ref[corner * LANES : (corner + 1) * LANES, :] = low_table(face_ref[corner : corner + 1, :])
    for part, local in enumerate(place_owner(owner_ref[...], vol_ref[0])):
        group = jnp.where(local < 0, -1, local * groups + segment // per_row)
        first = 2 + 4 * part
        rows_ref[first : first + 1, :] = group
        rows_ref[first + 1 : first + 2, :] = jnp.where(local < 0, -1, group % per_row)
        rows_ref[first + 2 : first + 3, :] = jnp.where(local < 0, -1, (group // per_row) * per_row + slot)
        rows_ref[first + 3 : first + 4, :] = jnp.where(local < 0, -1, local * PACK_ROWS + segment)
    area_ref[...] = -face_area_ref[...]
    nodes_ref[...] = face_ref[...] // LANES
    sixteen = jnp.concatenate([shape_ref[...], jnp.zeros((16 - shape_ref.shape[0], order), f32)], axis=0)
    zero = jnp.zeros_like(sixteen)
    diagonal = [
        jnp.concatenate([sixteen if r == c else zero for c in range(per_row)], axis=1) for r in range(per_row)
    ]
    both_ref[...] = jnp.concatenate(split(jnp.concatenate(diagonal, axis=0)), axis=0)


def contact_kernel(*refs, payloads, past, last, part, owners, chunk, tile):
    refs = list(refs)

    def take(count):
        taken = refs[:count]
        del refs[:count]
        return taken

    payload_refs = take(payloads)
    disp_ref, rows_ref, both_ref = take(3)
    (past_ref,) = take(1) if past else (None,)
    if last:
        area_ref, nodes_ref, table_ref, inner_ref, parity_ref = take(5)
        out_ref, near_ref, far_ref = take(3)
    else:
        (out_ref,) = take(1)
    blocks_ref, offsets_ref, map_ref, nodal_ref = refs
    order, faces = disp_ref.shape
    width = blocks_ref.shape[1]
    block_rows = blocks_ref.shape[0] // owners
    piece = block_rows + PACK_ROWS
    per_row = width // order
    chunks = blocks_ref.shape[0] // order // chunk
    quads = chunk // per_row
    rows = chunk * order
    size = 16 * per_row

    def at(number, count):
        return pl.ds(number * count if isinstance(number, int) else pl.multiple_of(number * count, count), count)

    place = 0
    for ref in payload_refs:
        for begin in range(0, ref.shape[0], piece):
            blocks_ref[place * block_rows : (place + 1) * block_rows, :] = ref[begin : begin + block_rows, :]
            offsets_ref[:, place * PACK_ROWS : (place + 1) * PACK_ROWS] = jnp.transpose(
                ref[begin + block_rows : begin + piece, :order].astype(f32)
            ).astype(bf16)
            place += 1

    def build(number, _):
        product = nt_dot(both_ref[...], blocks_ref[at(number, rows), :])
        product = product[:size] + product[size:]
        for quad in range(quads):
            both = jnp.concatenate(split(product[:, quad * width : (quad + 1) * width]), axis=0)
            map_ref[number, quad * 2 * size : (quad + 1) * 2 * size, :] = both
        return 0

    if chunks == 1:
        build(0, 0)
    else:
        lax.fori_loop(0, chunks, build, 0)

    def step(index, total):
        cols = at(index, tile)
        slot = rows_ref[0:1, cols]
        group, inner, outer, target = [rows_ref[2 + 4 * part + k : 3 + 4 * part + k, cols] for k in range(4)]
        shape = (owners * PACK_ROWS, tile)
        picks = jnp.broadcast_to(target, shape) == lax.broadcasted_iota(i32, shape, 0)
        gap = -jnp.dot(offsets_ref[...], picks.astype(f32).astype(bf16), preferred_element_type=f32)
        group_wide = jnp.broadcast_to(group, (order, tile))
        spread = jnp.concatenate([masked(disp_ref[:, cols], slot, place) for place in range(per_row)], axis=0)

        def add_gap(number, found):
            product = jnp.dot(blocks_ref[at(number, rows), :], spread, preferred_element_type=f32)
            for place in range(chunk):
                value = product[place * order : (place + 1) * order]
                found = jnp.where(group_wide == number * chunk + place, value, found)
            return found

        zero_gap = jnp.zeros((order, tile), f32)
        gap = gap + (add_gap(0, zero_gap) if chunks == 1 else lax.fori_loop(0, chunks, add_gap, zero_gap))
        pressure = -gap
        traction = jnp.maximum(pressure, 0.0) + jnp.log(1.0 + jnp.exp(-jnp.abs(pressure)))
        traction = traction.astype(bf16)
        pressed = jnp.concatenate([masked(traction, inner, place) for place in range(per_row)], axis=0)
        outer_wide = jnp.broadcast_to(outer, (16, tile))

        def add_nodal(number, found):
            product = jnp.dot(map_ref[number], pressed, preferred_element_type=f32)
            for quad in range(quads):
                for place in range(per_row):
                    row = quad * 2 * size + place * 16
                    value = product[row : row + 16] + product[row + size : row + size + 16]
                    key = (number * quads + quad) * per_row + place
                    found = jnp.where(outer_wide == key, value, found)
            return found

        nodal = past_ref[:, cols] if past else jnp.zeros((16, tile), f32)
        nodal = add_nodal(0, nodal) if chunks == 1 else lax.fori_loop(0, chunks, add_nodal, nodal)
        if not last:
            out_ref[:, cols] = nodal
            return total
        high_count = inner_ref.shape[0] // 3
        nodal_ref[:, cols] = nodal * area_ref[:, cols]
        for corner in range(nodes_ref.shape[0]):
            values = [nodal_ref[3 * corner + c : 3 * corner + c + 1, cols] for c in range(3)]
            placed = scatter_rows(values, nodes_ref[corner : corner + 1, cols], high_count)
            total = total + nt_dot(placed, table_ref[corner * LANES : (corner + 1) * LANES, cols])
        return total

    total = jnp.zeros((2 * inner_ref.shape[0], LANES), f32) if last else 0
    if chunks == 1:
        for index in range(faces // tile):
            total = step(index, total)
    else:
        total = lax.fori_loop(0, faces // tile, step, total)
    if last:
        inner_rows = inner_ref.shape[0]
        unsummed = total[:inner_rows] + total[inner_rows:] + inner_ref[...]
        high_count = inner_rows // 3
        edge = near_ref.shape[1] // LANES
        odd = parity_ref[0] == 1
        for c in range(3):
            for high in range(high_count):
                line = unsummed[c * high_count + high : c * high_count + high + 1]
                out_ref[c : c + 1, high * LANES : (high + 1) * LANES] = line
            for high in range(edge):
                low = unsummed[c * high_count + high : c * high_count + high + 1]
                top = (c + 1) * high_count - edge + high
                up = unsummed[top : top + 1]
                lanes = slice(high * LANES, (high + 1) * LANES)
                near_ref[c : c + 1, lanes] = jnp.where(odd, low, up)
                far_ref[c : c + 1, lanes] = jnp.where(odd, up, low)


def vmem():
    return pl.BlockSpec(memory_space=pltpu.VMEM)


def smem():
    return pl.BlockSpec(memory_space=pltpu.SMEM)


def call(kernel, out_shape, specs, scratch=(), flops=0, limit=LIMIT):
    single = not isinstance(out_shape, (list, tuple))
    return pl.pallas_call(
        kernel,
        out_shape=out_shape,
        in_specs=specs,
        out_specs=vmem() if single else [vmem()] * len(out_shape),
        scratch_shapes=list(scratch),
        compiler_params=pltpu.CompilerParams(vmem_limit_bytes=limit),
        cost_estimate=pl.CostEstimate(flops=flops, bytes_accessed=1_000_000, transcendentals=0),
    )


def place_exchanged(owner, vol):
    apart = owner ^ vol
    late = (apart >= 4) & (apart % 2 == 1)
    early = jnp.where(apart < 4, apart, 2 + apart // 2)
    return [jnp.where(late, -1, early), jnp.where(late, (apart - 4) // 2, -1)]


def shards(
    face_disp,
    contact_owner,
    segment,
    face_area,
    face_nodes,
    mortar_blocks,
    gap_offset,
    shape_table,
    node_disp,
    stiffness,
    connect,
    elem_matrix,
):
    vol_count, slab_count = lax.axis_size("vol"), lax.axis_size("slab")
    segments, order, _ = mortar_blocks.shape
    faces = face_disp.shape[1]
    face_corners = face_nodes.shape[0]
    node_count = node_disp.shape[1]
    corners, elem_count = connect.shape
    high_count = node_count // LANES
    per_row = 256 // order
    groups = segments // per_row
    block_rows = groups * order
    width = per_row * order
    vol = lax.axis_index("vol").astype(i32).reshape(1)
    slab = lax.axis_index("slab")
    parity = (slab & 1).astype(i32).reshape(1)

    def payload_shape(owners):
        return jax.ShapeDtypeStruct((owners * (block_rows + PACK_ROWS), width), bf16)

    payload = call(pack_kernel, payload_shape(1), [vmem()] * 2, flops=20_000_000_000)(mortar_blocks, gap_offset)

    exchanged = vol_count == 8
    if exchanged:
        place_owner, counts = place_exchanged, [6, 2]
    else:
        place_owner, counts = (lambda owner, _: [owner]), [vol_count]

    sources = [
        node_disp,
        connect,
        stiffness[None, :],
        elem_matrix,
        shape_table,
        contact_owner.reshape(1, faces),
        segment[None, :],
        face_area[None, :],
        face_nodes,
    ]
    tables, rows, area, nodes, both, internal = call(
        functools.partial(local_kernel, place_owner=place_owner, groups=groups),
        [
            jax.ShapeDtypeStruct((face_corners * LANES, faces), bf16),
            jax.ShapeDtypeStruct((2 + 4 * len(counts), faces), i32),
            jax.ShapeDtypeStruct((1, faces), f32),
            jax.ShapeDtypeStruct((face_corners, faces), i32),
            jax.ShapeDtypeStruct((32 * per_row, width), bf16),
            jax.ShapeDtypeStruct((3 * high_count, LANES), f32),
        ],
        [smem()] + [vmem()] * len(sources),
        [pltpu.VMEM((elem_count // LANES, 3 * corners, LANES), f32), pltpu.VMEM((3 * corners, elem_count), f32)],
        flops=2_000_000_000,
    )(vol, *sources)

    if exchanged:
        def swap(values, mask):
            return lax.ppermute(values, "vol", [(i, i ^ mask) for i in range(vol_count)])

        def join(*pieces):
            owners = sum(piece.shape[0] for piece in pieces if piece.shape[1] == width) // (block_rows + PACK_ROWS)
            return call(join_kernel, payload_shape(owners), [vmem()] * len(pieces))(*pieces)

        beside = swap(payload, 1)
        far, middle = swap(payload, 6), swap(payload, 4)
        near = swap(join(payload, beside), 2)
        late = swap(join(middle, far, area), 1)
        parts = [[payload, beside, near, middle, far], [late]]
    else:
        parts = [[lax.all_gather(payload, "vol", tiled=True)]]

    tile = min(512, faces)
    nodal = None
    for part, pieces in enumerate(parts):
        past, last = part > 0, part == len(parts) - 1
        owners = counts[part]
        chunk = min(CHUNK, owners * groups)
        operands = pieces + [face_disp, rows, both]
        specs = [vmem()] * len(operands)
        outs = jax.ShapeDtypeStruct((16, faces), f32)
        if past:
            operands.append(nodal)
            specs.append(vmem())
        if last:
            operands += [area, nodes, tables, internal, parity]
            specs += [vmem()] * 4 + [smem()]
            outs = [
                jax.ShapeDtypeStruct((3, node_count), f32),
                jax.ShapeDtypeStruct((3, SH), f32),
                jax.ShapeDtypeStruct((3, SH), f32),
            ]
        nodal = call(
            functools.partial(
                contact_kernel,
                payloads=len(pieces),
                past=past,
                last=last,
                part=part,
                owners=owners,
                chunk=chunk,
                tile=tile,
            ),
            outs,
            specs,
            [
                pltpu.VMEM((owners * block_rows, width), bf16),
                pltpu.VMEM((order, owners * PACK_ROWS), bf16),
                pltpu.VMEM((owners * groups // chunk, 32 * chunk, width), bf16),
                pltpu.VMEM((16, faces), f32),
            ],
            flops=1_000_000_000,
        )(*operands)
    unsummed, near_out, far_out = nodal
    near_pairs = [(i, i + 1) for i in range(0, slab_count - 1, 2)]
    far_pairs = [(i, i + 1) for i in range(1, slab_count - 1, 2)]
    far_in = lax.ppermute(far_out, "slab", far_pairs + [(b, a) for a, b in far_pairs])
    near_in = lax.ppermute(near_out, "slab", near_pairs + [(b, a) for a, b in near_pairs])
    odd = parity[0] == 1
    lower = unsummed[:, :SH] + jnp.where(odd, near_in, far_in)
    upper = unsummed[:, node_count - SH :] + jnp.where(odd, far_in, near_in)
    return jnp.concatenate([lower, unsummed[:, SH : node_count - SH], upper], axis=1)


def solution(mesh):
    in_specs = (
        P(None, ("vol", "slab")),
        P(("vol", "slab"), None),
        P(("vol", "slab")),
        P(("vol", "slab")),
        P(None, ("vol", "slab")),
        P(("vol", "slab"), None, None),
        P(("vol", "slab"), None),
        P(),
        P(None, ("vol", "slab")),
        P(("vol", "slab")),
        P(None, ("vol", "slab")),
        P(),
    )
    out_specs = P(None, ("vol", "slab"))
    return jax.shard_map(shards, mesh=mesh, in_specs=in_specs, out_specs=out_specs, check_vma=False)
```

time: 39.1 us -> 27.6 us (0.71)
  Pallas kernels: 13.8 us -> 7.13 us
  starting transfers between devices: 15.6 us -> 12.7 us
  waiting for transfers between devices: 7.48 us -> 5.19 us
  local copies, waits for them, and re-layouts: 1.23 us -> 1.63 us
    pallas_call x4 -> x6, Pallas kernels: 13.8 us -> 7.13 us  [the longest x2 4.69 us: shards(): call(functools.partial(contact_kernel, payloads=len(pieces), past=past, l...]
    ppermute x9 -> x7, starting transfers between devices: 15.6 us -> 12.7 us  [the longest x5 6.09 us: swap(): lax.ppermute(values, 'vol', [(i, i ^ mask) for i in range(vol_count)])]
    ppermute x9 -> x7, waiting for transfers between devices: 7.48 us -> 5.19 us  [the longest x5 3.35 us: swap(): lax.ppermute(values, 'vol', [(i, i ^ mask) for i in range(vol_count)])]
    another operation x1 -> x0, other arithmetic: 0.66 us -> none  [shards(): scalars = jnp.stack([vol, slab % 2]).astype(i32)]
    concatenate x0 -> x1, other arithmetic: none -> 0.61 us  [shards(): jnp.concatenate([lower, unsummed[:, SH:node_count - SH], upper], axis=1)]
    unnamed x20 -> x24, local copies, waits for them, and re-layouts: 1.23 us -> 1.63 us
  transfers between devices with their start and end apart: 9 -> 7, of which waited for: 3 -> 3; matrix products, arithmetic and copies ran while one was open for 2% -> 0% of each run, Pallas kernels for 7% -> 17%
where the time goes in v1:
time: 27.6 us; the launch traced here: 27.4 us
  starting transfers between devices  12.7 us (46%)
  Pallas kernels  7.13 us (26%)
  waiting for transfers between devices  5.19 us (19%)
  local copies, waits for them, and re-layouts  1.63 us (6%)
  other arithmetic  0.62 us (2%)
    ppermute x5, starting transfers between devices, swap(): lax.ppermute(values, 'vol', [(i, i ^ mask) for i in range(vol_count)])  6.09 us
    pallas_call x2, Pallas kernels, shards(): call(functools.partial(contact_kernel, payloads=len(pieces), past=past, l...  4.69 us
    ppermute x1, starting transfers between devices, shards(): lax.ppermute(near_out, 'slab', near_pairs + [(b, a) for a, b in near_pairs])  3.55 us
    ppermute x5, waiting for transfers between devices, swap(): lax.ppermute(values, 'vol', [(i, i ^ mask) for i in range(vol_count)])  3.35 us
    ppermute x1, starting transfers between devices, shards(): lax.ppermute(far_out, 'slab', far_pairs + [(b, a) for a, b in far_pairs])  3.05 us
    pallas_call x1, Pallas kernels, shards(): call(functools.partial(local_kernel, place_owner=place_owner, groups=grou...  2.34 us
    ppermute x1, waiting for transfers between devices, shards(): lax.ppermute(far_out, 'slab', far_pairs + [(b, a) for a, b in far_pairs])  1.84 us
    unnamed x24, local copies, waits for them, and re-layouts  1.63 us
  transfers between devices with their start and end apart: 7, of which 3 were waited for; matrix products, arithmetic and copies ran while one was open for 0% of the time, Pallas kernels for 17%

profile of v1, /device:TPU:1, one launch (start us, length us, event | category | flops | bytes accessed | tf_op | source)
XLA Modules:
  0.0 27.4 jit_solution(2716910879403378605)
XLA Ops:
  0.0 0.0 copy-start.1
  0.0 0.9 %copy-done.1 = bf16[8,64,64]{2,1,0:T(8,128)(2,1)S(1)} copy-done((bf16[8,64,64]{2,1,0:T(8,128)(2,1)S(1)}, bf16[8,64,64]{2,1,0:T(8,128)(2,1)}, u32[]{:S(2)}) %copy-start.1) | copy-done | bytes 65560
  0.9 0.0 copy-start.11
  0.9 0.7 %copy-done.11 = bf16[8,64]{1,0:T(8,128)(2,1)S(1)} copy-done((bf16[8,64]{1,0:T(8,128)(2,1)S(1)}, bf16[8,64]{1,0:T(8,128)(2,1)}, u32[]{:S(2)}) %copy-start.11) | copy-done | bytes 1048
  1.6 0.0 copy-start.2
  1.6 0.0 copy-start.3
  1.6 0.0 copy-start.4
  1.6 0.0 copy-start.5
  1.6 0.0 copy-start.6
  1.6 0.0 copy-start.7
  1.6 0.0 copy-start.8
  1.6 0.0 copy-start.9
  1.6 0.0 copy-start.10
  1.6 0.1 shard_map.118.refs_0_
  1.7 2.1 %collective-permute-start.3 = (bf16[144,256]{1,0:T(8,128)(2,1)S(1)}, bf16[144,256]{1,0:T(8,128)(2,1)S(1)}, u32[]{:S(2)}, u32[]{:S(2)}) collective-permute-start(bf16[144,256]{1,0:T(8,128)(2,1)S(1)} %shard_map.118.refs_0_), channel_id=1, source_target_pairs={{0,4},{4,0},{8,12},{12,8},{16,20},{20,16},{24,28},{28,24},{1,5},{5... | collective-permute-start | bytes 221192 | tf_op jit(solution)/shard_map/ppermute | solution.py:347
  3.8 2.3 %collective-permute-start = (bf16[144,256]{1,0:T(8,128)(2,1)S(1)}, bf16[144,256]{1,0:T(8,128)(2,1)S(1)}, u32[]{:S(2)}, u32[]{:S(2)}) collective-permute-start(bf16[144,256]{1,0:T(8,128)(2,1)S(1)} %shard_map.118.refs_0_), channel_id=1, source_target_pairs={{0,16},{4,20},{8,24},{12,28},{16,0},{20,4},{24,8},{28,12},{1,17},{... | collective-permute-start | bytes 221192 | tf_op jit(solution)/shard_map/ppermute | solution.py:347
  6.1 1.1 %collective-permute-start.1 = (bf16[144,256]{1,0:T(8,128)(2,1)S(1)}, bf16[144,256]{1,0:T(8,128)(2,1)S(1)}, u32[]{:S(2)}, u32[]{:S(2)}) collective-permute-start(bf16[144,256]{1,0:T(8,128)(2,1)S(1)} %shard_map.118.refs_0_), channel_id=1, source_target_pairs={{0,24},{4,28},{8,16},{12,20},{16,8},{20,12},{24,0},{28,4},{1,25},{... | collective-permute-start | bytes 221192 | tf_op jit(solution)/shard_map/ppermute | solution.py:347
  7.2 0.0 collective-permute-done.3.refs_1_
  7.2 0.3 %collective-permute-start.4 = (bf16[288,256]{1,0:T(8,128)(2,1)S(1)}, bf16[288,256]{1,0:T(8,128)(2,1)S(1)}, u32[]{:S(2)}, u32[]{:S(2)}) collective-permute-start(bf16[288,256]{1,0:T(8,128)(2,1)S(1)} %shard_map.121), channel_id=1, source_target_pairs={{0,8},{4,12},{8,0},{12,4},{16,24},{20,28},{24,16},{28,20},{1,9},{5... | collective-permute-start | bytes 442376 | tf_op jit(solution)/shard_map/ppermute | solution.py:347
  7.5 0.0 copy-done.2
  7.5 0.0 copy-done.3
  7.5 0.0 copy-done.4
  7.5 0.0 copy-done.5
  7.5 0.0 copy-done.6
  7.5 0.0 copy-done.7
  7.6 0.0 copy-done.8
  7.6 0.0 copy-done.9
  7.6 0.0 copy-done.10
  7.6 0.0 copy-start
  7.6 2.3 %shard_map.119 = (bf16[512,2048]{1,0:T(8,128)(2,1)S(1)}, s32[10,2048]{1,0:T(8,128)S(1)}, f32[1,2048]{1,0:T(1,128)S(1)}, s32[4,2048]{1,0:T(4,128)S(1)}, bf16[128,...) custom-call(s32[1]{0:T(128)} %bitcast.refs_0_, f32[3,1024]{1,0:T(4,128)S(1)} %copy-done.4, s32[8,1024]{1,0:T(8,128)S(1)} %copy-done.2, ...), custom_call_target="tpu_custom_call" | custom-call | flops 2000000000 | bytes 1000000 | tf_op jit(solution)/shard_map/pallas_call | solution.py:330
  9.9 0.0 collective-permute-done.refs_0_.refs_3_
  10.0 1.4 %collective-permute-done.1.refs_1_.refs_4_ = bf16[144,256]{1,0:T(8,128)(2,1)S(1)} collective-permute-done((bf16[144,256]{1,0:T(8,128)(2,1)S(1)}, bf16[144,256]{1,0:T(8,128)(2,1)S(1)}, u32[]{:S(2)}, u32[]{:S(2)}) %collective-permute-start.1) | collective-permute-done | bytes 73760 | tf_op jit(solution)/shard_map/ppermute | solution.py:347
  11.4 0.3 %collective-permute-start.2 = (bf16[288,256]{1,0:T(8,128)(2,1)S(1)}, bf16[288,256]{1,0:T(8,128)(2,1)S(1)}, u32[]{:S(2)}, u32[]{:S(2)}) collective-permute-start(bf16[288,256]{1,0:T(8,128)(2,1)S(1)} %shard_map.120), channel_id=1, source_target_pairs={{0,4},{4,0},{8,12},{12,8},{16,20},{20,16},{24,28},{28,24},{1,5},{5... | collective-permute-start | bytes 442376 | tf_op jit(solution)/shard_map/ppermute | solution.py:347
  11.7 1.9 %collective-permute-done.4.refs_2_ = bf16[288,256]{1,0:T(8,128)(2,1)S(1)} collective-permute-done((bf16[288,256]{1,0:T(8,128)(2,1)S(1)}, bf16[288,256]{1,0:T(8,128)(2,1)S(1)}, u32[]{:S(2)}, u32[]{:S(2)}) %collective-permute-start.4) | collective-permute-done | bytes 147488 | tf_op jit(solution)/shard_map/ppermute | solution.py:347
  13.6 0.0 copy-done
  13.6 2.4 %shard_map.122.refs_4_ = f32[16,2048]{1,0:T(8,128)S(1)} custom-call(bf16[144,256]{1,0:T(8,128)(2,1)S(1)} %shard_map.118.refs_0_, bf16[144,256]{1,0:T(8,128)(2,1)S(1)} %collective-permute-done.3.refs_1_, bf16[288,256]{1,0:T(8,128)(2,1)S(1)} %collective-permute-done.4.refs_2_, bf16[144,256]{1,0:T(8,128)(2,1)S(1)} %collective-permute-done.refs_0_.refs_3_, ...), custom_call_target="tpu_custom_call" | custom-call | flops 1000000000 | bytes 1000000 | tf_op jit(solution)/shard_map/pallas_call | solution.py:381
  16.1 0.0 collective-permute-done.2.refs_0_
  16.1 2.3 %shard_map.123 = (f32[3,1024]{1,0:T(4,128)S(1)}, f32[3,256]{1,0:T(4,128)S(1)}, f32[3,256]{1,0:T(4,128)S(1)}) custom-call(bf16[288,256]{1,0:T(8,128)(2,1)S(1)} %collective-permute-done.2.refs_0_, bf16[64,2048]{1,0:T(8,128)(2,1)S(1)} %copy-done, s32[10,2048]{1,0:T(8,128)S(1)} %get-tuple-element.15.refs_6_.refs_2_, ...), custom_call_target="tpu_custom_call" | custom-call | flops 1000000000 | bytes 1000000 | tf_op jit(solution)/shard_map/pallas_call | solution.py:381
  18.4 3.6 %collective-permute-start.5 = (f32[3,256]{1,0:T(4,128)S(1)}, f32[3,256]{1,0:T(4,128)S(1)}, u32[]{:S(2)}, u32[]{:S(2)}) collective-permute-start(f32[3,256]{1,0:T(4,128)S(1)} %get-tuple-element.21), channel_id=1, source_target_pairs={{0,1},{2,3},{1,0},{3,2},{4,5},{6,7},{5,4},{7,6},{8,9},{10,11},{9,8... | collective-permute-start | bytes 9224 | tf_op jit(solution)/shard_map/ppermute | solution.py:406
  21.9 3.0 %collective-permute-start.6 = (f32[3,256]{1,0:T(4,128)S(1)}, f32[3,256]{1,0:T(4,128)S(1)}, u32[]{:S(2)}, u32[]{:S(2)}) collective-permute-start(f32[3,256]{1,0:T(4,128)S(1)} %get-tuple-element.22), channel_id=1, source_target_pairs={{1,2},{2,1},{5,6},{6,5},{9,10},{10,9},{13,14},{14,13},{17,18},{18,... | collective-permute-start | bytes 9224 | tf_op jit(solution)/shard_map/ppermute | solution.py:405
  25.0 0.0 collective-permute-done.5
  25.0 1.8 %collective-permute-done.6 = f32[3,256]{1,0:T(4,128)S(1)} collective-permute-done((f32[3,256]{1,0:T(4,128)S(1)}, f32[3,256]{1,0:T(4,128)S(1)}, u32[]{:S(2)}, u32[]{:S(2)}) %collective-permute-start.6) | collective-permute-done | bytes 3104 | tf_op jit(solution)/shard_map/ppermute | solution.py:405
  26.8 0.6 %pad_maximum_fusion = f32[3,1024]{1,0:T(4,128)} fusion(f32[3,256]{1,0:T(4,128)S(1)} %get-tuple-element.24, f32[3,512]{1,0:T(4,128)S(1)} %slice.10, f32[3,256]{1,0:T(4,128)S(1)} %get-tuple-element.23), kind=kLoop, calls=%fused_computation | loop fusion | flops 6144 | bytes 24576 | tf_op jit(solution)/shard_map/concatenate | solution.py:410
  (4 shorter events, 0.0 us)
Async XLA Ops:
  0.0 0.9 %copy-start.1 = (bf16[8,64,64]{2,1,0:T(8,128)(2,1)S(1)}, bf16[8,64,64]{2,1,0:T(8,128)(2,1)}, u32[]{:S(2)}) copy-start(bf16[8,64,64]{2,1,0:T(8,128)(2,1)} %mortar_ref.1) | copy-start | bytes 196612
  0.9 0.7 %copy-start.11 = (bf16[8,64]{1,0:T(8,128)(2,1)S(1)}, bf16[8,64]{1,0:T(8,128)(2,1)}, u32[]{:S(2)}) copy-start(bf16[8,64]{1,0:T(8,128)(2,1)} %offset_ref.1) | copy-start | bytes 3076
  1.6 5.9 %copy-start.2 = (s32[8,1024]{1,0:T(8,128)S(1)}, s32[8,1024]{1,0:T(8,128)}, u32[]{:S(2)}) copy-start(s32[8,1024]{1,0:T(8,128)} %refs_2_.1) | copy-start | bytes 98308
  1.6 5.9 %copy-start.3 = (s32[4,2048]{1,0:T(4,128)S(1)}, s32[4,2048]{1,0:T(4,128)}, u32[]{:S(2)}) copy-start(s32[4,2048]{1,0:T(4,128)} %refs_9_.1) | copy-start | bytes 98308
  1.6 5.9 %copy-start.4 = (f32[3,1024]{1,0:T(4,128)S(1)}, f32[3,1024]{1,0:T(4,128)}, u32[]{:S(2)}) copy-start(f32[3,1024]{1,0:T(4,128)} %refs_1_.2) | copy-start | bytes 36868
  1.6 5.9 %copy-start.5 = (f32[24,24]{1,0:T(8,128)S(1)}, f32[24,24]{1,0:T(8,128)}, u32[]{:S(2)}) copy-start(f32[24,24]{1,0:T(8,128)} %refs_4_.1) | copy-start | bytes 6916
  1.6 5.9 %copy-start.6 = (f32[12,64]{1,0:T(8,128)S(1)}, f32[12,64]{1,0:T(8,128)}, u32[]{:S(2)}) copy-start(f32[12,64]{1,0:T(8,128)} %refs_5_.2) | copy-start | bytes 9220
  1.6 5.9 %copy-start.7 = (s32[2048,1]{0,1:T(1,128)S(1)}, s32[2048,1]{0,1:T(1,128)}, u32[]{:S(2)}) copy-start(s32[2048,1]{0,1:T(1,128)} %param.13) | copy-start | bytes 24580
  1.6 5.9 %copy-start.8 = (s32[2048]{0:T(1024)S(1)}, s32[2048]{0:T(1024)}, u32[]{:S(2)}) copy-start(s32[2048]{0:T(1024)} %param.14) | copy-start | bytes 24580
  1.6 5.9 %copy-start.9 = (f32[2048]{0:T(1024)S(1)}, f32[2048]{0:T(1024)}, u32[]{:S(2)}) copy-start(f32[2048]{0:T(1024)} %param.15) | copy-start | bytes 24580
  1.6 5.9 %copy-start.10 = (f32[1024]{0:T(1024)S(1)}, f32[1024]{0:T(1024)}, u32[]{:S(2)}) copy-start(f32[1024]{0:T(1024)} %param.21) | copy-start | bytes 12292
  1.7 5.5 %collective-permute-start.3 = (bf16[144,256]{1,0:T(8,128)(2,1)S(1)}, bf16[144,256]{1,0:T(8,128)(2,1)S(1)}, u32[]{:S(2)}, u32[]{:S(2)}) collective-permute-start(bf16[144,256]{1,0:T(8,128)(2,1)S(1)} %shard_map.118.refs_0_), channel_id=1, source_target_pairs={{0,4},{4,0},{8,12},{12,8},{16,20},{20,16},{24,28},{28,24},{1,5},{5... | collective-permute-start | bytes 221192 | tf_op jit(solution)/shard_map/ppermute | solution.py:347
  3.8 6.1 %collective-permute-start = (bf16[144,256]{1,0:T(8,128)(2,1)S(1)}, bf16[144,256]{1,0:T(8,128)(2,1)S(1)}, u32[]{:S(2)}, u32[]{:S(2)}) collective-permute-start(bf16[144,256]{1,0:T(8,128)(2,1)S(1)} %shard_map.118.refs_0_), channel_id=1, source_target_pairs={{0,16},{4,20},{8,24},{12,28},{16,0},{20,4},{24,8},{28,12},{1,17},{... | collective-permute-start | bytes 221192 | tf_op jit(solution)/shard_map/ppermute | solution.py:347
  6.1 5.2 %collective-permute-start.1 = (bf16[144,256]{1,0:T(8,128)(2,1)S(1)}, bf16[144,256]{1,0:T(8,128)(2,1)S(1)}, u32[]{:S(2)}, u32[]{:S(2)}) collective-permute-start(bf16[144,256]{1,0:T(8,128)(2,1)S(1)} %shard_map.118.refs_0_), channel_id=1, source_target_pairs={{0,24},{4,28},{8,16},{12,20},{16,8},{20,12},{24,0},{28,4},{1,25},{... | collective-permute-start | bytes 221192 | tf_op jit(solution)/shard_map/ppermute | solution.py:347
  7.2 6.4 %collective-permute-start.4 = (bf16[288,256]{1,0:T(8,128)(2,1)S(1)}, bf16[288,256]{1,0:T(8,128)(2,1)S(1)}, u32[]{:S(2)}, u32[]{:S(2)}) collective-permute-start(bf16[288,256]{1,0:T(8,128)(2,1)S(1)} %shard_map.121), channel_id=1, source_target_pairs={{0,8},{4,12},{8,0},{12,4},{16,24},{20,28},{24,16},{28,20},{1,9},{5... | collective-permute-start | bytes 442376 | tf_op jit(solution)/shard_map/ppermute | solution.py:347
  7.6 6.0 %copy-start = (bf16[64,2048]{1,0:T(8,128)(2,1)S(1)}, bf16[64,2048]{1,0:T(8,128)(2,1)}, u32[]{:S(2)}) copy-start(bf16[64,2048]{1,0:T(8,128)(2,1)} %refs_1_.3) | copy-start | bytes 786436
  11.4 4.7 %collective-permute-start.2 = (bf16[288,256]{1,0:T(8,128)(2,1)S(1)}, bf16[288,256]{1,0:T(8,128)(2,1)S(1)}, u32[]{:S(2)}, u32[]{:S(2)}) collective-permute-start(bf16[288,256]{1,0:T(8,128)(2,1)S(1)} %shard_map.120), channel_id=1, source_target_pairs={{0,4},{4,0},{8,12},{12,8},{16,20},{20,16},{24,28},{28,24},{1,5},{5... | collective-permute-start | bytes 442376 | tf_op jit(solution)/shard_map/ppermute | solution.py:347
  18.4 6.6 %collective-permute-start.5 = (f32[3,256]{1,0:T(4,128)S(1)}, f32[3,256]{1,0:T(4,128)S(1)}, u32[]{:S(2)}, u32[]{:S(2)}) collective-permute-start(f32[3,256]{1,0:T(4,128)S(1)} %get-tuple-element.21), channel_id=1, source_target_pairs={{0,1},{2,3},{1,0},{3,2},{4,5},{6,7},{5,4},{7,6},{8,9},{10,11},{9,8... | collective-permute-start | bytes 9224 | tf_op jit(solution)/shard_map/ppermute | solution.py:406
  21.9 4.9 %collective-permute-start.6 = (f32[3,256]{1,0:T(4,128)S(1)}, f32[3,256]{1,0:T(4,128)S(1)}, u32[]{:S(2)}, u32[]{:S(2)}) collective-permute-start(f32[3,256]{1,0:T(4,128)S(1)} %get-tuple-element.22), channel_id=1, source_target_pairs={{1,2},{2,1},{5,6},{6,5},{9,10},{10,9},{13,14},{14,13},{17,18},{18,... | collective-permute-start | bytes 9224 | tf_op jit(solution)/shard_map/ppermute | solution.py:405

commit v2 on v1

--- a/solution.py
+++ b/solution.py
@@ -9,7 +9,7 @@
 
 SH = 256
 LANES = 128
-PACK_ROWS = 16
+PACK_ROWS = 8
 CHUNK = 16
 LIMIT = 16 * 1024 * 1024
 
@@ -42,7 +42,11 @@
     return values * (row == number).astype(f32).astype(bf16)
 
 
-def pack_kernel(mortar_ref, offset_ref, out_ref):
+def lead_kernel(out_ref):
+    out_ref[...] = jnp.zeros(out_ref.shape, f32)
+
+
+def pack_kernel(mortar_ref, offset_ref, _, out_ref):
     segments, order, _ = mortar_ref.shape
     per_row = out_ref.shape[1] // order
     for first in range(0, segments, per_row):
@@ -154,13 +158,13 @@
         return pl.ds(number * count if isinstance(number, int) else pl.multiple_of(number * count, count), count)
 
     place = 0
+    lines = []
     for ref in payload_refs:
         for begin in range(0, ref.shape[0], piece):
             blocks_ref[place * block_rows : (place + 1) * block_rows, :] = ref[begin : begin + block_rows, :]
-            offsets_ref[:, place * PACK_ROWS : (place + 1) * PACK_ROWS] = jnp.transpose(
-                ref[begin + block_rows : begin + piece, :order].astype(f32)
-            ).astype(bf16)
+            lines.append(ref[begin + block_rows : begin + piece, :order].astype(f32))
             place += 1
+    offsets_ref[...] = jnp.transpose(jnp.concatenate(lines, axis=0)).astype(bf16)
 
     def build(number, _):
         product = nt_dot(both_ref[...], blocks_ref[at(number, rows), :])
@@ -272,7 +276,7 @@
 def place_exchanged(owner, vol):
     apart = owner ^ vol
     late = (apart >= 4) & (apart % 2 == 1)
-    early = jnp.where(apart < 4, apart, 2 + apart // 2)
+    early = jnp.where(apart < 4, (apart % 2) * 2 + apart // 2, 2 + apart // 2)
     return [jnp.where(late, -1, early), jnp.where(late, (apart - 4) // 2, -1)]
 
 
@@ -308,7 +312,8 @@
     def payload_shape(owners):
         return jax.ShapeDtypeStruct((owners * (block_rows + PACK_ROWS), width), bf16)
 
-    payload = call(pack_kernel, payload_shape(1), [vmem()] * 2, flops=20_000_000_000)(mortar_blocks, gap_offset)
+    lead = call(lead_kernel, jax.ShapeDtypeStruct((8, LANES), f32), [], flops=20_000_000_000)()
+    payload = call(pack_kernel, payload_shape(1), [vmem()] * 3, flops=20_000_000_000)(mortar_blocks, gap_offset, lead)
 
     exchanged = vol_count == 8
     if exchanged:
@@ -350,11 +355,10 @@
             owners = sum(piece.shape[0] for piece in pieces if piece.shape[1] == width) // (block_rows + PACK_ROWS)
             return call(join_kernel, payload_shape(owners), [vmem()] * len(pieces))(*pieces)
 
-        beside = swap(payload, 1)
-        far, middle = swap(payload, 6), swap(payload, 4)
-        near = swap(join(payload, beside), 2)
+        far, middle, near = swap(payload, 6), swap(payload, 4), swap(payload, 2)
+        early = swap(join(payload, near), 1)
         late = swap(join(middle, far, area), 1)
-        parts = [[payload, beside, near, middle, far], [late]]
+        parts = [[payload, near, early, middle, far], [late]]
     else:
         parts = [[lax.all_gather(payload, "vol", tiled=True)]]
 
@@ -402,9 +406,13 @@
     unsummed, near_out, far_out = nodal
     near_pairs = [(i, i + 1) for i in range(0, slab_count - 1, 2)]
     far_pairs = [(i, i + 1) for i in range(1, slab_count - 1, 2)]
+    if slab_count % 2 == 0:
+        far_pairs.append((0, slab_count - 1))
     far_in = lax.ppermute(far_out, "slab", far_pairs + [(b, a) for a, b in far_pairs])
     near_in = lax.ppermute(near_out, "slab", near_pairs + [(b, a) for a, b in near_pairs])
     odd = parity[0] == 1
+    inside = (slab > 0) & (slab < slab_count - 1) if slab_count % 2 == 0 else True
+    far_in = jnp.where(inside, far_in, 0.0)
     lower = unsummed[:, :SH] + jnp.where(odd, near_in, far_in)
     upper = unsummed[:, node_count - SH :] + jnp.where(odd, far_in, near_in)
     return jnp.concatenate([lower, unsummed[:, SH : node_count - SH], upper], axis=1)

time: 27.6 us -> 24.3 us (0.88)
  waiting for transfers between devices: 5.19 us -> 3.25 us
  starting transfers between devices: 12.7 us -> 11.9 us
  local copies, waits for them, and re-layouts: 1.63 us -> 0.96 us
    ppermute x5, waiting for transfers between devices: 3.35 us -> 1.43 us  [swap(): lax.ppermute(values, 'vol', [(i, i ^ mask) for i in range(vol_count)])]
    ppermute x1, starting transfers between devices: 3.05 us -> 1.2 us  [shards(): lax.ppermute(far_out, 'slab', far_pairs + [(b, a) for a, b in far_pairs])]
    ppermute x5, starting transfers between devices: 6.09 us -> 7.04 us  [swap(): lax.ppermute(values, 'vol', [(i, i ^ mask) for i in range(vol_count)])]
    unnamed x24, local copies, waits for them, and re-layouts: 1.63 us -> 0.96 us
  transfers between devices with their start and end apart: 7 -> 7, of which waited for: 3 -> 3; matrix products, arithmetic and copies ran while one was open for 0% -> 0% of each run, Pallas kernels for 17% -> 20%
where the time goes in v2:
time: 24.3 us; the launch traced here: 24.1 us
  starting transfers between devices  11.9 us (49%)
  Pallas kernels  7.14 us (29%)
  waiting for transfers between devices  3.25 us (13%)
  local copies, waits for them, and re-layouts  0.96 us (4%)
  other arithmetic  0.62 us (3%)
    ppermute x5, starting transfers between devices, swap(): lax.ppermute(values, 'vol', [(i, i ^ mask) for i in range(vol_count)])  7.04 us
    pallas_call x2, Pallas kernels, shards(): call(functools.partial(contact_kernel, payloads=len(pieces), past=past, l...  4.7 us
    ppermute x1, starting transfers between devices, shards(): lax.ppermute(near_out, 'slab', near_pairs + [(b, a) for a, b in near_pairs])  3.7 us
    pallas_call x1, Pallas kernels, shards(): call(functools.partial(local_kernel, place_owner=place_owner, groups=grou...  2.34 us
    ppermute x1, waiting for transfers between devices, shards(): lax.ppermute(far_out, 'slab', far_pairs + [(b, a) for a, b in far_pairs])  1.82 us
    ppermute x5, waiting for transfers between devices, swap(): lax.ppermute(values, 'vol', [(i, i ^ mask) for i in range(vol_count)])  1.43 us
    ppermute x1, starting transfers between devices, shards(): lax.ppermute(far_out, 'slab', far_pairs + [(b, a) for a, b in far_pairs])  1.2 us
    unnamed x24, local copies, waits for them, and re-layouts  0.96 us
  transfers between devices with their start and end apart: 7, of which 3 were waited for; matrix products, arithmetic and copies ran while one was open for 0% of the time, Pallas kernels for 20%

profile of v2, /device:TPU:1, one launch (start us, length us, event | category | flops | bytes accessed | tf_op | source)
XLA Modules:
  0.0 24.1 jit_solution(6399964447790597117)
XLA Ops:
  0.0 0.0 copy-start.1
  0.0 0.0 copy-start.11
  0.0 0.9 %copy-done.1 = bf16[8,64,64]{2,1,0:T(8,128)(2,1)S(1)} copy-done((bf16[8,64,64]{2,1,0:T(8,128)(2,1)S(1)}, bf16[8,64,64]{2,1,0:T(8,128)(2,1)}, u32[]{:S(2)}) %copy-start.1) | copy-done | bytes 65560
  0.9 0.0 copy-done.11
  0.9 0.0 copy-start.2
  0.9 0.0 copy-start.3
  0.9 0.0 copy-start.4
  0.9 0.0 copy-start.5
  0.9 0.0 copy-start.6
  0.9 0.0 copy-start.7
  1.0 0.0 copy-start.8
  1.0 0.0 copy-start.9
  1.0 0.0 copy-start.10
  1.0 0.1 shard_map.119.refs_0_
  1.1 2.2 %collective-permute-start.3 = (bf16[136,256]{1,0:T(8,128)(2,1)S(1)}, bf16[136,256]{1,0:T(8,128)(2,1)S(1)}, u32[]{:S(2)}, u32[]{:S(2)}) collective-permute-start(bf16[136,256]{1,0:T(8,128)(2,1)S(1)} %shard_map.119.refs_0_), channel_id=1, source_target_pairs={{0,8},{4,12},{8,0},{12,4},{16,24},{20,28},{24,16},{28,20},{1,9},{5... | collective-permute-start | bytes 208904 | tf_op jit(solution)/shard_map/ppermute | solution.py:352
  3.3 2.3 %collective-permute-start = (bf16[136,256]{1,0:T(8,128)(2,1)S(1)}, bf16[136,256]{1,0:T(8,128)(2,1)S(1)}, u32[]{:S(2)}, u32[]{:S(2)}) collective-permute-start(bf16[136,256]{1,0:T(8,128)(2,1)S(1)} %shard_map.119.refs_0_), channel_id=1, source_target_pairs={{0,16},{4,20},{8,24},{12,28},{16,0},{20,4},{24,8},{28,12},{1,17},{... | collective-permute-start | bytes 208904 | tf_op jit(solution)/shard_map/ppermute | solution.py:352
  5.6 0.0 collective-permute-start.1
  5.6 0.0 collective-permute-done.3.refs_1_
  5.6 1.3 %collective-permute-start.4 = (bf16[272,256]{1,0:T(8,128)(2,1)S(1)}, bf16[272,256]{1,0:T(8,128)(2,1)S(1)}, u32[]{:S(2)}, u32[]{:S(2)}) collective-permute-start(bf16[272,256]{1,0:T(8,128)(2,1)S(1)} %shard_map.122), channel_id=1, source_target_pairs={{0,4},{4,0},{8,12},{12,8},{16,20},{20,16},{24,28},{28,24},{1,5},{5... | collective-permute-start | bytes 417800 | tf_op jit(solution)/shard_map/ppermute | solution.py:352
  6.9 0.0 copy-done.2
  6.9 0.0 copy-done.3
  6.9 0.0 copy-done.4
  6.9 0.0 copy-done.5
  6.9 0.0 copy-done.6
  6.9 0.0 copy-done.7
  6.9 0.0 copy-done.8
  6.9 0.0 copy-done.9
  6.9 0.0 copy-done.10
  6.9 0.0 copy-start
  6.9 2.3 %shard_map.120 = (bf16[512,2048]{1,0:T(8,128)(2,1)S(1)}, s32[10,2048]{1,0:T(8,128)S(1)}, f32[1,2048]{1,0:T(1,128)S(1)}, s32[4,2048]{1,0:T(4,128)S(1)}, bf16[128,...) custom-call(s32[1]{0:T(128)} %bitcast.refs_0_, f32[3,1024]{1,0:T(4,128)S(1)} %copy-done.4, s32[8,1024]{1,0:T(8,128)S(1)} %copy-done.2, ...), custom_call_target="tpu_custom_call" | custom-call | flops 2000000000 | bytes 1000000 | tf_op jit(solution)/shard_map/pallas_call | solution.py:335
  9.3 0.0 collective-permute-done.refs_0_.refs_3_
  9.3 1.2 %collective-permute-done.1.refs_1_.refs_4_ = bf16[136,256]{1,0:T(8,128)(2,1)S(1)} collective-permute-done((bf16[136,256]{1,0:T(8,128)(2,1)S(1)}, bf16[136,256]{1,0:T(8,128)(2,1)S(1)}, u32[]{:S(2)}, u32[]{:S(2)}) %collective-permute-start.1) | collective-permute-done | bytes 69664 | tf_op jit(solution)/shard_map/ppermute | solution.py:352
  10.5 1.3 %collective-permute-start.2 = (bf16[272,256]{1,0:T(8,128)(2,1)S(1)}, bf16[272,256]{1,0:T(8,128)(2,1)S(1)}, u32[]{:S(2)}, u32[]{:S(2)}) collective-permute-start(bf16[272,256]{1,0:T(8,128)(2,1)S(1)} %shard_map.121), channel_id=1, source_target_pairs={{0,4},{4,0},{8,12},{12,8},{16,20},{20,16},{24,28},{28,24},{1,5},{5... | collective-permute-start | bytes 417800 | tf_op jit(solution)/shard_map/ppermute | solution.py:352
  11.8 0.0 collective-permute-done.4.refs_2_
  11.8 0.0 copy-done
  11.8 2.5 %shard_map.123.refs_4_ = f32[16,2048]{1,0:T(8,128)S(1)} custom-call(bf16[136,256]{1,0:T(8,128)(2,1)S(1)} %shard_map.119.refs_0_, bf16[136,256]{1,0:T(8,128)(2,1)S(1)} %collective-permute-done.3.refs_1_, bf16[272,256]{1,0:T(8,128)(2,1)S(1)} %collective-permute-done.4.refs_2_, bf16[136,256]{1,0:T(8,128)(2,1)S(1)} %collective-permute-done.refs_0_.refs_3_, ...), custom_call_target="tpu_custom_call" | custom-call | flops 1000000000 | bytes 1000000 | tf_op jit(solution)/shard_map/pallas_call | solution.py:385
  14.3 0.2 collective-permute-done.2.refs_0_
  14.5 2.2 %shard_map.124 = (f32[3,1024]{1,0:T(4,128)S(1)}, f32[3,256]{1,0:T(4,128)S(1)}, f32[3,256]{1,0:T(4,128)S(1)}) custom-call(bf16[272,256]{1,0:T(8,128)(2,1)S(1)} %collective-permute-done.2.refs_0_, bf16[64,2048]{1,0:T(8,128)(2,1)S(1)} %copy-done, s32[10,2048]{1,0:T(8,128)S(1)} %get-tuple-element.15.refs_6_.refs_2_, ...), custom_call_target="tpu_custom_call" | custom-call | flops 1000000000 | bytes 1000000 | tf_op jit(solution)/shard_map/pallas_call | solution.py:385
  16.7 3.7 %collective-permute-start.5 = (f32[3,256]{1,0:T(4,128)S(1)}, f32[3,256]{1,0:T(4,128)S(1)}, u32[]{:S(2)}, u32[]{:S(2)}) collective-permute-start(f32[3,256]{1,0:T(4,128)S(1)} %get-tuple-element.21), channel_id=1, source_target_pairs={{0,1},{2,3},{1,0},{3,2},{4,5},{6,7},{5,4},{7,6},{8,9},{10,11},{9,8... | collective-permute-start | bytes 9224 | tf_op jit(solution)/shard_map/ppermute | solution.py:412
  20.4 1.2 %collective-permute-start.6 = (f32[3,256]{1,0:T(4,128)S(1)}, f32[3,256]{1,0:T(4,128)S(1)}, u32[]{:S(2)}, u32[]{:S(2)}) collective-permute-start(f32[3,256]{1,0:T(4,128)S(1)} %get-tuple-element.22), channel_id=1, source_target_pairs={{1,2},{0,3},{2,1},{3,0},{5,6},{4,7},{6,5},{7,4},{9,10},{8,11},{10,... | collective-permute-start | bytes 9224 | tf_op jit(solution)/shard_map/ppermute | solution.py:411
  21.6 0.0 collective-permute-done.5
  21.6 1.8 %collective-permute-done.6 = f32[3,256]{1,0:T(4,128)S(1)} collective-permute-done((f32[3,256]{1,0:T(4,128)S(1)}, f32[3,256]{1,0:T(4,128)S(1)}, u32[]{:S(2)}, u32[]{:S(2)}) %collective-permute-start.6) | collective-permute-done | bytes 3104 | tf_op jit(solution)/shard_map/ppermute | solution.py:411
  23.5 0.6 %pad_maximum_fusion = f32[3,1024]{1,0:T(4,128)} fusion(f32[3,256]{1,0:T(4,128)S(1)} %get-tuple-element.24, f32[3,512]{1,0:T(4,128)S(1)} %slice.10, f32[3,256]{1,0:T(4,128)S(1)} %get-tuple-element.23), kind=kLoop, calls=%fused_computation | loop fusion | flops 6144 | bytes 24576 | tf_op jit(solution)/shard_map/concatenate | solution.py:418
  (5 shorter events, 0.0 us)
Async XLA Ops:
  0.0 0.9 %copy-start.1 = (bf16[8,64,64]{2,1,0:T(8,128)(2,1)S(1)}, bf16[8,64,64]{2,1,0:T(8,128)(2,1)}, u32[]{:S(2)}) copy-start(bf16[8,64,64]{2,1,0:T(8,128)(2,1)} %mortar_ref.1) | copy-start | bytes 196612
  0.0 0.9 %copy-start.11 = (bf16[8,64]{1,0:T(8,128)(2,1)S(1)}, bf16[8,64]{1,0:T(8,128)(2,1)}, u32[]{:S(2)}) copy-start(bf16[8,64]{1,0:T(8,128)(2,1)} %offset_ref.1) | copy-start | bytes 3076
  0.9 6.0 %copy-start.2 = (s32[8,1024]{1,0:T(8,128)S(1)}, s32[8,1024]{1,0:T(8,128)}, u32[]{:S(2)}) copy-start(s32[8,1024]{1,0:T(8,128)} %refs_2_.1) | copy-start | bytes 98308
  0.9 6.0 %copy-start.3 = (s32[4,2048]{1,0:T(4,128)S(1)}, s32[4,2048]{1,0:T(4,128)}, u32[]{:S(2)}) copy-start(s32[4,2048]{1,0:T(4,128)} %refs_9_.1) | copy-start | bytes 98308
  0.9 6.0 %copy-start.4 = (f32[3,1024]{1,0:T(4,128)S(1)}, f32[3,1024]{1,0:T(4,128)}, u32[]{:S(2)}) copy-start(f32[3,1024]{1,0:T(4,128)} %refs_1_.2) | copy-start | bytes 36868
  0.9 6.0 %copy-start.5 = (f32[24,24]{1,0:T(8,128)S(1)}, f32[24,24]{1,0:T(8,128)}, u32[]{:S(2)}) copy-start(f32[24,24]{1,0:T(8,128)} %refs_4_.1) | copy-start | bytes 6916
  0.9 5.9 %copy-start.6 = (f32[12,64]{1,0:T(8,128)S(1)}, f32[12,64]{1,0:T(8,128)}, u32[]{:S(2)}) copy-start(f32[12,64]{1,0:T(8,128)} %refs_5_.2) | copy-start | bytes 9220
  0.9 5.9 %copy-start.7 = (s32[2048,1]{0,1:T(1,128)S(1)}, s32[2048,1]{0,1:T(1,128)}, u32[]{:S(2)}) copy-start(s32[2048,1]{0,1:T(1,128)} %param.13) | copy-start | bytes 24580
  1.0 5.9 %copy-start.8 = (s32[2048]{0:T(1024)S(1)}, s32[2048]{0:T(1024)}, u32[]{:S(2)}) copy-start(s32[2048]{0:T(1024)} %param.14) | copy-start | bytes 24580
  1.0 5.9 %copy-start.9 = (f32[2048]{0:T(1024)S(1)}, f32[2048]{0:T(1024)}, u32[]{:S(2)}) copy-start(f32[2048]{0:T(1024)} %param.15) | copy-start | bytes 24580
  1.0 5.9 %copy-start.10 = (f32[1024]{0:T(1024)S(1)}, f32[1024]{0:T(1024)}, u32[]{:S(2)}) copy-start(f32[1024]{0:T(1024)} %param.21) | copy-start | bytes 12292
  1.1 4.5 %collective-permute-start.3 = (bf16[136,256]{1,0:T(8,128)(2,1)S(1)}, bf16[136,256]{1,0:T(8,128)(2,1)S(1)}, u32[]{:S(2)}, u32[]{:S(2)}) collective-permute-start(bf16[136,256]{1,0:T(8,128)(2,1)S(1)} %shard_map.119.refs_0_), channel_id=1, source_target_pairs={{0,8},{4,12},{8,0},{12,4},{16,24},{20,28},{24,16},{28,20},{1,9},{5... | collective-permute-start | bytes 208904 | tf_op jit(solution)/shard_map/ppermute | solution.py:352
  3.3 6.0 %collective-permute-start = (bf16[136,256]{1,0:T(8,128)(2,1)S(1)}, bf16[136,256]{1,0:T(8,128)(2,1)S(1)}, u32[]{:S(2)}, u32[]{:S(2)}) collective-permute-start(bf16[136,256]{1,0:T(8,128)(2,1)S(1)} %shard_map.119.refs_0_), channel_id=1, source_target_pairs={{0,16},{4,20},{8,24},{12,28},{16,0},{20,4},{24,8},{28,12},{1,17},{... | collective-permute-start | bytes 208904 | tf_op jit(solution)/shard_map/ppermute | solution.py:352
  5.6 5.0 %collective-permute-start.1 = (bf16[136,256]{1,0:T(8,128)(2,1)S(1)}, bf16[136,256]{1,0:T(8,128)(2,1)S(1)}, u32[]{:S(2)}, u32[]{:S(2)}) collective-permute-start(bf16[136,256]{1,0:T(8,128)(2,1)S(1)} %shard_map.119.refs_0_), channel_id=1, source_target_pairs={{0,24},{4,28},{8,16},{12,20},{16,8},{20,12},{24,0},{28,4},{1,25},{... | collective-permute-start | bytes 208904 | tf_op jit(solution)/shard_map/ppermute | solution.py:352
  5.6 6.2 %collective-permute-start.4 = (bf16[272,256]{1,0:T(8,128)(2,1)S(1)}, bf16[272,256]{1,0:T(8,128)(2,1)S(1)}, u32[]{:S(2)}, u32[]{:S(2)}) collective-permute-start(bf16[272,256]{1,0:T(8,128)(2,1)S(1)} %shard_map.122), channel_id=1, source_target_pairs={{0,4},{4,0},{8,12},{12,8},{16,20},{20,16},{24,28},{28,24},{1,5},{5... | collective-permute-start | bytes 417800 | tf_op jit(solution)/shard_map/ppermute | solution.py:352
  6.9 4.9 %copy-start = (bf16[64,2048]{1,0:T(8,128)(2,1)S(1)}, bf16[64,2048]{1,0:T(8,128)(2,1)}, u32[]{:S(2)}) copy-start(bf16[64,2048]{1,0:T(8,128)(2,1)} %refs_1_.3) | copy-start | bytes 786436
  10.5 4.0 %collective-permute-start.2 = (bf16[272,256]{1,0:T(8,128)(2,1)S(1)}, bf16[272,256]{1,0:T(8,128)(2,1)S(1)}, u32[]{:S(2)}, u32[]{:S(2)}) collective-permute-start(bf16[272,256]{1,0:T(8,128)(2,1)S(1)} %shard_map.121), channel_id=1, source_target_pairs={{0,4},{4,0},{8,12},{12,8},{16,20},{20,16},{24,28},{28,24},{1,5},{5... | collective-permute-start | bytes 417800 | tf_op jit(solution)/shard_map/ppermute | solution.py:352
  16.7 4.9 %collective-permute-start.5 = (f32[3,256]{1,0:T(4,128)S(1)}, f32[3,256]{1,0:T(4,128)S(1)}, u32[]{:S(2)}, u32[]{:S(2)}) collective-permute-start(f32[3,256]{1,0:T(4,128)S(1)} %get-tuple-element.21), channel_id=1, source_target_pairs={{0,1},{2,3},{1,0},{3,2},{4,5},{6,7},{5,4},{7,6},{8,9},{10,11},{9,8... | collective-permute-start | bytes 9224 | tf_op jit(solution)/shard_map/ppermute | solution.py:412
  20.4 3.0 %collective-permute-start.6 = (f32[3,256]{1,0:T(4,128)S(1)}, f32[3,256]{1,0:T(4,128)S(1)}, u32[]{:S(2)}, u32[]{:S(2)}) collective-permute-start(f32[3,256]{1,0:T(4,128)S(1)} %get-tuple-element.22), channel_id=1, source_target_pairs={{1,2},{0,3},{2,1},{3,0},{5,6},{4,7},{6,5},{7,4},{9,10},{8,11},{10,... | collective-permute-start | bytes 9224 | tf_op jit(solution)/shard_map/ppermute | solution.py:411

commit v3 on v2

--- a/solution.py
+++ b/solution.py
@@ -31,11 +31,23 @@
     return (low == lax.broadcasted_iota(i32, shape, 0)).astype(f32).astype(bf16)
 
 
-def scatter_rows(value_rows, high_row, high_count):
+def scatter_rows(highs, lows, high_row, high_count):
     shape = (high_count, high_row.shape[1])
     mask = jnp.broadcast_to(high_row, shape) == lax.broadcasted_iota(i32, shape, 0)
-    rows = [jnp.where(mask, jnp.broadcast_to(v, shape), 0.0) for v in value_rows]
-    return jnp.concatenate(split(jnp.concatenate(rows, axis=0)), axis=0)
+    rows = [jnp.where(mask, jnp.broadcast_to(v, shape), 0.0) for v in highs + lows]
+    return jnp.concatenate(rows, axis=0).astype(bf16)
+
+
+def store_split(ref, cols, values):
+    high, low = split(values)
+    size = values.shape[0]
+    ref[:size, cols] = high.astype(f32)
+    ref[size : 2 * size, cols] = low.astype(f32)
+
+
+def split_rows(ref, corner, size, cols):
+    rows = [3 * corner + c for c in range(3)]
+    return [ref[r : r + 1, cols] for r in rows], [ref[size + r : size + r + 1, cols] for r in rows]
 
 
 def masked(values, row, number):
@@ -89,18 +101,19 @@
         + jnp.dot(m_high, d_low, preferred_element_type=f32)
         + jnp.dot(m_low, d_high, preferred_element_type=f32)
     )
-    force_ref[...] = force * stiffness_ref[...]
+    every = slice(0, elem_count)
+    store_split(force_ref, every, force * stiffness_ref[...])
     total = jnp.zeros((6 * high_count, LANES), f32)
     for corner in range(corners):
-        values = [force_ref[3 * corner + c : 3 * corner + c + 1, :] for c in range(3)]
         row = connect_ref[corner : corner + 1, :]
-        total = total + nt_dot(scatter_rows(values, row // LANES, high_count), low_table(row))
+        placed = scatter_rows(*split_rows(force_ref, corner, 3 * corners, every), row // LANES, high_count)
+        total = total + nt_dot(placed, low_table(row))
     out_ref[...] = total[: 3 * high_count] + total[3 * high_count :]
 
 
 def local_kernel(*refs, place_owner, groups):
-    vol_ref, node_ref, connect_ref, stiff_ref, matrix_ref, shape_ref, owner_ref, segment_ref, face_area_ref, face_ref = refs[:10]
-    table_ref, rows_ref, area_ref, nodes_ref, both_ref, inner_ref, elem_ref, force_ref = refs[10:]
+    vol_ref, odd_ref, node_ref, connect_ref, stiff_ref, matrix_ref, shape_ref, owner_ref, segment_ref, face_area_ref, face_ref = refs[:11]
+    table_ref, rows_ref, area_ref, nodes_ref, both_ref, inner_ref, elem_ref, force_ref = refs[11:]
     element_part(node_ref, connect_ref, stiff_ref, matrix_ref, inner_ref, elem_ref, force_ref)
     order = shape_ref.shape[1]
     per_row = both_ref.shape[1] // order
@@ -110,7 +123,7 @@
     rows_ref[1:2, :] = segment
     for corner in range(face_ref.shape[0]):
         table_ref[corner * LANES : (corner + 1) * LANES, :] = low_table(face_ref[corner : corner + 1, :])
-    for part, local in enumerate(place_owner(owner_ref[...], vol_ref[0])):
+    for part, local in enumerate(place_owner(owner_ref[...], vol_ref[0], odd_ref[0])):
         group = jnp.where(local < 0, -1, local * groups + segment // per_row)
         first = 2 + 4 * part
         rows_ref[first : first + 1, :] = group
@@ -179,7 +192,7 @@
     else:
         lax.fori_loop(0, chunks, build, 0)
 
-    def step(index, total):
+    def find_gap(index):
         cols = at(index, tile)
         slot = rows_ref[0:1, cols]
         group, inner, outer, target = [rows_ref[2 + 4 * part + k : 3 + 4 * part + k, cols] for k in range(4)]
@@ -198,6 +211,10 @@
 
         zero_gap = jnp.zeros((order, tile), f32)
         gap = gap + (add_gap(0, zero_gap) if chunks == 1 else lax.fori_loop(0, chunks, add_gap, zero_gap))
+        return index, gap, inner, outer
+
+    def find_nodal(index, gap, inner, outer):
+        cols = at(index, tile)
         pressure = -gap
         traction = jnp.maximum(pressure, 0.0) + jnp.log(1.0 + jnp.exp(-jnp.abs(pressure)))
         traction = traction.astype(bf16)
@@ -218,21 +235,39 @@
         nodal = add_nodal(0, nodal) if chunks == 1 else lax.fori_loop(0, chunks, add_nodal, nodal)
         if not last:
             out_ref[:, cols] = nodal
+        else:
+            store_split(nodal_ref, cols, nodal * area_ref[:, cols])
+
+    def scatter(index, total):
+        if not last:
             return total
+        cols = at(index, tile)
         high_count = inner_ref.shape[0] // 3
-        nodal_ref[:, cols] = nodal * area_ref[:, cols]
+        placed, tables = [], []
         for corner in range(nodes_ref.shape[0]):
-            values = [nodal_ref[3 * corner + c : 3 * corner + c + 1, cols] for c in range(3)]
-            placed = scatter_rows(values, nodes_ref[corner : corner + 1, cols], high_count)
-            total = total + nt_dot(placed, table_ref[corner * LANES : (corner + 1) * LANES, cols])
-        return total
+            halves = split_rows(nodal_ref, corner, 16, cols)
+            placed.append(scatter_rows(*halves, nodes_ref[corner : corner + 1, cols], high_count))
+            tables.append(table_ref[corner * LANES : (corner + 1) * LANES, cols])
+        return total + nt_dot(jnp.concatenate(placed, axis=1), jnp.concatenate(tables, axis=1))
 
     total = jnp.zeros((2 * inner_ref.shape[0], LANES), f32) if last else 0
+    count = faces // tile
     if chunks == 1:
-        for index in range(faces // tile):
-            total = step(index, total)
+        found = {}
+        for turn in range(count + 2):
+            if turn < count:
+                found[turn] = find_gap(turn)
+            if 0 <= turn - 1 < count:
+                find_nodal(*found.pop(turn - 1))
+            if 0 <= turn - 2:
+                total = scatter(turn - 2, total)
     else:
-        total = lax.fori_loop(0, faces // tile, step, total)
+
+        def step(index, total):
+            find_nodal(*find_gap(index))
+            return scatter(index, total)
+
+        total = lax.fori_loop(0, count, step, total)
     if last:
         inner_rows = inner_ref.shape[0]
         unsummed = total[:inner_rows] + total[inner_rows:] + inner_ref[...]
@@ -273,11 +308,17 @@
     )
 
 
-def place_exchanged(owner, vol):
+ORDERS = ((2, 4, 6), (4, 6, 2))
+
+
+def place_exchanged(owner, vol, odd_slab):
     apart = owner ^ vol
-    late = (apart >= 4) & (apart % 2 == 1)
-    early = jnp.where(apart < 4, (apart % 2) * 2 + apart // 2, 2 + apart // 2)
-    return [jnp.where(late, -1, early), jnp.where(late, (apart - 4) // 2, -1)]
+    beside, pair = apart % 2, apart // 2
+    turned = jnp.where(pair == 0, 0, (pair + 1) % 3 + 1)
+    step = jnp.where(odd_slab == 1, turned, pair)
+    late = (step >= 2) & (beside == 1)
+    early = jnp.where(step < 2, beside * 2 + step, step + 2)
+    return [jnp.where(late, -1, early), jnp.where(late, step - 2, -1)]
 
 
 def shards(
@@ -319,7 +360,7 @@
     if exchanged:
         place_owner, counts = place_exchanged, [6, 2]
     else:
-        place_owner, counts = (lambda owner, _: [owner]), [vol_count]
+        place_owner, counts = (lambda owner, *_: [owner]), [vol_count]
 
     sources = [
         node_disp,
@@ -342,32 +383,37 @@
             jax.ShapeDtypeStruct((32 * per_row, width), bf16),
             jax.ShapeDtypeStruct((3 * high_count, LANES), f32),
         ],
-        [smem()] + [vmem()] * len(sources),
-        [pltpu.VMEM((elem_count // LANES, 3 * corners, LANES), f32), pltpu.VMEM((3 * corners, elem_count), f32)],
+        [smem()] * 2 + [vmem()] * len(sources),
+        [pltpu.VMEM((elem_count // LANES, 3 * corners, LANES), f32), pltpu.VMEM((6 * corners, elem_count), f32)],
         flops=2_000_000_000,
-    )(vol, *sources)
+    )(vol, parity, *sources)
 
     if exchanged:
-        def swap(values, mask):
-            return lax.ppermute(values, "vol", [(i, i ^ mask) for i in range(vol_count)])
+        def swap(values, masks):
+            pairs = [
+                (v * slab_count + s, (v ^ masks[s % 2]) * slab_count + s)
+                for v in range(vol_count)
+                for s in range(slab_count)
+            ]
+            return lax.ppermute(values, ("vol", "slab"), pairs)
 
         def join(*pieces):
             owners = sum(piece.shape[0] for piece in pieces if piece.shape[1] == width) // (block_rows + PACK_ROWS)
             return call(join_kernel, payload_shape(owners), [vmem()] * len(pieces))(*pieces)
 
-        far, middle, near = swap(payload, 6), swap(payload, 4), swap(payload, 2)
-        early = swap(join(payload, near), 1)
-        late = swap(join(middle, far, area), 1)
-        parts = [[payload, near, early, middle, far], [late]]
+        one, two, three = [swap(payload, masks) for masks in zip(*ORDERS)]
+        early = swap(join(payload, one), (1, 1))
+        late = [swap(join(two, area), (1, 1)), swap(three, (1, 1))]
+        parts = [[payload, one, early, two, three], late]
     else:
         parts = [[lax.all_gather(payload, "vol", tiled=True)]]
 
-    tile = min(512, faces)
     nodal = None
     for part, pieces in enumerate(parts):
         past, last = part > 0, part == len(parts) - 1
         owners = counts[part]
         chunk = min(CHUNK, owners * groups)
+        tile = min(256 if last else 512, faces)
         operands = pieces + [face_disp, rows, both]
         specs = [vmem()] * len(operands)
         outs = jax.ShapeDtypeStruct((16, faces), f32)
@@ -399,7 +445,7 @@
                 pltpu.VMEM((owners * block_rows, width), bf16),
                 pltpu.VMEM((order, owners * PACK_ROWS), bf16),
                 pltpu.VMEM((owners * groups // chunk, 32 * chunk, width), bf16),
-                pltpu.VMEM((16, faces), f32),
+                pltpu.VMEM((32, faces), f32),
             ],
             flops=1_000_000_000,
         )(*operands)

time: 24.3 us -> 23.1 us (0.951)
  Pallas kernels: 7.14 us -> 6.29 us
  starting transfers between devices: 11.9 us -> 11.5 us
    pallas_call x2, Pallas kernels: 4.7 us -> 3.8 us  [shards(): call(functools.partial(contact_kernel, payloads=len(pieces), past=past, l...]
    ppermute x1, starting transfers between devices: 3.7 us -> 3.03 us  [shards(): lax.ppermute(near_out, 'slab', near_pairs + [(b, a) for a, b in near_pairs])]
    ppermute x5 -> x6, starting transfers between devices: 7.04 us -> 7.3 us  [swap(): return lax.ppermute(values, ('vol', 'slab'), pairs)]
    ppermute x5 -> x6, waiting for transfers between devices: 1.43 us -> 1.46 us  [swap(): return lax.ppermute(values, ('vol', 'slab'), pairs)]
  transfers between devices with their start and end apart: 7 -> 8, of which waited for: 3 -> 3; matrix products, arithmetic and copies ran while one was open for 0% -> 0% of each run, Pallas kernels for 20% -> 19%
where the time goes in v3:
time: 23.1 us; the launch traced here: 22.9 us
  starting transfers between devices  11.5 us (50%)
  Pallas kernels  6.29 us (27%)
  waiting for transfers between devices  3.28 us (14%)
  local copies, waits for them, and re-layouts  0.96 us (4%)
  other arithmetic  0.62 us (3%)
    ppermute x6, starting transfers between devices, swap(): return lax.ppermute(values, ('vol', 'slab'), pairs)  7.3 us
    pallas_call x2, Pallas kernels, shards(): call(functools.partial(contact_kernel, payloads=len(pieces), past=past, l...  3.8 us
    ppermute x1, starting transfers between devices, shards(): lax.ppermute(near_out, 'slab', near_pairs + [(b, a) for a, b in near_pairs])  3.03 us
    pallas_call x1, Pallas kernels, shards(): call(functools.partial(local_kernel, place_owner=place_owner, groups=grou...  2.38 us
    ppermute x1, waiting for transfers between devices, shards(): lax.ppermute(far_out, 'slab', far_pairs + [(b, a) for a, b in far_pairs])  1.82 us
    ppermute x6, waiting for transfers between devices, swap(): return lax.ppermute(values, ('vol', 'slab'), pairs)  1.46 us
    ppermute x1, starting transfers between devices, shards(): lax.ppermute(far_out, 'slab', far_pairs + [(b, a) for a, b in far_pairs])  1.2 us
    unnamed x24, local copies, waits for them, and re-layouts  0.96 us
  transfers between devices with their start and end apart: 8, of which 3 were waited for; matrix products, arithmetic and copies ran while one was open for 0% of the time, Pallas kernels for 19%

profile of v3, /device:TPU:1, one launch (start us, length us, event | category | flops | bytes accessed | tf_op | source)
XLA Modules:
  0.0 22.9 jit_solution(693772181158344217)
XLA Ops:
  0.0 0.0 copy-start.1
  0.0 0.0 copy-start.11
  0.0 0.9 %copy-done.1 = bf16[8,64,64]{2,1,0:T(8,128)(2,1)S(1)} copy-done((bf16[8,64,64]{2,1,0:T(8,128)(2,1)S(1)}, bf16[8,64,64]{2,1,0:T(8,128)(2,1)}, u32[]{:S(2)}) %copy-start.1) | copy-done | bytes 65560
  0.9 0.0 copy-done.11
  0.9 0.0 copy-start.2
  0.9 0.0 copy-start.3
  0.9 0.0 copy-start.4
  0.9 0.0 copy-start.5
  0.9 0.0 copy-start.6
  0.9 0.0 copy-start.7
  1.0 0.0 copy-start.8
  1.0 0.0 copy-start.9
  1.0 0.0 copy-start.10
  1.0 0.1 shard_map.119.refs_0_
  1.1 3.2 %collective-permute-start.4 = (bf16[136,256]{1,0:T(8,128)(2,1)S(1)}, bf16[136,256]{1,0:T(8,128)(2,1)S(1)}, u32[]{:S(2)}, u32[]{:S(2)}) collective-permute-start(bf16[136,256]{1,0:T(8,128)(2,1)S(1)} %shard_map.119.refs_0_), channel_id=1, source_target_pairs={{0,8},{1,17},{2,10},{3,19},{4,12},{5,21},{6,14},{7,23},{8,0},{9,25... | collective-permute-start | bytes 208904 | tf_op jit(solution)/shard_map/ppermute | solution.py:398
  4.3 1.1 %collective-permute-start = (bf16[136,256]{1,0:T(8,128)(2,1)S(1)}, bf16[136,256]{1,0:T(8,128)(2,1)S(1)}, u32[]{:S(2)}, u32[]{:S(2)}) collective-permute-start(bf16[136,256]{1,0:T(8,128)(2,1)S(1)} %shard_map.119.refs_0_), channel_id=1, source_target_pairs={{0,16},{1,25},{2,18},{3,27},{4,20},{5,29},{6,22},{7,31},{8,24},{9,... | collective-permute-start | bytes 208904 | tf_op jit(solution)/shard_map/ppermute | solution.py:398
  5.4 0.2 collective-permute-start.2
  5.6 0.6 %collective-permute-done.4.refs_1_ = bf16[136,256]{1,0:T(8,128)(2,1)S(1)} collective-permute-done((bf16[136,256]{1,0:T(8,128)(2,1)S(1)}, bf16[136,256]{1,0:T(8,128)(2,1)S(1)}, u32[]{:S(2)}, u32[]{:S(2)}) %collective-permute-start.4) | collective-permute-done | bytes 69664 | tf_op jit(solution)/shard_map/ppermute | solution.py:398
  6.2 1.3 %collective-permute-start.5 = (bf16[272,256]{1,0:T(8,128)(2,1)S(1)}, bf16[272,256]{1,0:T(8,128)(2,1)S(1)}, u32[]{:S(2)}, u32[]{:S(2)}) collective-permute-start(bf16[272,256]{1,0:T(8,128)(2,1)S(1)} %shard_map.122), channel_id=1, source_target_pairs={{0,4},{1,5},{2,6},{3,7},{4,0},{5,1},{6,2},{7,3},{8,12},{9,13},{10,... | collective-permute-start | bytes 417800 | tf_op jit(solution)/shard_map/ppermute | solution.py:398
  7.4 0.0 copy-done.2
  7.4 0.0 copy-done.3
  7.4 0.0 copy-done.4
  7.4 0.0 copy-done.5
  7.4 0.0 copy-done.6
  7.5 0.0 copy-done.7
  7.5 0.0 copy-done.8
  7.5 0.0 copy-done.9
  7.5 0.0 copy-done.10
  7.5 0.0 copy-start
  7.5 2.4 %shard_map.120 = (bf16[512,2048]{1,0:T(8,128)(2,1)S(1)}, s32[10,2048]{1,0:T(8,128)S(1)}, f32[1,2048]{1,0:T(1,128)S(1)}, s32[4,2048]{1,0:T(4,128)S(1)}, bf16[128,...) custom-call(s32[1]{0:T(128)} %bitcast.refs_0_, s32[1]{0:T(128)} %bitcast.1.refs_1_.refs_10_, f32[3,1024]{1,0:T(4,128)S(1)} %copy-done.4, ...), custom_call_target="tpu_custom_call" | custom-call | flops 2000000000 | bytes 1000000 | tf_op jit(solution)/shard_map/pallas_call | solution.py:376
  9.9 0.0 collective-permute-done.refs_0_.refs_3_
  9.9 1.2 %collective-permute-start.1 = (bf16[136,256]{1,0:T(8,128)(2,1)S(1)}, bf16[136,256]{1,0:T(8,128)(2,1)S(1)}, u32[]{:S(2)}, u32[]{:S(2)}) collective-permute-start(bf16[136,256]{1,0:T(8,128)(2,1)S(1)} %shard_map.121), channel_id=1, source_target_pairs={{0,4},{1,5},{2,6},{3,7},{4,0},{5,1},{6,2},{7,3},{8,12},{9,13},{10,... | collective-permute-start | bytes 208904 | tf_op jit(solution)/shard_map/ppermute | solution.py:398
  11.1 0.0 collective-permute-done.2.refs_4_
  11.1 0.4 %collective-permute-start.3 = (bf16[136,256]{1,0:T(8,128)(2,1)S(1)}, bf16[136,256]{1,0:T(8,128)(2,1)S(1)}, u32[]{:S(2)}, u32[]{:S(2)}) collective-permute-start(bf16[136,256]{1,0:T(8,128)(2,1)S(1)} %collective-permute-done.2.refs_4_), channel_id=1, source_target_pairs={{0,4},{1,5},{2,6},{3,7},{4,0},{5,1},{6,2},{7,3},{8,12},{9,13},{10,... | collective-permute-start | bytes 208904 | tf_op jit(solution)/shard_map/ppermute | solution.py:398
  11.5 0.0 collective-permute-done.5.refs_2_
  11.5 0.0 copy-done
  11.5 1.9 %shard_map.123.refs_5_ = f32[16,2048]{1,0:T(8,128)S(1)} custom-call(bf16[136,256]{1,0:T(8,128)(2,1)S(1)} %shard_map.119.refs_0_, bf16[136,256]{1,0:T(8,128)(2,1)S(1)} %collective-permute-done.4.refs_1_, bf16[272,256]{1,0:T(8,128)(2,1)S(1)} %collective-permute-done.5.refs_2_, bf16[136,256]{1,0:T(8,128)(2,1)S(1)} %collective-permute-done.refs_0_.refs_3_, ...), custom_call_target="tpu_custom_call" | custom-call | flops 1000000000 | bytes 1000000 | tf_op jit(solution)/shard_map/pallas_call | solution.py:431
  13.4 0.0 collective-permute-done.1.refs_0_
  13.4 0.9 %collective-permute-done.3.refs_1_ = bf16[136,256]{1,0:T(8,128)(2,1)S(1)} collective-permute-done((bf16[136,256]{1,0:T(8,128)(2,1)S(1)}, bf16[136,256]{1,0:T(8,128)(2,1)S(1)}, u32[]{:S(2)}, u32[]{:S(2)}) %collective-permute-start.3) | collective-permute-done | bytes 69664 | tf_op jit(solution)/shard_map/ppermute | solution.py:398
  14.3 1.9 %shard_map.124 = (f32[3,1024]{1,0:T(4,128)S(1)}, f32[3,256]{1,0:T(4,128)S(1)}, f32[3,256]{1,0:T(4,128)S(1)}) custom-call(bf16[136,256]{1,0:T(8,128)(2,1)S(1)} %collective-permute-done.1.refs_0_, bf16[136,256]{1,0:T(8,128)(2,1)S(1)} %collective-permute-done.3.refs_1_, bf16[64,2048]{1,0:T(8,128)(2,1)S(1)} %copy-done, ...), custom_call_target="tpu_custom_call" | custom-call | flops 1000000000 | bytes 1000000 | tf_op jit(solution)/shard_map/pallas_call | solution.py:431
  16.2 3.0 %collective-permute-start.6 = (f32[3,256]{1,0:T(4,128)S(1)}, f32[3,256]{1,0:T(4,128)S(1)}, u32[]{:S(2)}, u32[]{:S(2)}) collective-permute-start(f32[3,256]{1,0:T(4,128)S(1)} %get-tuple-element.21), channel_id=1, source_target_pairs={{0,1},{2,3},{1,0},{3,2},{4,5},{6,7},{5,4},{7,6},{8,9},{10,11},{9,8... | collective-permute-start | bytes 9224 | tf_op jit(solution)/shard_map/ppermute | solution.py:458
  19.2 1.2 %collective-permute-start.7 = (f32[3,256]{1,0:T(4,128)S(1)}, f32[3,256]{1,0:T(4,128)S(1)}, u32[]{:S(2)}, u32[]{:S(2)}) collective-permute-start(f32[3,256]{1,0:T(4,128)S(1)} %get-tuple-element.22), channel_id=1, source_target_pairs={{1,2},{0,3},{2,1},{3,0},{5,6},{4,7},{6,5},{7,4},{9,10},{8,11},{10,... | collective-permute-start | bytes 9224 | tf_op jit(solution)/shard_map/ppermute | solution.py:457
  20.4 0.0 collective-permute-done.6
  20.4 1.8 %collective-permute-done.7 = f32[3,256]{1,0:T(4,128)S(1)} collective-permute-done((f32[3,256]{1,0:T(4,128)S(1)}, f32[3,256]{1,0:T(4,128)S(1)}, u32[]{:S(2)}, u32[]{:S(2)}) %collective-permute-start.7) | collective-permute-done | bytes 3104 | tf_op jit(solution)/shard_map/ppermute | solution.py:457
  22.2 0.6 %pad_maximum_fusion = f32[3,1024]{1,0:T(4,128)} fusion(f32[3,256]{1,0:T(4,128)S(1)} %get-tuple-element.24, f32[3,512]{1,0:T(4,128)S(1)} %slice.10, f32[3,256]{1,0:T(4,128)S(1)} %get-tuple-element.23), kind=kLoop, calls=%fused_computation | loop fusion | flops 6144 | bytes 24576 | tf_op jit(solution)/shard_map/concatenate | solution.py:464
  (5 shorter events, 0.0 us)
Async XLA Ops:
  0.0 0.9 %copy-start.1 = (bf16[8,64,64]{2,1,0:T(8,128)(2,1)S(1)}, bf16[8,64,64]{2,1,0:T(8,128)(2,1)}, u32[]{:S(2)}) copy-start(bf16[8,64,64]{2,1,0:T(8,128)(2,1)} %mortar_ref.1) | copy-start | bytes 196612
  0.0 0.9 %copy-start.11 = (bf16[8,64]{1,0:T(8,128)(2,1)S(1)}, bf16[8,64]{1,0:T(8,128)(2,1)}, u32[]{:S(2)}) copy-start(bf16[8,64]{1,0:T(8,128)(2,1)} %offset_ref.1) | copy-start | bytes 3076
  0.9 6.5 %copy-start.2 = (s32[8,1024]{1,0:T(8,128)S(1)}, s32[8,1024]{1,0:T(8,128)}, u32[]{:S(2)}) copy-start(s32[8,1024]{1,0:T(8,128)} %refs_3_.1) | copy-start | bytes 98308
  0.9 6.5 %copy-start.3 = (s32[4,2048]{1,0:T(4,128)S(1)}, s32[4,2048]{1,0:T(4,128)}, u32[]{:S(2)}) copy-start(s32[4,2048]{1,0:T(4,128)} %refs_10_.1) | copy-start | bytes 98308
  0.9 6.5 %copy-start.4 = (f32[3,1024]{1,0:T(4,128)S(1)}, f32[3,1024]{1,0:T(4,128)}, u32[]{:S(2)}) copy-start(f32[3,1024]{1,0:T(4,128)} %refs_2_.2) | copy-start | bytes 36868
  0.9 6.5 %copy-start.5 = (f32[24,24]{1,0:T(8,128)S(1)}, f32[24,24]{1,0:T(8,128)}, u32[]{:S(2)}) copy-start(f32[24,24]{1,0:T(8,128)} %refs_5_.2) | copy-start | bytes 6916
  0.9 6.5 %copy-start.6 = (f32[12,64]{1,0:T(8,128)S(1)}, f32[12,64]{1,0:T(8,128)}, u32[]{:S(2)}) copy-start(f32[12,64]{1,0:T(8,128)} %refs_6_.1) | copy-start | bytes 9220
  0.9 6.5 %copy-start.7 = (s32[2048,1]{0,1:T(1,128)S(1)}, s32[2048,1]{0,1:T(1,128)}, u32[]{:S(2)}) copy-start(s32[2048,1]{0,1:T(1,128)} %param.13) | copy-start | bytes 24580
  1.0 6.5 %copy-start.8 = (s32[2048]{0:T(1024)S(1)}, s32[2048]{0:T(1024)}, u32[]{:S(2)}) copy-start(s32[2048]{0:T(1024)} %param.14) | copy-start | bytes 24580
  1.0 6.5 %copy-start.9 = (f32[2048]{0:T(1024)S(1)}, f32[2048]{0:T(1024)}, u32[]{:S(2)}) copy-start(f32[2048]{0:T(1024)} %param.15) | copy-start | bytes 24580
  1.0 6.5 %copy-start.10 = (f32[1024]{0:T(1024)S(1)}, f32[1024]{0:T(1024)}, u32[]{:S(2)}) copy-start(f32[1024]{0:T(1024)} %param.21) | copy-start | bytes 12292
  1.1 5.1 %collective-permute-start.4 = (bf16[136,256]{1,0:T(8,128)(2,1)S(1)}, bf16[136,256]{1,0:T(8,128)(2,1)S(1)}, u32[]{:S(2)}, u32[]{:S(2)}) collective-permute-start(bf16[136,256]{1,0:T(8,128)(2,1)S(1)} %shard_map.119.refs_0_), channel_id=1, source_target_pairs={{0,8},{1,17},{2,10},{3,19},{4,12},{5,21},{6,14},{7,23},{8,0},{9,25... | collective-permute-start | bytes 208904 | tf_op jit(solution)/shard_map/ppermute | solution.py:398
  4.3 5.6 %collective-permute-start = (bf16[136,256]{1,0:T(8,128)(2,1)S(1)}, bf16[136,256]{1,0:T(8,128)(2,1)S(1)}, u32[]{:S(2)}, u32[]{:S(2)}) collective-permute-start(bf16[136,256]{1,0:T(8,128)(2,1)S(1)} %shard_map.119.refs_0_), channel_id=1, source_target_pairs={{0,16},{1,25},{2,18},{3,27},{4,20},{5,29},{6,22},{7,31},{8,24},{9,... | collective-permute-start | bytes 208904 | tf_op jit(solution)/shard_map/ppermute | solution.py:398
  5.4 5.7 %collective-permute-start.2 = (bf16[136,256]{1,0:T(8,128)(2,1)S(1)}, bf16[136,256]{1,0:T(8,128)(2,1)S(1)}, u32[]{:S(2)}, u32[]{:S(2)}) collective-permute-start(bf16[136,256]{1,0:T(8,128)(2,1)S(1)} %shard_map.119.refs_0_), channel_id=1, source_target_pairs={{0,24},{1,9},{2,26},{3,11},{4,28},{5,13},{6,30},{7,15},{8,16},{9,1... | collective-permute-start | bytes 208904 | tf_op jit(solution)/shard_map/ppermute | solution.py:398
  6.2 5.3 %collective-permute-start.5 = (bf16[272,256]{1,0:T(8,128)(2,1)S(1)}, bf16[272,256]{1,0:T(8,128)(2,1)S(1)}, u32[]{:S(2)}, u32[]{:S(2)}) collective-permute-start(bf16[272,256]{1,0:T(8,128)(2,1)S(1)} %shard_map.122), channel_id=1, source_target_pairs={{0,4},{1,5},{2,6},{3,7},{4,0},{5,1},{6,2},{7,3},{8,12},{9,13},{10,... | collective-permute-start | bytes 417800 | tf_op jit(solution)/shard_map/ppermute | solution.py:398
  7.5 4.0 %copy-start = (bf16[64,2048]{1,0:T(8,128)(2,1)S(1)}, bf16[64,2048]{1,0:T(8,128)(2,1)}, u32[]{:S(2)}) copy-start(bf16[64,2048]{1,0:T(8,128)(2,1)} %refs_2_.3) | copy-start | bytes 786436
  9.9 3.4 %collective-permute-start.1 = (bf16[136,256]{1,0:T(8,128)(2,1)S(1)}, bf16[136,256]{1,0:T(8,128)(2,1)S(1)}, u32[]{:S(2)}, u32[]{:S(2)}) collective-permute-start(bf16[136,256]{1,0:T(8,128)(2,1)S(1)} %shard_map.121), channel_id=1, source_target_pairs={{0,4},{1,5},{2,6},{3,7},{4,0},{5,1},{6,2},{7,3},{8,12},{9,13},{10,... | collective-permute-start | bytes 208904 | tf_op jit(solution)/shard_map/ppermute | solution.py:398
  11.1 3.2 %collective-permute-start.3 = (bf16[136,256]{1,0:T(8,128)(2,1)S(1)}, bf16[136,256]{1,0:T(8,128)(2,1)S(1)}, u32[]{:S(2)}, u32[]{:S(2)}) collective-permute-start(bf16[136,256]{1,0:T(8,128)(2,1)S(1)} %collective-permute-done.2.refs_4_), channel_id=1, source_target_pairs={{0,4},{1,5},{2,6},{3,7},{4,0},{5,1},{6,2},{7,3},{8,12},{9,13},{10,... | collective-permute-start | bytes 208904 | tf_op jit(solution)/shard_map/ppermute | solution.py:398
  16.2 4.2 %collective-permute-start.6 = (f32[3,256]{1,0:T(4,128)S(1)}, f32[3,256]{1,0:T(4,128)S(1)}, u32[]{:S(2)}, u32[]{:S(2)}) collective-permute-start(f32[3,256]{1,0:T(4,128)S(1)} %get-tuple-element.21), channel_id=1, source_target_pairs={{0,1},{2,3},{1,0},{3,2},{4,5},{6,7},{5,4},{7,6},{8,9},{10,11},{9,8... | collective-permute-start | bytes 9224 | tf_op jit(solution)/shard_map/ppermute | solution.py:458
  19.2 3.0 %collective-permute-start.7 = (f32[3,256]{1,0:T(4,128)S(1)}, f32[3,256]{1,0:T(4,128)S(1)}, u32[]{:S(2)}, u32[]{:S(2)}) collective-permute-start(f32[3,256]{1,0:T(4,128)S(1)} %get-tuple-element.22), channel_id=1, source_target_pairs={{1,2},{0,3},{2,1},{3,0},{5,6},{4,7},{6,5},{7,4},{9,10},{8,11},{10,... | collective-permute-start | bytes 9224 | tf_op jit(solution)/shard_map/ppermute | solution.py:457

commit v4 on v3

--- a/solution.py
+++ b/solution.py
@@ -27,8 +27,9 @@
 
 def low_table(node_row):
     shape = (LANES, node_row.shape[1])
-    low = jnp.broadcast_to(node_row % LANES, shape)
-    return (low == lax.broadcasted_iota(i32, shape, 0)).astype(f32).astype(bf16)
+    low = jnp.broadcast_to((node_row % LANES).astype(f32).astype(bf16), shape)
+    lines = lax.broadcasted_iota(i32, shape, 0).astype(f32).astype(bf16)
+    return jnp.where(low == lines, jnp.ones((), bf16), jnp.zeros((), bf16))
 
 
 def scatter_rows(highs, lows, high_row, high_count):
@@ -79,7 +80,7 @@
             place += ref.shape[0]
 
 
-def element_part(disp_ref, connect_ref, stiffness_ref, matrix_ref, out_ref, elem_ref, force_ref):
+def element_kernel(disp_ref, connect_ref, stiffness_ref, matrix_ref, out_ref, elem_ref, force_ref):
     node_count = disp_ref.shape[1]
     corners, elem_count = connect_ref.shape
     high_count = node_count // LANES
@@ -111,10 +112,9 @@
     out_ref[...] = total[: 3 * high_count] + total[3 * high_count :]
 
 
-def local_kernel(*refs, place_owner, groups):
-    vol_ref, odd_ref, node_ref, connect_ref, stiff_ref, matrix_ref, shape_ref, owner_ref, segment_ref, face_area_ref, face_ref = refs[:11]
-    table_ref, rows_ref, area_ref, nodes_ref, both_ref, inner_ref, elem_ref, force_ref = refs[11:]
-    element_part(node_ref, connect_ref, stiff_ref, matrix_ref, inner_ref, elem_ref, force_ref)
+def table_kernel(
+    vol_ref, odd_ref, shape_ref, owner_ref, segment_ref, face_area_ref, face_ref, table_ref, rows_ref, area_ref, nodes_ref, both_ref, *, place_owner, groups
+):
     order = shape_ref.shape[1]
     per_row = both_ref.shape[1] // order
     segment = segment_ref[...]
@@ -187,18 +187,13 @@
             map_ref[number, quad * 2 * size : (quad + 1) * 2 * size, :] = both
         return 0
 
-    if chunks == 1:
-        build(0, 0)
-    else:
-        lax.fori_loop(0, chunks, build, 0)
-
     def find_gap(index):
         cols = at(index, tile)
         slot = rows_ref[0:1, cols]
         group, inner, outer, target = [rows_ref[2 + 4 * part + k : 3 + 4 * part + k, cols] for k in range(4)]
         shape = (owners * PACK_ROWS, tile)
         picks = jnp.broadcast_to(target, shape) == lax.broadcasted_iota(i32, shape, 0)
-        gap = -jnp.dot(offsets_ref[...], picks.astype(f32).astype(bf16), preferred_element_type=f32)
+        offset = jnp.dot(offsets_ref[...], picks.astype(f32).astype(bf16), preferred_element_type=f32)
         group_wide = jnp.broadcast_to(group, (order, tile))
         spread = jnp.concatenate([masked(disp_ref[:, cols], slot, place) for place in range(per_row)], axis=0)
 
@@ -210,12 +205,11 @@
             return found
 
         zero_gap = jnp.zeros((order, tile), f32)
-        gap = gap + (add_gap(0, zero_gap) if chunks == 1 else lax.fori_loop(0, chunks, add_gap, zero_gap))
-        return index, gap, inner, outer
-
-    def find_nodal(index, gap, inner, outer):
+        product = add_gap(0, zero_gap) if chunks == 1 else lax.fori_loop(0, chunks, add_gap, zero_gap)
+        return index, offset - product, inner, outer
+
+    def find_nodal(index, pressure, inner, outer):
         cols = at(index, tile)
-        pressure = -gap
         traction = jnp.maximum(pressure, 0.0) + jnp.log(1.0 + jnp.exp(-jnp.abs(pressure)))
         traction = traction.astype(bf16)
         pressed = jnp.concatenate([masked(traction, inner, place) for place in range(per_row)], axis=0)
@@ -257,11 +251,14 @@
         for turn in range(count + 2):
             if turn < count:
                 found[turn] = find_gap(turn)
+            if turn == 0:
+                build(0, 0)
             if 0 <= turn - 1 < count:
                 find_nodal(*found.pop(turn - 1))
             if 0 <= turn - 2:
                 total = scatter(turn - 2, total)
     else:
+        lax.fori_loop(0, chunks, build, 0)
 
         def step(index, total):
             find_nodal(*find_gap(index))
@@ -308,17 +305,23 @@
     )
 
 
-ORDERS = ((2, 4, 6), (4, 6, 2))
+STEPS = ((2, 6, 4, 1, 1, 1), (4, 2, 3, 1, 4, 4))
+
+
+def arrivals(masks):
+    one, two, three, early, late_two, late_three = masks
+    return [0, one, early, early ^ one, two, three], [late_two ^ two, late_three ^ three]
 
 
 def place_exchanged(owner, vol, odd_slab):
     apart = owner ^ vol
-    beside, pair = apart % 2, apart // 2
-    turned = jnp.where(pair == 0, 0, (pair + 1) % 3 + 1)
-    step = jnp.where(odd_slab == 1, turned, pair)
-    late = (step >= 2) & (beside == 1)
-    early = jnp.where(step < 2, beside * 2 + step, step + 2)
-    return [jnp.where(late, -1, early), jnp.where(late, step - 2, -1)]
+    places = []
+    for even, odd in zip(*[arrivals(masks) for masks in STEPS]):
+        place = jnp.full_like(apart, -1)
+        for index, (even_mask, odd_mask) in enumerate(zip(even, odd)):
+            place = jnp.where(apart == jnp.where(odd_slab == 1, odd_mask, even_mask), index, place)
+        places.append(place)
+    return places
 
 
 def shards(
@@ -362,31 +365,26 @@
     else:
         place_owner, counts = (lambda owner, *_: [owner]), [vol_count]
 
-    sources = [
-        node_disp,
-        connect,
-        stiffness[None, :],
-        elem_matrix,
-        shape_table,
-        contact_owner.reshape(1, faces),
-        segment[None, :],
-        face_area[None, :],
-        face_nodes,
-    ]
-    tables, rows, area, nodes, both, internal = call(
-        functools.partial(local_kernel, place_owner=place_owner, groups=groups),
+    tables, rows, area, nodes, both = call(
+        functools.partial(table_kernel, place_owner=place_owner, groups=groups),
         [
             jax.ShapeDtypeStruct((face_corners * LANES, faces), bf16),
             jax.ShapeDtypeStruct((2 + 4 * len(counts), faces), i32),
             jax.ShapeDtypeStruct((1, faces), f32),
             jax.ShapeDtypeStruct((face_corners, faces), i32),
             jax.ShapeDtypeStruct((32 * per_row, width), bf16),
-            jax.ShapeDtypeStruct((3 * high_count, LANES), f32),
         ],
-        [smem()] * 2 + [vmem()] * len(sources),
+        [smem()] * 2 + [vmem()] * 5,
+        flops=2_000_000_000,
+    )(vol, parity, shape_table, contact_owner.reshape(1, faces), segment[None, :], face_area[None, :], face_nodes)
+
+    internal = call(
+        element_kernel,
+        jax.ShapeDtypeStruct((3 * high_count, LANES), f32),
+        [vmem()] * 4,
         [pltpu.VMEM((elem_count // LANES, 3 * corners, LANES), f32), pltpu.VMEM((6 * corners, elem_count), f32)],
         flops=2_000_000_000,
-    )(vol, parity, *sources)
+    )(node_disp, connect, stiffness[None, :], elem_matrix)
 
     if exchanged:
         def swap(values, masks):
@@ -401,9 +399,10 @@
             owners = sum(piece.shape[0] for piece in pieces if piece.shape[1] == width) // (block_rows + PACK_ROWS)
             return call(join_kernel, payload_shape(owners), [vmem()] * len(pieces))(*pieces)
 
-        one, two, three = [swap(payload, masks) for masks in zip(*ORDERS)]
-        early = swap(join(payload, one), (1, 1))
-        late = [swap(join(two, area), (1, 1)), swap(three, (1, 1))]
+        masks = list(zip(*STEPS))
+        one, two, three = [swap(payload, masks[k]) for k in range(3)]
+        early = swap(join(payload, one), masks[3])
+        late = [swap(join(two, internal), masks[4]), swap(three, masks[5])]
         parts = [[payload, one, early, two, three], late]
     else:
         parts = [[lax.all_gather(payload, "vol", tiled=True)]]

time: 23.1 us -> 22.7 us (0.983)
  Pallas kernels: 6.29 us -> 5.75 us
  waiting for transfers between devices: 3.28 us -> 3.81 us
  starting transfers between devices: 11.5 us -> 11.2 us
    ppermute x1, starting transfers between devices: 3.03 us -> 1.66 us  [shards(): lax.ppermute(near_out, 'slab', near_pairs + [(b, a) for a, b in near_pairs])]
    ppermute x6, starting transfers between devices: 7.3 us -> 8.34 us  [swap(): return lax.ppermute(values, ('vol', 'slab'), pairs)]
    pallas_call x1 -> x2, Pallas kernels: 2.38 us -> 1.85 us  [the longest x1 1.49 us: shards(): call(element_kernel, jax.ShapeDtypeStruct((3 * high_count, LANES), f32),...]
    ppermute x6, waiting for transfers between devices: 1.46 us -> 1.99 us  [swap(): return lax.ppermute(values, ('vol', 'slab'), pairs)]
  transfers between devices with their start and end apart: 8 -> 8, of which waited for: 3 -> 2; matrix products, arithmetic and copies ran while one was open for 0% -> 0% of each run, Pallas kernels for 19% -> 17%
where the time goes in v4:
time: 22.7 us; the launch traced here: 22.5 us
  starting transfers between devices  11.2 us (49%)
  Pallas kernels  5.75 us (25%)
  waiting for transfers between devices  3.81 us (17%)
  local copies, waits for them, and re-layouts  0.96 us (4%)
  other arithmetic  0.62 us (3%)
    ppermute x6, starting transfers between devices, swap(): return lax.ppermute(values, ('vol', 'slab'), pairs)  8.34 us
    pallas_call x2, Pallas kernels, shards(): call(functools.partial(contact_kernel, payloads=len(pieces), past=past, l...  3.8 us
    ppermute x6, waiting for transfers between devices, swap(): return lax.ppermute(values, ('vol', 'slab'), pairs)  1.99 us
    ppermute x1, waiting for transfers between devices, shards(): lax.ppermute(far_out, 'slab', far_pairs + [(b, a) for a, b in far_pairs])  1.82 us
    ppermute x1, starting transfers between devices, shards(): lax.ppermute(near_out, 'slab', near_pairs + [(b, a) for a, b in near_pairs])  1.66 us
    pallas_call x1, Pallas kernels, shards(): call(element_kernel, jax.ShapeDtypeStruct((3 * high_count, LANES), f32),...  1.49 us
    ppermute x1, starting transfers between devices, shards(): lax.ppermute(far_out, 'slab', far_pairs + [(b, a) for a, b in far_pairs])  1.2 us
    unnamed x24, local copies, waits for them, and re-layouts  0.96 us
  transfers between devices with their start and end apart: 8, of which 2 were waited for; matrix products, arithmetic and copies ran while one was open for 0% of the time, Pallas kernels for 17%

profile of v4, /device:TPU:1, one launch (start us, length us, event | category | flops | bytes accessed | tf_op | source)
XLA Modules:
  0.0 22.5 jit_solution(14263941963350255920)
XLA Ops:
  0.0 0.0 copy-start.1
  0.0 0.0 copy-start.11
  0.0 0.9 %copy-done.1 = bf16[8,64,64]{2,1,0:T(8,128)(2,1)S(1)} copy-done((bf16[8,64,64]{2,1,0:T(8,128)(2,1)S(1)}, bf16[8,64,64]{2,1,0:T(8,128)(2,1)}, u32[]{:S(2)}) %copy-start.1) | copy-done | bytes 65560
  0.9 0.0 copy-done.11
  0.9 0.0 copy-start.2
  0.9 0.0 copy-start.4
  0.9 0.0 copy-start.5
  0.9 0.0 copy-start.10
  0.9 0.1 shard_map.119.refs_0_
  1.0 3.2 %collective-permute-start.4 = (bf16[136,256]{1,0:T(8,128)(2,1)S(1)}, bf16[136,256]{1,0:T(8,128)(2,1)S(1)}, u32[]{:S(2)}, u32[]{:S(2)}) collective-permute-start(bf16[136,256]{1,0:T(8,128)(2,1)S(1)} %shard_map.119.refs_0_), channel_id=1, source_target_pairs={{0,8},{1,17},{2,10},{3,19},{4,12},{5,21},{6,14},{7,23},{8,0},{9,25... | collective-permute-start | bytes 208904 | tf_op jit(solution)/shard_map/ppermute | solution.py:396
  4.2 1.3 %collective-permute-start = (bf16[136,256]{1,0:T(8,128)(2,1)S(1)}, bf16[136,256]{1,0:T(8,128)(2,1)S(1)}, u32[]{:S(2)}, u32[]{:S(2)}) collective-permute-start(bf16[136,256]{1,0:T(8,128)(2,1)S(1)} %shard_map.119.refs_0_), channel_id=1, source_target_pairs={{0,24},{1,9},{2,26},{3,11},{4,28},{5,13},{6,30},{7,15},{8,16},{9,1... | collective-permute-start | bytes 208904 | tf_op jit(solution)/shard_map/ppermute | solution.py:396
  5.5 1.1 %collective-permute-start.2 = (bf16[136,256]{1,0:T(8,128)(2,1)S(1)}, bf16[136,256]{1,0:T(8,128)(2,1)S(1)}, u32[]{:S(2)}, u32[]{:S(2)}) collective-permute-start(bf16[136,256]{1,0:T(8,128)(2,1)S(1)} %shard_map.119.refs_0_), channel_id=1, source_target_pairs={{0,16},{1,13},{2,18},{3,15},{4,20},{5,9},{6,22},{7,11},{8,24},{9,5... | collective-permute-start | bytes 208904 | tf_op jit(solution)/shard_map/ppermute | solution.py:396
  6.6 0.0 copy-done.2
  6.6 0.0 copy-done.4
  6.6 0.0 copy-done.5
  6.6 0.0 copy-done.10
  6.6 0.0 copy-start.3
  6.6 0.0 copy-start.6
  6.6 0.0 copy-start.7
  6.7 0.0 copy-start.8
  6.7 0.0 copy-start.9
  6.7 1.5 %shard_map.120.refs_1_.refs_9_ = f32[24,128]{1,0:T(8,128)S(1)} custom-call(f32[3,1024]{1,0:T(4,128)S(1)} %copy-done.4, s32[8,1024]{1,0:T(8,128)S(1)} %copy-done.2, f32[1,1024]{1,0:T(1,128)S(1)} %bitcast.9, f32[24,24]{1,0:T(8,128)S(1)} %copy-done.5), custom_call_target="tpu_custom_call" | custom-call | flops 2000000000 | bytes 1000000 | tf_op jit(solution)/shard_map/pallas_call | solution.py:381
  8.2 0.0 collective-permute-done.4.refs_1_
  8.2 0.3 %collective-permute-start.5 = (bf16[272,256]{1,0:T(8,128)(2,1)S(1)}, bf16[272,256]{1,0:T(8,128)(2,1)S(1)}, u32[]{:S(2)}, u32[]{:S(2)}) collective-permute-start(bf16[272,256]{1,0:T(8,128)(2,1)S(1)} %shard_map.123), channel_id=1, source_target_pairs={{0,4},{1,5},{2,6},{3,7},{4,0},{5,1},{6,2},{7,3},{8,12},{9,13},{10,... | collective-permute-start | bytes 417800 | tf_op jit(solution)/shard_map/ppermute | solution.py:396
  8.5 0.0 copy-done.3
  8.5 0.0 copy-done.6
  8.5 0.0 copy-done.7
  8.5 0.0 copy-done.8
  8.5 0.0 copy-done.9
  8.6 0.0 copy-start
  8.6 0.4 %shard_map.122 = (bf16[512,2048]{1,0:T(8,128)(2,1)S(1)}, s32[10,2048]{1,0:T(8,128)S(1)}, f32[1,2048]{1,0:T(1,128)S(1)}, s32[4,2048]{1,0:T(4,128)S(1)}, bf16[128,256]{1,0:T(8,128)(2,1)S(1)}) custom-call(s32[1]{0:T(128)} %bitcast.1.vol_ref, s32[1]{0:T(128)} %bitcast.2.odd_ref.refs_10_, f32[12,64]{1,0:T(8,128)S(1)} %copy-done.6, s32[1,2048]{1,0:T(1,128)S(1)} %bitcast.6, ...), custom_call_target="tpu_custom_call" | custom-call | flops 2000000000 | bytes 1000000 | tf_op jit(solution)/shard_map/pallas_call | solution.py:368
  8.9 0.0 collective-permute-done.refs_0_.refs_3_
  9.0 1.7 %collective-permute-start.1 = (bf16[136,256]{1,0:T(8,128)(2,1)S(1)}, bf16[136,256]{1,0:T(8,128)(2,1)S(1)}, u32[]{:S(2)}, u32[]{:S(2)}) collective-permute-start(bf16[136,256]{1,0:T(8,128)(2,1)S(1)} %shard_map.121), channel_id=1, source_target_pairs={{0,4},{1,17},{2,6},{3,19},{4,0},{5,21},{6,2},{7,23},{8,12},{9,25},... | collective-permute-start | bytes 208904 | tf_op jit(solution)/shard_map/ppermute | solution.py:396
  10.7 0.0 collective-permute-done.2.refs_4_
  10.7 0.7 %collective-permute-start.3 = (bf16[136,256]{1,0:T(8,128)(2,1)S(1)}, bf16[136,256]{1,0:T(8,128)(2,1)S(1)}, u32[]{:S(2)}, u32[]{:S(2)}) collective-permute-start(bf16[136,256]{1,0:T(8,128)(2,1)S(1)} %collective-permute-done.2.refs_4_), channel_id=1, source_target_pairs={{0,4},{1,17},{2,6},{3,19},{4,0},{5,21},{6,2},{7,23},{8,12},{9,25},... | collective-permute-start | bytes 208904 | tf_op jit(solution)/shard_map/ppermute | solution.py:396
  11.4 2.0 %collective-permute-done.5.refs_2_ = bf16[272,256]{1,0:T(8,128)(2,1)S(1)} collective-permute-done((bf16[272,256]{1,0:T(8,128)(2,1)S(1)}, bf16[272,256]{1,0:T(8,128)(2,1)S(1)}, u32[]{:S(2)}, u32[]{:S(2)}) %collective-permute-start.5) | collective-permute-done | bytes 139296 | tf_op jit(solution)/shard_map/ppermute | solution.py:396
  13.4 0.0 copy-done
  13.4 1.9 %shard_map.124.refs_5_ = f32[16,2048]{1,0:T(8,128)S(1)} custom-call(bf16[136,256]{1,0:T(8,128)(2,1)S(1)} %shard_map.119.refs_0_, bf16[136,256]{1,0:T(8,128)(2,1)S(1)} %collective-permute-done.4.refs_1_, bf16[272,256]{1,0:T(8,128)(2,1)S(1)} %collective-permute-done.5.refs_2_, bf16[136,256]{1,0:T(8,128)(2,1)S(1)} %collective-permute-done.refs_0_.refs_3_, ...), custom_call_target="tpu_custom_call" | custom-call | flops 1000000000 | bytes 1000000 | tf_op jit(solution)/shard_map/pallas_call | solution.py:430
  15.3 0.0 collective-permute-done.1.refs_0_
  15.3 0.0 collective-permute-done.3.refs_1_
  15.3 1.9 %shard_map.125 = (f32[3,1024]{1,0:T(4,128)S(1)}, f32[3,256]{1,0:T(4,128)S(1)}, f32[3,256]{1,0:T(4,128)S(1)}) custom-call(bf16[136,256]{1,0:T(8,128)(2,1)S(1)} %collective-permute-done.1.refs_0_, bf16[136,256]{1,0:T(8,128)(2,1)S(1)} %collective-permute-done.3.refs_1_, bf16[64,2048]{1,0:T(8,128)(2,1)S(1)} %copy-done, ...), custom_call_target="tpu_custom_call" | custom-call | flops 1000000000 | bytes 1000000 | tf_op jit(solution)/shard_map/pallas_call | solution.py:430
  17.2 1.7 %collective-permute-start.6 = (f32[3,256]{1,0:T(4,128)S(1)}, f32[3,256]{1,0:T(4,128)S(1)}, u32[]{:S(2)}, u32[]{:S(2)}) collective-permute-start(f32[3,256]{1,0:T(4,128)S(1)} %get-tuple-element.19), channel_id=1, source_target_pairs={{0,1},{2,3},{1,0},{3,2},{4,5},{6,7},{5,4},{7,6},{8,9},{10,11},{9,8... | collective-permute-start | bytes 9224 | tf_op jit(solution)/shard_map/ppermute | solution.py:457
  18.9 1.2 %collective-permute-start.7 = (f32[3,256]{1,0:T(4,128)S(1)}, f32[3,256]{1,0:T(4,128)S(1)}, u32[]{:S(2)}, u32[]{:S(2)}) collective-permute-start(f32[3,256]{1,0:T(4,128)S(1)} %get-tuple-element.20), channel_id=1, source_target_pairs={{1,2},{0,3},{2,1},{3,0},{5,6},{4,7},{6,5},{7,4},{9,10},{8,11},{10,... | collective-permute-start | bytes 9224 | tf_op jit(solution)/shard_map/ppermute | solution.py:456
  20.1 0.0 collective-permute-done.6
  20.1 1.8 %collective-permute-done.7 = f32[3,256]{1,0:T(4,128)S(1)} collective-permute-done((f32[3,256]{1,0:T(4,128)S(1)}, f32[3,256]{1,0:T(4,128)S(1)}, u32[]{:S(2)}, u32[]{:S(2)}) %collective-permute-start.7) | collective-permute-done | bytes 3104 | tf_op jit(solution)/shard_map/ppermute | solution.py:456
  21.9 0.6 %pad_maximum_fusion = f32[3,1024]{1,0:T(4,128)} fusion(f32[3,256]{1,0:T(4,128)S(1)} %get-tuple-element.22, f32[3,512]{1,0:T(4,128)S(1)} %slice.10, f32[3,256]{1,0:T(4,128)S(1)} %get-tuple-element.21), kind=kLoop, calls=%fused_computation | loop fusion | flops 6144 | bytes 24576 | tf_op jit(solution)/shard_map/concatenate | solution.py:463
  (5 shorter events, 0.0 us)
Async XLA Ops:
  0.0 0.9 %copy-start.1 = (bf16[8,64,64]{2,1,0:T(8,128)(2,1)S(1)}, bf16[8,64,64]{2,1,0:T(8,128)(2,1)}, u32[]{:S(2)}) copy-start(bf16[8,64,64]{2,1,0:T(8,128)(2,1)} %mortar_ref.1) | copy-start | bytes 196612
  0.0 0.9 %copy-start.11 = (bf16[8,64]{1,0:T(8,128)(2,1)S(1)}, bf16[8,64]{1,0:T(8,128)(2,1)}, u32[]{:S(2)}) copy-start(bf16[8,64]{1,0:T(8,128)(2,1)} %offset_ref.1) | copy-start | bytes 3076
  0.9 5.7 %copy-start.2 = (s32[8,1024]{1,0:T(8,128)S(1)}, s32[8,1024]{1,0:T(8,128)}, u32[]{:S(2)}) copy-start(s32[8,1024]{1,0:T(8,128)} %connect_ref.1) | copy-start | bytes 98308
  0.9 5.7 %copy-start.4 = (f32[3,1024]{1,0:T(4,128)S(1)}, f32[3,1024]{1,0:T(4,128)}, u32[]{:S(2)}) copy-start(f32[3,1024]{1,0:T(4,128)} %disp_ref.1) | copy-start | bytes 36868
  0.9 5.7 %copy-start.5 = (f32[24,24]{1,0:T(8,128)S(1)}, f32[24,24]{1,0:T(8,128)}, u32[]{:S(2)}) copy-start(f32[24,24]{1,0:T(8,128)} %matrix_ref.1) | copy-start | bytes 6916
  0.9 5.7 %copy-start.10 = (f32[1024]{0:T(1024)S(1)}, f32[1024]{0:T(1024)}, u32[]{:S(2)}) copy-start(f32[1024]{0:T(1024)} %param.21) | copy-start | bytes 12292
  1.0 7.2 %collective-permute-start.4 = (bf16[136,256]{1,0:T(8,128)(2,1)S(1)}, bf16[136,256]{1,0:T(8,128)(2,1)S(1)}, u32[]{:S(2)}, u32[]{:S(2)}) collective-permute-start(bf16[136,256]{1,0:T(8,128)(2,1)S(1)} %shard_map.119.refs_0_), channel_id=1, source_target_pairs={{0,8},{1,17},{2,10},{3,19},{4,12},{5,21},{6,14},{7,23},{8,0},{9,25... | collective-permute-start | bytes 208904 | tf_op jit(solution)/shard_map/ppermute | solution.py:396
  4.2 4.7 %collective-permute-start = (bf16[136,256]{1,0:T(8,128)(2,1)S(1)}, bf16[136,256]{1,0:T(8,128)(2,1)S(1)}, u32[]{:S(2)}, u32[]{:S(2)}) collective-permute-start(bf16[136,256]{1,0:T(8,128)(2,1)S(1)} %shard_map.119.refs_0_), channel_id=1, source_target_pairs={{0,24},{1,9},{2,26},{3,11},{4,28},{5,13},{6,30},{7,15},{8,16},{9,1... | collective-permute-start | bytes 208904 | tf_op jit(solution)/shard_map/ppermute | solution.py:396
  5.5 5.2 %collective-permute-start.2 = (bf16[136,256]{1,0:T(8,128)(2,1)S(1)}, bf16[136,256]{1,0:T(8,128)(2,1)S(1)}, u32[]{:S(2)}, u32[]{:S(2)}) collective-permute-start(bf16[136,256]{1,0:T(8,128)(2,1)S(1)} %shard_map.119.refs_0_), channel_id=1, source_target_pairs={{0,16},{1,13},{2,18},{3,15},{4,20},{5,9},{6,22},{7,11},{8,24},{9,5... | collective-permute-start | bytes 208904 | tf_op jit(solution)/shard_map/ppermute | solution.py:396
  6.6 1.9 %copy-start.3 = (s32[4,2048]{1,0:T(4,128)S(1)}, s32[4,2048]{1,0:T(4,128)}, u32[]{:S(2)}) copy-start(s32[4,2048]{1,0:T(4,128)} %face_ref.1) | copy-start | bytes 98308
  6.6 1.9 %copy-start.6 = (f32[12,64]{1,0:T(8,128)S(1)}, f32[12,64]{1,0:T(8,128)}, u32[]{:S(2)}) copy-start(f32[12,64]{1,0:T(8,128)} %shape_ref.1) | copy-start | bytes 9220
  6.6 1.9 %copy-start.7 = (s32[2048,1]{0,1:T(1,128)S(1)}, s32[2048,1]{0,1:T(1,128)}, u32[]{:S(2)}) copy-start(s32[2048,1]{0,1:T(1,128)} %param.13) | copy-start | bytes 24580
  6.7 1.9 %copy-start.8 = (s32[2048]{0:T(1024)S(1)}, s32[2048]{0:T(1024)}, u32[]{:S(2)}) copy-start(s32[2048]{0:T(1024)} %param.14) | copy-start | bytes 24580
  6.7 1.9 %copy-start.9 = (f32[2048]{0:T(1024)S(1)}, f32[2048]{0:T(1024)}, u32[]{:S(2)}) copy-start(f32[2048]{0:T(1024)} %param.15) | copy-start | bytes 24580
  8.2 5.2 %collective-permute-start.5 = (bf16[272,256]{1,0:T(8,128)(2,1)S(1)}, bf16[272,256]{1,0:T(8,128)(2,1)S(1)}, u32[]{:S(2)}, u32[]{:S(2)}) collective-permute-start(bf16[272,256]{1,0:T(8,128)(2,1)S(1)} %shard_map.123), channel_id=1, source_target_pairs={{0,4},{1,5},{2,6},{3,7},{4,0},{5,1},{6,2},{7,3},{8,12},{9,13},{10,... | collective-permute-start | bytes 417800 | tf_op jit(solution)/shard_map/ppermute | solution.py:396
  8.6 4.8 %copy-start = (bf16[64,2048]{1,0:T(8,128)(2,1)S(1)}, bf16[64,2048]{1,0:T(8,128)(2,1)}, u32[]{:S(2)}) copy-start(bf16[64,2048]{1,0:T(8,128)(2,1)} %refs_2_.1) | copy-start | bytes 786436
  9.0 6.3 %collective-permute-start.1 = (bf16[136,256]{1,0:T(8,128)(2,1)S(1)}, bf16[136,256]{1,0:T(8,128)(2,1)S(1)}, u32[]{:S(2)}, u32[]{:S(2)}) collective-permute-start(bf16[136,256]{1,0:T(8,128)(2,1)S(1)} %shard_map.121), channel_id=1, source_target_pairs={{0,4},{1,17},{2,6},{3,19},{4,0},{5,21},{6,2},{7,23},{8,12},{9,25},... | collective-permute-start | bytes 208904 | tf_op jit(solution)/shard_map/ppermute | solution.py:396
  10.7 4.6 %collective-permute-start.3 = (bf16[136,256]{1,0:T(8,128)(2,1)S(1)}, bf16[136,256]{1,0:T(8,128)(2,1)S(1)}, u32[]{:S(2)}, u32[]{:S(2)}) collective-permute-start(bf16[136,256]{1,0:T(8,128)(2,1)S(1)} %collective-permute-done.2.refs_4_), channel_id=1, source_target_pairs={{0,4},{1,17},{2,6},{3,19},{4,0},{5,21},{6,2},{7,23},{8,12},{9,25},... | collective-permute-start | bytes 208904 | tf_op jit(solution)/shard_map/ppermute | solution.py:396
  17.2 2.9 %collective-permute-start.6 = (f32[3,256]{1,0:T(4,128)S(1)}, f32[3,256]{1,0:T(4,128)S(1)}, u32[]{:S(2)}, u32[]{:S(2)}) collective-permute-start(f32[3,256]{1,0:T(4,128)S(1)} %get-tuple-element.19), channel_id=1, source_target_pairs={{0,1},{2,3},{1,0},{3,2},{4,5},{6,7},{5,4},{7,6},{8,9},{10,11},{9,8... | collective-permute-start | bytes 9224 | tf_op jit(solution)/shard_map/ppermute | solution.py:457
  18.9 3.0 %collective-permute-start.7 = (f32[3,256]{1,0:T(4,128)S(1)}, f32[3,256]{1,0:T(4,128)S(1)}, u32[]{:S(2)}, u32[]{:S(2)}) collective-permute-start(f32[3,256]{1,0:T(4,128)S(1)} %get-tuple-element.20), channel_id=1, source_target_pairs={{1,2},{0,3},{2,1},{3,0},{5,6},{4,7},{6,5},{7,4},{9,10},{8,11},{10,... | collective-permute-start | bytes 9224 | tf_op jit(solution)/shard_map/ppermute | solution.py:456

commit v5 on v4

--- a/solution.py
+++ b/solution.py
@@ -30,6 +30,16 @@
     low = jnp.broadcast_to((node_row % LANES).astype(f32).astype(bf16), shape)
     lines = lax.broadcasted_iota(i32, shape, 0).astype(f32).astype(bf16)
     return jnp.where(low == lines, jnp.ones((), bf16), jnp.zeros((), bf16))
+
+
+def low_columns(node_row):
+    pieces = []
+    for start in range(0, node_row.shape[1], LANES):
+        low = (node_row[:, start : start + LANES] % LANES).astype(f32)
+        lines = jnp.transpose(jnp.broadcast_to(low, (LANES, LANES)))
+        hit = lines == lax.broadcasted_iota(i32, (LANES, LANES), 1).astype(f32)
+        pieces.append(hit.astype(f32).astype(bf16))
+    return jnp.concatenate(pieces, axis=0)
 
 
 def scatter_rows(highs, lows, high_row, high_count):
@@ -113,7 +123,7 @@
 
 
 def table_kernel(
-    vol_ref, odd_ref, shape_ref, owner_ref, segment_ref, face_area_ref, face_ref, table_ref, rows_ref, area_ref, nodes_ref, both_ref, *, place_owner, groups
+    vol_ref, odd_ref, shape_ref, owner_ref, segment_ref, face_area_ref, face_ref, disp_ref, table_ref, rows_ref, area_ref, nodes_ref, both_ref, spread_ref, *, place_owner, groups
 ):
     order = shape_ref.shape[1]
     per_row = both_ref.shape[1] // order
@@ -122,7 +132,8 @@
     rows_ref[0:1, :] = slot
     rows_ref[1:2, :] = segment
     for corner in range(face_ref.shape[0]):
-        table_ref[corner * LANES : (corner + 1) * LANES, :] = low_table(face_ref[corner : corner + 1, :])
+        faces = face_ref.shape[1]
+        table_ref[corner * faces : (corner + 1) * faces, :] = low_columns(face_ref[corner : corner + 1, :])
     for part, local in enumerate(place_owner(owner_ref[...], vol_ref[0], odd_ref[0])):
         group = jnp.where(local < 0, -1, local * groups + segment // per_row)
         first = 2 + 4 * part
@@ -130,6 +141,8 @@
         rows_ref[first + 1 : first + 2, :] = jnp.where(local < 0, -1, group % per_row)
         rows_ref[first + 2 : first + 3, :] = jnp.where(local < 0, -1, (group // per_row) * per_row + slot)
         rows_ref[first + 3 : first + 4, :] = jnp.where(local < 0, -1, local * PACK_ROWS + segment)
+    for place in range(per_row):
+        spread_ref[place * order : (place + 1) * order, :] = masked(disp_ref[...], slot, place)
     area_ref[...] = -face_area_ref[...]
     nodes_ref[...] = face_ref[...] // LANES
     sixteen = jnp.concatenate([shape_ref[...], jnp.zeros((16 - shape_ref.shape[0], order), f32)], axis=0)
@@ -157,8 +170,8 @@
     else:
         (out_ref,) = take(1)
     blocks_ref, offsets_ref, map_ref, nodal_ref = refs
-    order, faces = disp_ref.shape
-    width = blocks_ref.shape[1]
+    width, faces = disp_ref.shape
+    order = offsets_ref.shape[0]
     block_rows = blocks_ref.shape[0] // owners
     piece = block_rows + PACK_ROWS
     per_row = width // order
@@ -189,13 +202,12 @@
 
     def find_gap(index):
         cols = at(index, tile)
-        slot = rows_ref[0:1, cols]
         group, inner, outer, target = [rows_ref[2 + 4 * part + k : 3 + 4 * part + k, cols] for k in range(4)]
         shape = (owners * PACK_ROWS, tile)
         picks = jnp.broadcast_to(target, shape) == lax.broadcasted_iota(i32, shape, 0)
         offset = jnp.dot(offsets_ref[...], picks.astype(f32).astype(bf16), preferred_element_type=f32)
         group_wide = jnp.broadcast_to(group, (order, tile))
-        spread = jnp.concatenate([masked(disp_ref[:, cols], slot, place) for place in range(per_row)], axis=0)
+        spread = disp_ref[:, cols]
 
         def add_gap(number, found):
             product = jnp.dot(blocks_ref[at(number, rows), :], spread, preferred_element_type=f32)
@@ -241,8 +253,12 @@
         for corner in range(nodes_ref.shape[0]):
             halves = split_rows(nodal_ref, corner, 16, cols)
             placed.append(scatter_rows(*halves, nodes_ref[corner : corner + 1, cols], high_count))
-            tables.append(table_ref[corner * LANES : (corner + 1) * LANES, cols])
-        return total + nt_dot(jnp.concatenate(placed, axis=1), jnp.concatenate(tables, axis=1))
+            begin = corner * faces + index * tile
+            begin = begin if isinstance(index, int) else pl.multiple_of(begin, tile)
+            tables.append(table_ref[pl.ds(begin, tile), :])
+        return total + jnp.dot(
+            jnp.concatenate(placed, axis=1), jnp.concatenate(tables, axis=0), preferred_element_type=f32
+        )
 
     total = jnp.zeros((2 * inner_ref.shape[0], LANES), f32) if last else 0
     count = faces // tile
@@ -365,18 +381,19 @@
     else:
         place_owner, counts = (lambda owner, *_: [owner]), [vol_count]
 
-    tables, rows, area, nodes, both = call(
+    tables, rows, area, nodes, both, spread = call(
         functools.partial(table_kernel, place_owner=place_owner, groups=groups),
         [
-            jax.ShapeDtypeStruct((face_corners * LANES, faces), bf16),
+            jax.ShapeDtypeStruct((face_corners * faces, LANES), bf16),
             jax.ShapeDtypeStruct((2 + 4 * len(counts), faces), i32),
             jax.ShapeDtypeStruct((1, faces), f32),
             jax.ShapeDtypeStruct((face_corners, faces), i32),
             jax.ShapeDtypeStruct((32 * per_row, width), bf16),
+            jax.ShapeDtypeStruct((width, faces), bf16),
         ],
-        [smem()] * 2 + [vmem()] * 5,
+        [smem()] * 2 + [vmem()] * 6,
         flops=2_000_000_000,
-    )(vol, parity, shape_table, contact_owner.reshape(1, faces), segment[None, :], face_area[None, :], face_nodes)
+    )(vol, parity, shape_table, contact_owner.reshape(1, faces), segment[None, :], face_area[None, :], face_nodes, face_disp)
 
     internal = call(
         element_kernel,
@@ -412,8 +429,8 @@
         past, last = part > 0, part == len(parts) - 1
         owners = counts[part]
         chunk = min(CHUNK, owners * groups)
-        tile = min(256 if last else 512, faces)
-        operands = pieces + [face_disp, rows, both]
+        tile = min(512 if last else 1024, faces)
+        operands = pieces + [spread, rows, both]
         specs = [vmem()] * len(operands)
         outs = jax.ShapeDtypeStruct((16, faces), f32)
         if past:

time: 22.7 us -> 22.2 us (0.978)
  starting transfers between devices: 11.2 us -> 10.7 us
    pallas_call x1, Pallas kernels: 0.35 us -> 1.29 us  [shards(): call(functools.partial(table_kernel, place_owner=place_owner, groups=grou...]
    pallas_call x2, Pallas kernels: 3.8 us -> 3.04 us  [shards(): call(functools.partial(contact_kernel, payloads=len(pieces), past=past, l...]
    ppermute x1, starting transfers between devices: 1.66 us -> 1.17 us  [shards(): lax.ppermute(near_out, 'slab', near_pairs + [(b, a) for a, b in near_pairs])]
    ppermute x6, waiting for transfers between devices: 1.99 us -> 1.76 us  [swap(): return lax.ppermute(values, ('vol', 'slab'), pairs)]
  transfers between devices with their start and end apart: 8 -> 8, of which waited for: 2 -> 3; matrix products, arithmetic and copies ran while one was open for 0% -> 0% of each run, Pallas kernels for 17% -> 20%
where the time goes in v5:
time: 22.2 us; the launch traced here: 22 us
  starting transfers between devices  10.7 us (48%)
  Pallas kernels  5.93 us (27%)
  waiting for transfers between devices  3.59 us (16%)
  local copies, waits for them, and re-layouts  0.96 us (4%)
  other arithmetic  0.62 us (3%)
    ppermute x6, starting transfers between devices, swap(): return lax.ppermute(values, ('vol', 'slab'), pairs)  8.33 us
    pallas_call x2, Pallas kernels, shards(): call(functools.partial(contact_kernel, payloads=len(pieces), past=past, l...  3.04 us
    ppermute x1, waiting for transfers between devices, shards(): lax.ppermute(far_out, 'slab', far_pairs + [(b, a) for a, b in far_pairs])  1.83 us
    ppermute x6, waiting for transfers between devices, swap(): return lax.ppermute(values, ('vol', 'slab'), pairs)  1.76 us
    pallas_call x1, Pallas kernels, shards(): call(element_kernel, jax.ShapeDtypeStruct((3 * high_count, LANES), f32),...  1.5 us
    pallas_call x1, Pallas kernels, shards(): call(functools.partial(table_kernel, place_owner=place_owner, groups=grou...  1.29 us
    ppermute x1, starting transfers between devices, shards(): lax.ppermute(far_out, 'slab', far_pairs + [(b, a) for a, b in far_pairs])  1.2 us
    ppermute x1, starting transfers between devices, shards(): lax.ppermute(near_out, 'slab', near_pairs + [(b, a) for a, b in near_pairs])  1.17 us
  transfers between devices with their start and end apart: 8, of which 3 were waited for; matrix products, arithmetic and copies ran while one was open for 0% of the time, Pallas kernels for 20%

profile of v5, /device:TPU:1, one launch (start us, length us, event | category | flops | bytes accessed | tf_op | source)
XLA Modules:
  0.0 22.0 jit_solution(15111281347590627808)
XLA Ops:
  0.0 0.0 copy-start.1
  0.0 0.0 copy-start.11
  0.0 0.9 %copy-done.1 = bf16[8,64,64]{2,1,0:T(8,128)(2,1)S(1)} copy-done((bf16[8,64,64]{2,1,0:T(8,128)(2,1)S(1)}, bf16[8,64,64]{2,1,0:T(8,128)(2,1)}, u32[]{:S(2)}) %copy-start.1) | copy-done | bytes 65560
  0.9 0.0 copy-done.11
  0.9 0.0 copy-start.2
  0.9 0.0 copy-start.4
  0.9 0.0 copy-start.5
  0.9 0.0 copy-start.10
  0.9 0.1 shard_map.119.refs_0_
  1.0 3.2 %collective-permute-start.4 = (bf16[136,256]{1,0:T(8,128)(2,1)S(1)}, bf16[136,256]{1,0:T(8,128)(2,1)S(1)}, u32[]{:S(2)}, u32[]{:S(2)}) collective-permute-start(bf16[136,256]{1,0:T(8,128)(2,1)S(1)} %shard_map.119.refs_0_), channel_id=1, source_target_pairs={{0,8},{1,17},{2,10},{3,19},{4,12},{5,21},{6,14},{7,23},{8,0},{9,25... | collective-permute-start | bytes 208904 | tf_op jit(solution)/shard_map/ppermute | solution.py:413
  4.2 1.3 %collective-permute-start = (bf16[136,256]{1,0:T(8,128)(2,1)S(1)}, bf16[136,256]{1,0:T(8,128)(2,1)S(1)}, u32[]{:S(2)}, u32[]{:S(2)}) collective-permute-start(bf16[136,256]{1,0:T(8,128)(2,1)S(1)} %shard_map.119.refs_0_), channel_id=1, source_target_pairs={{0,24},{1,9},{2,26},{3,11},{4,28},{5,13},{6,30},{7,15},{8,16},{9,1... | collective-permute-start | bytes 208904 | tf_op jit(solution)/shard_map/ppermute | solution.py:413
  5.5 1.1 %collective-permute-start.2 = (bf16[136,256]{1,0:T(8,128)(2,1)S(1)}, bf16[136,256]{1,0:T(8,128)(2,1)S(1)}, u32[]{:S(2)}, u32[]{:S(2)}) collective-permute-start(bf16[136,256]{1,0:T(8,128)(2,1)S(1)} %shard_map.119.refs_0_), channel_id=1, source_target_pairs={{0,16},{1,13},{2,18},{3,15},{4,20},{5,9},{6,22},{7,11},{8,24},{9,5... | collective-permute-start | bytes 208904 | tf_op jit(solution)/shard_map/ppermute | solution.py:413
  6.6 0.0 copy-done.2
  6.6 0.0 copy-done.4
  6.6 0.0 copy-done.5
  6.6 0.0 copy-done.10
  6.6 0.0 copy-start
  6.6 0.0 copy-start.3
  6.6 0.0 copy-start.6
  6.7 0.0 copy-start.7
  6.7 0.0 copy-start.8
  6.7 0.0 copy-start.9
  6.7 1.5 %shard_map.120.refs_1_.refs_9_ = f32[24,128]{1,0:T(8,128)S(1)} custom-call(f32[3,1024]{1,0:T(4,128)S(1)} %copy-done.4, s32[8,1024]{1,0:T(8,128)S(1)} %copy-done.2, f32[1,1024]{1,0:T(1,128)S(1)} %bitcast.9, f32[24,24]{1,0:T(8,128)S(1)} %copy-done.5), custom_call_target="tpu_custom_call" | custom-call | flops 2000000000 | bytes 1000000 | tf_op jit(solution)/shard_map/pallas_call | solution.py:398
  8.2 0.0 collective-permute-done.4.refs_1_
  8.2 0.3 %collective-permute-start.5 = (bf16[272,256]{1,0:T(8,128)(2,1)S(1)}, bf16[272,256]{1,0:T(8,128)(2,1)S(1)}, u32[]{:S(2)}, u32[]{:S(2)}) collective-permute-start(bf16[272,256]{1,0:T(8,128)(2,1)S(1)} %shard_map.123), channel_id=1, source_target_pairs={{0,4},{1,5},{2,6},{3,7},{4,0},{5,1},{6,2},{7,3},{8,12},{9,13},{10,... | collective-permute-start | bytes 417800 | tf_op jit(solution)/shard_map/ppermute | solution.py:413
  8.5 0.0 copy-done
  8.6 0.0 copy-done.3
  8.6 0.0 copy-done.6
  8.6 0.0 copy-done.7
  8.6 0.0 copy-done.8
  8.6 0.0 copy-done.9
  8.6 1.3 %shard_map.122 = (bf16[8192,128]{1,0:T(8,128)(2,1)S(1)}, s32[10,2048]{1,0:T(8,128)S(1)}, f32[1,2048]{1,0:T(1,128)S(1)}, s32[4,2048]{1,0:T(4,128)S(1)}, bf16[128,...) custom-call(s32[1]{0:T(128)} %bitcast.1.vol_ref, s32[1]{0:T(128)} %bitcast.2.odd_ref.refs_10_, f32[12,64]{1,0:T(8,128)S(1)} %copy-done.6, ...), custom_call_target="tpu_custom_call" | custom-call | flops 2000000000 | bytes 1000000 | tf_op jit(solution)/shard_map/pallas_call | solution.py:384
  9.9 0.0 collective-permute-done.refs_0_.refs_3_
  9.9 1.7 %collective-permute-start.1 = (bf16[136,256]{1,0:T(8,128)(2,1)S(1)}, bf16[136,256]{1,0:T(8,128)(2,1)S(1)}, u32[]{:S(2)}, u32[]{:S(2)}) collective-permute-start(bf16[136,256]{1,0:T(8,128)(2,1)S(1)} %shard_map.121), channel_id=1, source_target_pairs={{0,4},{1,17},{2,6},{3,19},{4,0},{5,21},{6,2},{7,23},{8,12},{9,25},... | collective-permute-start | bytes 208904 | tf_op jit(solution)/shard_map/ppermute | solution.py:413
  11.6 0.0 collective-permute-done.2.refs_4_
  11.6 0.7 %collective-permute-start.3 = (bf16[136,256]{1,0:T(8,128)(2,1)S(1)}, bf16[136,256]{1,0:T(8,128)(2,1)S(1)}, u32[]{:S(2)}, u32[]{:S(2)}) collective-permute-start(bf16[136,256]{1,0:T(8,128)(2,1)S(1)} %collective-permute-done.2.refs_4_), channel_id=1, source_target_pairs={{0,4},{1,17},{2,6},{3,19},{4,0},{5,21},{6,2},{7,23},{8,12},{9,25},... | collective-permute-start | bytes 208904 | tf_op jit(solution)/shard_map/ppermute | solution.py:413
  12.3 1.0 %collective-permute-done.5.refs_2_ = bf16[272,256]{1,0:T(8,128)(2,1)S(1)} collective-permute-done((bf16[272,256]{1,0:T(8,128)(2,1)S(1)}, bf16[272,256]{1,0:T(8,128)(2,1)S(1)}, u32[]{:S(2)}, u32[]{:S(2)}) %collective-permute-start.5) | collective-permute-done | bytes 139296 | tf_op jit(solution)/shard_map/ppermute | solution.py:413
  13.4 1.7 %shard_map.124.refs_5_ = f32[16,2048]{1,0:T(8,128)S(1)} custom-call(bf16[136,256]{1,0:T(8,128)(2,1)S(1)} %shard_map.119.refs_0_, bf16[136,256]{1,0:T(8,128)(2,1)S(1)} %collective-permute-done.4.refs_1_, bf16[272,256]{1,0:T(8,128)(2,1)S(1)} %collective-permute-done.5.refs_2_, bf16[136,256]{1,0:T(8,128)(2,1)S(1)} %collective-permute-done.refs_0_.refs_3_, ...), custom_call_target="tpu_custom_call" | custom-call | flops 1000000000 | bytes 1000000 | tf_op jit(solution)/shard_map/pallas_call | solution.py:447
  15.1 0.0 collective-permute-done.1.refs_0_
  15.1 0.7 %collective-permute-done.3.refs_1_ = bf16[136,256]{1,0:T(8,128)(2,1)S(1)} collective-permute-done((bf16[136,256]{1,0:T(8,128)(2,1)S(1)}, bf16[136,256]{1,0:T(8,128)(2,1)S(1)}, u32[]{:S(2)}, u32[]{:S(2)}) %collective-permute-start.3) | collective-permute-done | bytes 69664 | tf_op jit(solution)/shard_map/ppermute | solution.py:413
  15.8 1.4 %shard_map.125 = (f32[3,1024]{1,0:T(4,128)S(1)}, f32[3,256]{1,0:T(4,128)S(1)}, f32[3,256]{1,0:T(4,128)S(1)}) custom-call(bf16[136,256]{1,0:T(8,128)(2,1)S(1)} %collective-permute-done.1.refs_0_, bf16[136,256]{1,0:T(8,128)(2,1)S(1)} %collective-permute-done.3.refs_1_, bf16[256,2048]{1,0:T(8,128)(2,1)S(1)} %get-tuple-element.14.refs_5_.refs_2_, ...), custom_call_target="tpu_custom_call" | custom-call | flops 1000000000 | bytes 1000000 | tf_op jit(solution)/shard_map/pallas_call | solution.py:447
  17.2 1.2 %collective-permute-start.6 = (f32[3,256]{1,0:T(4,128)S(1)}, f32[3,256]{1,0:T(4,128)S(1)}, u32[]{:S(2)}, u32[]{:S(2)}) collective-permute-start(f32[3,256]{1,0:T(4,128)S(1)} %get-tuple-element.21), channel_id=1, source_target_pairs={{0,1},{2,3},{1,0},{3,2},{4,5},{6,7},{5,4},{7,6},{8,9},{10,11},{9,8... | collective-permute-start | bytes 9224 | tf_op jit(solution)/shard_map/ppermute | solution.py:474
  18.3 1.2 %collective-permute-start.7 = (f32[3,256]{1,0:T(4,128)S(1)}, f32[3,256]{1,0:T(4,128)S(1)}, u32[]{:S(2)}, u32[]{:S(2)}) collective-permute-start(f32[3,256]{1,0:T(4,128)S(1)} %get-tuple-element.22), channel_id=1, source_target_pairs={{1,2},{0,3},{2,1},{3,0},{5,6},{4,7},{6,5},{7,4},{9,10},{8,11},{10,... | collective-permute-start | bytes 9224 | tf_op jit(solution)/shard_map/ppermute | solution.py:473
  19.5 0.0 collective-permute-done.6
  19.5 1.8 %collective-permute-done.7 = f32[3,256]{1,0:T(4,128)S(1)} collective-permute-done((f32[3,256]{1,0:T(4,128)S(1)}, f32[3,256]{1,0:T(4,128)S(1)}, u32[]{:S(2)}, u32[]{:S(2)}) %collective-permute-start.7) | collective-permute-done | bytes 3104 | tf_op jit(solution)/shard_map/ppermute | solution.py:473
  21.4 0.6 %pad_maximum_fusion = f32[3,1024]{1,0:T(4,128)} fusion(f32[3,256]{1,0:T(4,128)S(1)} %get-tuple-element.24, f32[3,512]{1,0:T(4,128)S(1)} %slice.10, f32[3,256]{1,0:T(4,128)S(1)} %get-tuple-element.23), kind=kLoop, calls=%fused_computation | loop fusion | flops 6144 | bytes 24576 | tf_op jit(solution)/shard_map/concatenate | solution.py:480
  (5 shorter events, 0.0 us)
Async XLA Ops:
  0.0 0.9 %copy-start.1 = (bf16[8,64,64]{2,1,0:T(8,128)(2,1)S(1)}, bf16[8,64,64]{2,1,0:T(8,128)(2,1)}, u32[]{:S(2)}) copy-start(bf16[8,64,64]{2,1,0:T(8,128)(2,1)} %mortar_ref.1) | copy-start | bytes 196612
  0.0 0.9 %copy-start.11 = (bf16[8,64]{1,0:T(8,128)(2,1)S(1)}, bf16[8,64]{1,0:T(8,128)(2,1)}, u32[]{:S(2)}) copy-start(bf16[8,64]{1,0:T(8,128)(2,1)} %offset_ref.1) | copy-start | bytes 3076
  0.9 5.7 %copy-start.2 = (s32[8,1024]{1,0:T(8,128)S(1)}, s32[8,1024]{1,0:T(8,128)}, u32[]{:S(2)}) copy-start(s32[8,1024]{1,0:T(8,128)} %connect_ref.1) | copy-start | bytes 98308
  0.9 5.7 %copy-start.4 = (f32[3,1024]{1,0:T(4,128)S(1)}, f32[3,1024]{1,0:T(4,128)}, u32[]{:S(2)}) copy-start(f32[3,1024]{1,0:T(4,128)} %disp_ref.2) | copy-start | bytes 36868
  0.9 5.7 %copy-start.5 = (f32[24,24]{1,0:T(8,128)S(1)}, f32[24,24]{1,0:T(8,128)}, u32[]{:S(2)}) copy-start(f32[24,24]{1,0:T(8,128)} %matrix_ref.1) | copy-start | bytes 6916
  0.9 5.7 %copy-start.10 = (f32[1024]{0:T(1024)S(1)}, f32[1024]{0:T(1024)}, u32[]{:S(2)}) copy-start(f32[1024]{0:T(1024)} %param.21) | copy-start | bytes 12292
  1.0 7.2 %collective-permute-start.4 = (bf16[136,256]{1,0:T(8,128)(2,1)S(1)}, bf16[136,256]{1,0:T(8,128)(2,1)S(1)}, u32[]{:S(2)}, u32[]{:S(2)}) collective-permute-start(bf16[136,256]{1,0:T(8,128)(2,1)S(1)} %shard_map.119.refs_0_), channel_id=1, source_target_pairs={{0,8},{1,17},{2,10},{3,19},{4,12},{5,21},{6,14},{7,23},{8,0},{9,25... | collective-permute-start | bytes 208904 | tf_op jit(solution)/shard_map/ppermute | solution.py:413
  4.2 5.7 %collective-permute-start = (bf16[136,256]{1,0:T(8,128)(2,1)S(1)}, bf16[136,256]{1,0:T(8,128)(2,1)S(1)}, u32[]{:S(2)}, u32[]{:S(2)}) collective-permute-start(bf16[136,256]{1,0:T(8,128)(2,1)S(1)} %shard_map.119.refs_0_), channel_id=1, source_target_pairs={{0,24},{1,9},{2,26},{3,11},{4,28},{5,13},{6,30},{7,15},{8,16},{9,1... | collective-permute-start | bytes 208904 | tf_op jit(solution)/shard_map/ppermute | solution.py:413
  5.5 6.1 %collective-permute-start.2 = (bf16[136,256]{1,0:T(8,128)(2,1)S(1)}, bf16[136,256]{1,0:T(8,128)(2,1)S(1)}, u32[]{:S(2)}, u32[]{:S(2)}) collective-permute-start(bf16[136,256]{1,0:T(8,128)(2,1)S(1)} %shard_map.119.refs_0_), channel_id=1, source_target_pairs={{0,16},{1,13},{2,18},{3,15},{4,20},{5,9},{6,22},{7,11},{8,24},{9,5... | collective-permute-start | bytes 208904 | tf_op jit(solution)/shard_map/ppermute | solution.py:413
  6.6 1.9 %copy-start = (bf16[64,2048]{1,0:T(8,128)(2,1)S(1)}, bf16[64,2048]{1,0:T(8,128)(2,1)}, u32[]{:S(2)}) copy-start(bf16[64,2048]{1,0:T(8,128)(2,1)} %disp_ref.3) | copy-start | bytes 786436
  6.6 1.9 %copy-start.3 = (s32[4,2048]{1,0:T(4,128)S(1)}, s32[4,2048]{1,0:T(4,128)}, u32[]{:S(2)}) copy-start(s32[4,2048]{1,0:T(4,128)} %face_ref.1) | copy-start | bytes 98308
  6.6 1.9 %copy-start.6 = (f32[12,64]{1,0:T(8,128)S(1)}, f32[12,64]{1,0:T(8,128)}, u32[]{:S(2)}) copy-start(f32[12,64]{1,0:T(8,128)} %shape_ref.1) | copy-start | bytes 9220
  6.7 1.9 %copy-start.7 = (s32[2048,1]{0,1:T(1,128)S(1)}, s32[2048,1]{0,1:T(1,128)}, u32[]{:S(2)}) copy-start(s32[2048,1]{0,1:T(1,128)} %param.13) | copy-start | bytes 24580
  6.7 1.9 %copy-start.8 = (s32[2048]{0:T(1024)S(1)}, s32[2048]{0:T(1024)}, u32[]{:S(2)}) copy-start(s32[2048]{0:T(1024)} %param.14) | copy-start | bytes 24580
  6.7 1.9 %copy-start.9 = (f32[2048]{0:T(1024)S(1)}, f32[2048]{0:T(1024)}, u32[]{:S(2)}) copy-start(f32[2048]{0:T(1024)} %param.15) | copy-start | bytes 24580
  8.2 5.2 %collective-permute-start.5 = (bf16[272,256]{1,0:T(8,128)(2,1)S(1)}, bf16[272,256]{1,0:T(8,128)(2,1)S(1)}, u32[]{:S(2)}, u32[]{:S(2)}) collective-permute-start(bf16[272,256]{1,0:T(8,128)(2,1)S(1)} %shard_map.123), channel_id=1, source_target_pairs={{0,4},{1,5},{2,6},{3,7},{4,0},{5,1},{6,2},{7,3},{8,12},{9,13},{10,... | collective-permute-start | bytes 417800 | tf_op jit(solution)/shard_map/ppermute | solution.py:413
  9.9 5.2 %collective-permute-start.1 = (bf16[136,256]{1,0:T(8,128)(2,1)S(1)}, bf16[136,256]{1,0:T(8,128)(2,1)S(1)}, u32[]{:S(2)}, u32[]{:S(2)}) collective-permute-start(bf16[136,256]{1,0:T(8,128)(2,1)S(1)} %shard_map.121), channel_id=1, source_target_pairs={{0,4},{1,17},{2,6},{3,19},{4,0},{5,21},{6,2},{7,23},{8,12},{9,25},... | collective-permute-start | bytes 208904 | tf_op jit(solution)/shard_map/ppermute | solution.py:413
  11.6 4.2 %collective-permute-start.3 = (bf16[136,256]{1,0:T(8,128)(2,1)S(1)}, bf16[136,256]{1,0:T(8,128)(2,1)S(1)}, u32[]{:S(2)}, u32[]{:S(2)}) collective-permute-start(bf16[136,256]{1,0:T(8,128)(2,1)S(1)} %collective-permute-done.2.refs_4_), channel_id=1, source_target_pairs={{0,4},{1,17},{2,6},{3,19},{4,0},{5,21},{6,2},{7,23},{8,12},{9,25},... | collective-permute-start | bytes 208904 | tf_op jit(solution)/shard_map/ppermute | solution.py:413
  17.2 2.4 %collective-permute-start.6 = (f32[3,256]{1,0:T(4,128)S(1)}, f32[3,256]{1,0:T(4,128)S(1)}, u32[]{:S(2)}, u32[]{:S(2)}) collective-permute-start(f32[3,256]{1,0:T(4,128)S(1)} %get-tuple-element.21), channel_id=1, source_target_pairs={{0,1},{2,3},{1,0},{3,2},{4,5},{6,7},{5,4},{7,6},{8,9},{10,11},{9,8... | collective-permute-start | bytes 9224 | tf_op jit(solution)/shard_map/ppermute | solution.py:474
  18.3 3.0 %collective-permute-start.7 = (f32[3,256]{1,0:T(4,128)S(1)}, f32[3,256]{1,0:T(4,128)S(1)}, u32[]{:S(2)}, u32[]{:S(2)}) collective-permute-start(f32[3,256]{1,0:T(4,128)S(1)} %get-tuple-element.22), channel_id=1, source_target_pairs={{1,2},{0,3},{2,1},{3,0},{5,6},{4,7},{6,5},{7,4},{9,10},{8,11},{10,... | collective-permute-start | bytes 9224 | tf_op jit(solution)/shard_map/ppermute | solution.py:473

commit v6 on v5

--- a/solution.py
+++ b/solution.py
@@ -33,12 +33,8 @@
 
 
 def low_columns(node_row):
-    pieces = []
-    for start in range(0, node_row.shape[1], LANES):
-        low = (node_row[:, start : start + LANES] % LANES).astype(f32)
-        lines = jnp.transpose(jnp.broadcast_to(low, (LANES, LANES)))
-        hit = lines == lax.broadcasted_iota(i32, (LANES, LANES), 1).astype(f32)
-        pieces.append(hit.astype(f32).astype(bf16))
+    table = low_table(node_row)
+    pieces = [jnp.transpose(table[:, start : start + LANES]) for start in range(0, node_row.shape[1], LANES)]
     return jnp.concatenate(pieces, axis=0)
 
 
@@ -321,7 +317,7 @@
     )
 
 
-STEPS = ((2, 6, 4, 1, 1, 1), (4, 2, 3, 1, 4, 4))
+STEPS = ((2, 6, 4, 1, 1, 1), (4, 3, 2, 1, 4, 4))
 
 
 def arrivals(masks):
@@ -419,7 +415,7 @@
         masks = list(zip(*STEPS))
         one, two, three = [swap(payload, masks[k]) for k in range(3)]
         early = swap(join(payload, one), masks[3])
-        late = [swap(join(two, internal), masks[4]), swap(three, masks[5])]
+        late = [swap(lax.optimization_barrier((two, internal))[0], masks[4]), swap(three, masks[5])]
         parts = [[payload, one, early, two, three], late]
     else:
         parts = [[lax.all_gather(payload, "vol", tiled=True)]]

time: 22.2 us -> 22.2 us (level)
  starting transfers between devices: 10.7 us -> 11.3 us
  Pallas kernels: 5.93 us -> 5.35 us
    ppermute x1, starting transfers between devices: 1.17 us -> 1.74 us  [shards(): lax.ppermute(near_out, 'slab', near_pairs + [(b, a) for a, b in near_pairs])]
    pallas_call x1, Pallas kernels: 1.29 us -> 0.73 us  [shards(): call(functools.partial(table_kernel, place_owner=place_owner, groups=grou...]
  transfers between devices with their start and end apart: 8 -> 8, of which waited for: 3 -> 3; matrix products, arithmetic and copies ran while one was open for 0% -> 0% of each run, Pallas kernels for 20% -> 18%
where the time goes in v6:
time: 22.2 us; the launch traced here: 22 us
  starting transfers between devices  11.3 us (51%)
  Pallas kernels  5.35 us (24%)
  waiting for transfers between devices  3.58 us (16%)
  local copies, waits for them, and re-layouts  0.96 us (4%)
  other arithmetic  0.62 us (3%)
    ppermute x6, starting transfers between devices, swap(): return lax.ppermute(values, ('vol', 'slab'), pairs)  8.33 us
    pallas_call x2, Pallas kernels, shards(): call(functools.partial(contact_kernel, payloads=len(pieces), past=past, l...  3.03 us
    ppermute x1, waiting for transfers between devices, shards(): lax.ppermute(far_out, 'slab', far_pairs + [(b, a) for a, b in far_pairs])  1.82 us
    ppermute x6, waiting for transfers between devices, swap(): return lax.ppermute(values, ('vol', 'slab'), pairs)  1.76 us
    ppermute x1, starting transfers between devices, shards(): lax.ppermute(near_out, 'slab', near_pairs + [(b, a) for a, b in near_pairs])  1.74 us
    pallas_call x1, Pallas kernels, shards(): call(element_kernel, jax.ShapeDtypeStruct((3 * high_count, LANES), f32),...  1.5 us
    ppermute x1, starting transfers between devices, shards(): lax.ppermute(far_out, 'slab', far_pairs + [(b, a) for a, b in far_pairs])  1.21 us
    unnamed x24, local copies, waits for them, and re-layouts  0.96 us
  transfers between devices with their start and end apart: 8, of which 3 were waited for; matrix products, arithmetic and copies ran while one was open for 0% of the time, Pallas kernels for 18%

profile of v6, /device:TPU:1, one launch (start us, length us, event | category | flops | bytes accessed | tf_op | source)
XLA Modules:
  0.0 22.0 jit_solution(12282292106495587300)
XLA Ops:
  0.0 0.0 copy-start.1
  0.0 0.0 copy-start.11
  0.0 0.9 %copy-done.1 = bf16[8,64,64]{2,1,0:T(8,128)(2,1)S(1)} copy-done((bf16[8,64,64]{2,1,0:T(8,128)(2,1)S(1)}, bf16[8,64,64]{2,1,0:T(8,128)(2,1)}, u32[]{:S(2)}) %copy-start.1) | copy-done | bytes 65560
  0.9 0.0 copy-done.11
  0.9 0.0 copy-start.2
  0.9 0.0 copy-start.4
  0.9 0.0 copy-start.5
  0.9 0.0 copy-start.10
  0.9 0.1 shard_map.119.refs_0_
  1.0 3.2 %collective-permute-start.4 = (bf16[136,256]{1,0:T(8,128)(2,1)S(1)}, bf16[136,256]{1,0:T(8,128)(2,1)S(1)}, u32[]{:S(2)}, u32[]{:S(2)}) collective-permute-start(bf16[136,256]{1,0:T(8,128)(2,1)S(1)} %shard_map.119.refs_0_), channel_id=1, source_target_pairs={{0,8},{1,17},{2,10},{3,19},{4,12},{5,21},{6,14},{7,23},{8,0},{9,25... | collective-permute-start | bytes 208904 | tf_op jit(solution)/shard_map/ppermute | solution.py:409
  4.2 2.2 %collective-permute-start = (bf16[136,256]{1,0:T(8,128)(2,1)S(1)}, bf16[136,256]{1,0:T(8,128)(2,1)S(1)}, u32[]{:S(2)}, u32[]{:S(2)}) collective-permute-start(bf16[136,256]{1,0:T(8,128)(2,1)S(1)} %shard_map.119.refs_0_), channel_id=1, source_target_pairs={{0,24},{1,13},{2,26},{3,15},{4,28},{5,9},{6,30},{7,11},{8,16},{9,5... | collective-permute-start | bytes 208904 | tf_op jit(solution)/shard_map/ppermute | solution.py:409
  6.4 0.2 collective-permute-start.2
  6.6 0.0 copy-done.2
  6.6 0.0 copy-done.4
  6.6 0.0 copy-done.5
  6.6 0.0 copy-done.10
  6.6 0.0 copy-start
  6.6 0.0 copy-start.3
  6.6 0.0 copy-start.6
  6.7 0.0 copy-start.7
  6.7 0.0 copy-start.8
  6.7 0.0 copy-start.9
  6.7 1.5 %shard_map.120.refs_9_ = f32[24,128]{1,0:T(8,128)S(1)} custom-call(f32[3,1024]{1,0:T(4,128)S(1)} %copy-done.4, s32[8,1024]{1,0:T(8,128)S(1)} %copy-done.2, f32[1,1024]{1,0:T(1,128)S(1)} %bitcast.9, f32[24,24]{1,0:T(8,128)S(1)} %copy-done.5), custom_call_target="tpu_custom_call" | custom-call | flops 2000000000 | bytes 1000000 | tf_op jit(solution)/shard_map/pallas_call | solution.py:394
  8.2 0.0 collective-permute-done.4.refs_1_
  8.2 0.3 %collective-permute-start.5 = (bf16[272,256]{1,0:T(8,128)(2,1)S(1)}, bf16[272,256]{1,0:T(8,128)(2,1)S(1)}, u32[]{:S(2)}, u32[]{:S(2)}) collective-permute-start(bf16[272,256]{1,0:T(8,128)(2,1)S(1)} %shard_map.122), channel_id=1, source_target_pairs={{0,4},{1,5},{2,6},{3,7},{4,0},{5,1},{6,2},{7,3},{8,12},{9,13},{10,... | collective-permute-start | bytes 417800 | tf_op jit(solution)/shard_map/ppermute | solution.py:409
  8.5 0.0 copy-done
  8.6 0.0 copy-done.3
  8.6 0.0 copy-done.6
  8.6 0.0 copy-done.7
  8.6 0.0 copy-done.8
  8.6 0.0 copy-done.9
  8.6 0.7 %shard_map.121 = (bf16[8192,128]{1,0:T(8,128)(2,1)S(1)}, s32[10,2048]{1,0:T(8,128)S(1)}, f32[1,2048]{1,0:T(1,128)S(1)}, s32[4,2048]{1,0:T(4,128)S(1)}, bf16[128,...) custom-call(s32[1]{0:T(128)} %bitcast.1.vol_ref, s32[1]{0:T(128)} %bitcast.2.odd_ref.refs_10_, f32[12,64]{1,0:T(8,128)S(1)} %copy-done.6, ...), custom_call_target="tpu_custom_call" | custom-call | flops 2000000000 | bytes 1000000 | tf_op jit(solution)/shard_map/pallas_call | solution.py:380
  9.3 0.0 collective-permute-done.refs_3_
  9.3 1.7 %collective-permute-start.1 = (bf16[136,256]{1,0:T(8,128)(2,1)S(1)}, bf16[136,256]{1,0:T(8,128)(2,1)S(1)}, u32[]{:S(2)}, u32[]{:S(2)}) collective-permute-start(bf16[136,256]{1,0:T(8,128)(2,1)S(1)} %collective-permute-done.refs_3_), channel_id=1, source_target_pairs={{0,4},{1,17},{2,6},{3,19},{4,0},{5,21},{6,2},{7,23},{8,12},{9,25},... | collective-permute-start | bytes 208904 | tf_op jit(solution)/shard_map/ppermute | solution.py:409
  11.0 0.0 collective-permute-done.2.refs_4_
  11.0 0.7 %collective-permute-start.3 = (bf16[136,256]{1,0:T(8,128)(2,1)S(1)}, bf16[136,256]{1,0:T(8,128)(2,1)S(1)}, u32[]{:S(2)}, u32[]{:S(2)}) collective-permute-start(bf16[136,256]{1,0:T(8,128)(2,1)S(1)} %collective-permute-done.2.refs_4_), channel_id=1, source_target_pairs={{0,4},{1,17},{2,6},{3,19},{4,0},{5,21},{6,2},{7,23},{8,12},{9,25},... | collective-permute-start | bytes 208904 | tf_op jit(solution)/shard_map/ppermute | solution.py:409
  11.8 1.6 %collective-permute-done.5.refs_2_ = bf16[272,256]{1,0:T(8,128)(2,1)S(1)} collective-permute-done((bf16[272,256]{1,0:T(8,128)(2,1)S(1)}, bf16[272,256]{1,0:T(8,128)(2,1)S(1)}, u32[]{:S(2)}, u32[]{:S(2)}) %collective-permute-start.5) | collective-permute-done | bytes 139296 | tf_op jit(solution)/shard_map/ppermute | solution.py:409
  13.4 1.7 %shard_map.123.refs_5_ = f32[16,2048]{1,0:T(8,128)S(1)} custom-call(bf16[136,256]{1,0:T(8,128)(2,1)S(1)} %shard_map.119.refs_0_, bf16[136,256]{1,0:T(8,128)(2,1)S(1)} %collective-permute-done.4.refs_1_, bf16[272,256]{1,0:T(8,128)(2,1)S(1)} %collective-permute-done.5.refs_2_, bf16[136,256]{1,0:T(8,128)(2,1)S(1)} %collective-permute-done.refs_3_, ...), custom_call_target="tpu_custom_call" | custom-call | flops 1000000000 | bytes 1000000 | tf_op jit(solution)/shard_map/pallas_call | solution.py:443
  15.1 0.0 collective-permute-done.1.refs_0_
  15.1 0.1 collective-permute-done.3.refs_1_
  15.2 1.4 %shard_map.124 = (f32[3,1024]{1,0:T(4,128)S(1)}, f32[3,256]{1,0:T(4,128)S(1)}, f32[3,256]{1,0:T(4,128)S(1)}) custom-call(bf16[136,256]{1,0:T(8,128)(2,1)S(1)} %collective-permute-done.1.refs_0_, bf16[136,256]{1,0:T(8,128)(2,1)S(1)} %collective-permute-done.3.refs_1_, bf16[256,2048]{1,0:T(8,128)(2,1)S(1)} %get-tuple-element.16.refs_5_.refs_2_, ...), custom_call_target="tpu_custom_call" | custom-call | flops 1000000000 | bytes 1000000 | tf_op jit(solution)/shard_map/pallas_call | solution.py:443
  16.6 1.7 %collective-permute-start.6 = (f32[3,256]{1,0:T(4,128)S(1)}, f32[3,256]{1,0:T(4,128)S(1)}, u32[]{:S(2)}, u32[]{:S(2)}) collective-permute-start(f32[3,256]{1,0:T(4,128)S(1)} %get-tuple-element.23), channel_id=1, source_target_pairs={{0,1},{2,3},{1,0},{3,2},{4,5},{6,7},{5,4},{7,6},{8,9},{10,11},{9,8... | collective-permute-start | bytes 9224 | tf_op jit(solution)/shard_map/ppermute | solution.py:470
  18.3 1.2 %collective-permute-start.7 = (f32[3,256]{1,0:T(4,128)S(1)}, f32[3,256]{1,0:T(4,128)S(1)}, u32[]{:S(2)}, u32[]{:S(2)}) collective-permute-start(f32[3,256]{1,0:T(4,128)S(1)} %get-tuple-element.24), channel_id=1, source_target_pairs={{1,2},{0,3},{2,1},{3,0},{5,6},{4,7},{6,5},{7,4},{9,10},{8,11},{10,... | collective-permute-start | bytes 9224 | tf_op jit(solution)/shard_map/ppermute | solution.py:469
  19.5 0.0 collective-permute-done.6
  19.5 1.8 %collective-permute-done.7 = f32[3,256]{1,0:T(4,128)S(1)} collective-permute-done((f32[3,256]{1,0:T(4,128)S(1)}, f32[3,256]{1,0:T(4,128)S(1)}, u32[]{:S(2)}, u32[]{:S(2)}) %collective-permute-start.7) | collective-permute-done | bytes 3104 | tf_op jit(solution)/shard_map/ppermute | solution.py:469
  21.4 0.6 %pad_maximum_fusion = f32[3,1024]{1,0:T(4,128)} fusion(f32[3,256]{1,0:T(4,128)S(1)} %get-tuple-element.26, f32[3,512]{1,0:T(4,128)S(1)} %slice.10, f32[3,256]{1,0:T(4,128)S(1)} %get-tuple-element.25), kind=kLoop, calls=%fused_computation | loop fusion | flops 6144 | bytes 24576 | tf_op jit(solution)/shard_map/concatenate | solution.py:476
  (4 shorter events, 0.0 us)
Async XLA Ops:
  0.0 0.9 %copy-start.1 = (bf16[8,64,64]{2,1,0:T(8,128)(2,1)S(1)}, bf16[8,64,64]{2,1,0:T(8,128)(2,1)}, u32[]{:S(2)}) copy-start(bf16[8,64,64]{2,1,0:T(8,128)(2,1)} %mortar_ref.1) | copy-start | bytes 196612
  0.0 0.9 %copy-start.11 = (bf16[8,64]{1,0:T(8,128)(2,1)S(1)}, bf16[8,64]{1,0:T(8,128)(2,1)}, u32[]{:S(2)}) copy-start(bf16[8,64]{1,0:T(8,128)(2,1)} %offset_ref.1) | copy-start | bytes 3076
  0.9 5.7 %copy-start.2 = (s32[8,1024]{1,0:T(8,128)S(1)}, s32[8,1024]{1,0:T(8,128)}, u32[]{:S(2)}) copy-start(s32[8,1024]{1,0:T(8,128)} %connect_ref.1) | copy-start | bytes 98308
  0.9 5.7 %copy-start.4 = (f32[3,1024]{1,0:T(4,128)S(1)}, f32[3,1024]{1,0:T(4,128)}, u32[]{:S(2)}) copy-start(f32[3,1024]{1,0:T(4,128)} %disp_ref.2) | copy-start | bytes 36868
  0.9 5.7 %copy-start.5 = (f32[24,24]{1,0:T(8,128)S(1)}, f32[24,24]{1,0:T(8,128)}, u32[]{:S(2)}) copy-start(f32[24,24]{1,0:T(8,128)} %matrix_ref.1) | copy-start | bytes 6916
  0.9 5.7 %copy-start.10 = (f32[1024]{0:T(1024)S(1)}, f32[1024]{0:T(1024)}, u32[]{:S(2)}) copy-start(f32[1024]{0:T(1024)} %param.21) | copy-start | bytes 12292
  1.0 7.2 %collective-permute-start.4 = (bf16[136,256]{1,0:T(8,128)(2,1)S(1)}, bf16[136,256]{1,0:T(8,128)(2,1)S(1)}, u32[]{:S(2)}, u32[]{:S(2)}) collective-permute-start(bf16[136,256]{1,0:T(8,128)(2,1)S(1)} %shard_map.119.refs_0_), channel_id=1, source_target_pairs={{0,8},{1,17},{2,10},{3,19},{4,12},{5,21},{6,14},{7,23},{8,0},{9,25... | collective-permute-start | bytes 208904 | tf_op jit(solution)/shard_map/ppermute | solution.py:409
  4.2 5.1 %collective-permute-start = (bf16[136,256]{1,0:T(8,128)(2,1)S(1)}, bf16[136,256]{1,0:T(8,128)(2,1)S(1)}, u32[]{:S(2)}, u32[]{:S(2)}) collective-permute-start(bf16[136,256]{1,0:T(8,128)(2,1)S(1)} %shard_map.119.refs_0_), channel_id=1, source_target_pairs={{0,24},{1,13},{2,26},{3,15},{4,28},{5,9},{6,30},{7,11},{8,16},{9,5... | collective-permute-start | bytes 208904 | tf_op jit(solution)/shard_map/ppermute | solution.py:409
  6.4 4.6 %collective-permute-start.2 = (bf16[136,256]{1,0:T(8,128)(2,1)S(1)}, bf16[136,256]{1,0:T(8,128)(2,1)S(1)}, u32[]{:S(2)}, u32[]{:S(2)}) collective-permute-start(bf16[136,256]{1,0:T(8,128)(2,1)S(1)} %shard_map.119.refs_0_), channel_id=1, source_target_pairs={{0,16},{1,9},{2,18},{3,11},{4,20},{5,13},{6,22},{7,15},{8,24},{9,1... | collective-permute-start | bytes 208904 | tf_op jit(solution)/shard_map/ppermute | solution.py:409
  6.6 1.9 %copy-start = (bf16[64,2048]{1,0:T(8,128)(2,1)S(1)}, bf16[64,2048]{1,0:T(8,128)(2,1)}, u32[]{:S(2)}) copy-start(bf16[64,2048]{1,0:T(8,128)(2,1)} %disp_ref.3) | copy-start | bytes 786436
  6.6 1.9 %copy-start.3 = (s32[4,2048]{1,0:T(4,128)S(1)}, s32[4,2048]{1,0:T(4,128)}, u32[]{:S(2)}) copy-start(s32[4,2048]{1,0:T(4,128)} %face_ref.1) | copy-start | bytes 98308
  6.6 1.9 %copy-start.6 = (f32[12,64]{1,0:T(8,128)S(1)}, f32[12,64]{1,0:T(8,128)}, u32[]{:S(2)}) copy-start(f32[12,64]{1,0:T(8,128)} %shape_ref.1) | copy-start | bytes 9220
  6.7 1.9 %copy-start.7 = (s32[2048,1]{0,1:T(1,128)S(1)}, s32[2048,1]{0,1:T(1,128)}, u32[]{:S(2)}) copy-start(s32[2048,1]{0,1:T(1,128)} %param.13) | copy-start | bytes 24580
  6.7 1.9 %copy-start.8 = (s32[2048]{0:T(1024)S(1)}, s32[2048]{0:T(1024)}, u32[]{:S(2)}) copy-start(s32[2048]{0:T(1024)} %param.14) | copy-start | bytes 24580
  6.7 1.9 %copy-start.9 = (f32[2048]{0:T(1024)S(1)}, f32[2048]{0:T(1024)}, u32[]{:S(2)}) copy-start(f32[2048]{0:T(1024)} %param.15) | copy-start | bytes 24580
  8.2 5.2 %collective-permute-start.5 = (bf16[272,256]{1,0:T(8,128)(2,1)S(1)}, bf16[272,256]{1,0:T(8,128)(2,1)S(1)}, u32[]{:S(2)}, u32[]{:S(2)}) collective-permute-start(bf16[272,256]{1,0:T(8,128)(2,1)S(1)} %shard_map.122), channel_id=1, source_target_pairs={{0,4},{1,5},{2,6},{3,7},{4,0},{5,1},{6,2},{7,3},{8,12},{9,13},{10,... | collective-permute-start | bytes 417800 | tf_op jit(solution)/shard_map/ppermute | solution.py:409
  9.3 5.7 %collective-permute-start.1 = (bf16[136,256]{1,0:T(8,128)(2,1)S(1)}, bf16[136,256]{1,0:T(8,128)(2,1)S(1)}, u32[]{:S(2)}, u32[]{:S(2)}) collective-permute-start(bf16[136,256]{1,0:T(8,128)(2,1)S(1)} %collective-permute-done.refs_3_), channel_id=1, source_target_pairs={{0,4},{1,17},{2,6},{3,19},{4,0},{5,21},{6,2},{7,23},{8,12},{9,25},... | collective-permute-start | bytes 208904 | tf_op jit(solution)/shard_map/ppermute | solution.py:409
  11.0 4.2 %collective-permute-start.3 = (bf16[136,256]{1,0:T(8,128)(2,1)S(1)}, bf16[136,256]{1,0:T(8,128)(2,1)S(1)}, u32[]{:S(2)}, u32[]{:S(2)}) collective-permute-start(bf16[136,256]{1,0:T(8,128)(2,1)S(1)} %collective-permute-done.2.refs_4_), channel_id=1, source_target_pairs={{0,4},{1,17},{2,6},{3,19},{4,0},{5,21},{6,2},{7,23},{8,12},{9,25},... | collective-permute-start | bytes 208904 | tf_op jit(solution)/shard_map/ppermute | solution.py:409
  16.6 3.0 %collective-permute-start.6 = (f32[3,256]{1,0:T(4,128)S(1)}, f32[3,256]{1,0:T(4,128)S(1)}, u32[]{:S(2)}, u32[]{:S(2)}) collective-permute-start(f32[3,256]{1,0:T(4,128)S(1)} %get-tuple-element.23), channel_id=1, source_target_pairs={{0,1},{2,3},{1,0},{3,2},{4,5},{6,7},{5,4},{7,6},{8,9},{10,11},{9,8... | collective-permute-start | bytes 9224 | tf_op jit(solution)/shard_map/ppermute | solution.py:470
  18.3 3.0 %collective-permute-start.7 = (f32[3,256]{1,0:T(4,128)S(1)}, f32[3,256]{1,0:T(4,128)S(1)}, u32[]{:S(2)}, u32[]{:S(2)}) collective-permute-start(f32[3,256]{1,0:T(4,128)S(1)} %get-tuple-element.24), channel_id=1, source_target_pairs={{1,2},{0,3},{2,1},{3,0},{5,6},{4,7},{6,5},{7,4},{9,10},{8,11},{10,... | collective-permute-start | bytes 9224 | tf_op jit(solution)/shard_map/ppermute | solution.py:469
